TPU v7x, 32 devices: a whole 2x2x4 slice. The times are simulated.
32 devices in a mesh: section: 2 (over x), expert: 16 (over z, y, core).
Axes of the slice: x: 2, y: 2, z: 4, core: 2. Of those that a mesh axis runs over, the one named last changes fastest.
Arguments:
- carried: bfloat16 [2, 3072, 2048], P('section', 'expert'), may hold values from -6 to 6
- norm_gain: float32 [2, 2048], P('section'), may hold values from 0.25 to 1.75
- w_up: bfloat16 [2, 2048, 3072], P('section', None, 'expert'), may hold values from -0.125 to 0.125
- w_down: bfloat16 [2, 3072, 2048], P('section', 'expert'), may hold values from -0.21875 to 0.21875
- routes: int32 [1, 2, 3072, 2], P(None, 'section', 'expert'), may hold values from 0 to 3, all different within a row; in each aligned block of 192 rows (0 to 191, 192 to 383, ..., all dimensions but the last counted through in order) at most 120 rows name the same one
- gate_weights: float32 [1, 2, 3072, 2], P(None, 'section', 'expert'), may hold values from 0.3 to 1
Outputs:
- advanced: bfloat16 [2, 3072, 2048], P('section', 'expert')
Inputs may be any that keep to these rules, and one draw needn't show every extreme that they name: `routes`: each token names two different experts. Among the 192 tokens of one device at one step and section, no expert is named more than 120 times, a bound that some block reaches.
All inputs are finite; a program needn't handle non-finite values.
Results may differ from a plain program's by a relative error of at most 0.0052.
Values may be sent and summed in bfloat16 or wider, within the bound.
No kernel may reach another device: no remote copies, remote signals or barrier semaphores. Data moves between devices by JAX's collectives and lax.ppermute only.
A program may use at most 64 MiB of HBM per device.

v0:
```python
import functools

import jax
import jax.numpy as jnp
from jax import lax
from jax.experimental import pallas as pl
from jax.experimental.pallas import tpu as pltpu
from jax.sharding import PartitionSpec as P


VMEM = pl.BlockSpec(memory_space=pltpu.VMEM)
ANY = pl.BlockSpec(memory_space=pl.ANY)
VMEM_LIMIT = 32 * 2**20
BF16, F32 = jnp.bfloat16, jnp.float32


def exchanged(value, distance):
    count = lax.axis_size("expert")
    return lax.ppermute(value, "expert", [(i, i ^ distance) for i in range(count)])


def advanced(value, distance):
    sections, count = lax.axis_size("section"), lax.axis_size("expert")
    pairs = [
        (s * count + i, (s + 1) % sections * count + (i ^ distance))
        for s in range(sections)
        for i in range(count)
    ]
    return lax.ppermute(value, ("section", "expert"), pairs)


def dispatch_kernel(experts, capacity, x_ref, gain_ref, routes_ref, gates_ref, info_ref, *out_refs):
    rows = x_ref.shape[0]
    own = lax.axis_index("expert") // 4
    r0, r1 = routes_ref[0:1, :], routes_ref[1:2, :]
    padded = max(experts, 8)
    ids = lax.broadcasted_iota(jnp.int32, (padded, rows), 0)
    named = jnp.where((ids == r0) | (ids == r1), 1.0, 0.0)
    before = lax.broadcasted_iota(jnp.int32, (rows, rows), 0) < lax.broadcasted_iota(
        jnp.int32, (rows, rows), 1
    )
    place = jnp.dot(
        named.astype(BF16), jnp.where(before, 1.0, 0.0).astype(BF16), preferred_element_type=F32
    )
    p0 = jnp.sum(jnp.where(ids == r0, place, 0.0), axis=0, keepdims=True)
    p1 = jnp.sum(jnp.where(ids == r1, place, 0.0), axis=0, keepdims=True)
    t0 = (r0 ^ own) * capacity + p0.astype(jnp.int32)
    t1 = (r1 ^ own) * capacity + p1.astype(jnp.int32)
    info_ref[0:1, :] = t0.astype(F32)
    info_ref[1:2, :] = t1.astype(F32)
    info_ref[2:4, :] = gates_ref[...]
    info_ref[4:8, :] = jnp.zeros((4, rows), F32)
    slots = lax.broadcasted_iota(jnp.int32, (experts * capacity, rows), 0)
    chosen = jnp.where((slots == t0) | (slots == t1), 1.0, 0.0).astype(BF16)
    values = x_ref[...].astype(F32)
    scale = lax.rsqrt(jnp.mean(values * values, axis=-1, keepdims=True) + 1e-05)
    normed = (values * scale * gain_ref[...]).astype(BF16)
    sent = jnp.dot(chosen, normed, preferred_element_type=F32)
    for d, out_ref in enumerate(out_refs):
        out_ref[...] = sent[d * capacity : (d + 1) * capacity].astype(BF16)


def dispatch(x, gain, routes, gates, experts, capacity):
    rows, width = x.shape
    return pl.pallas_call(
        functools.partial(dispatch_kernel, experts, capacity),
        out_shape=[jax.ShapeDtypeStruct((8, rows), F32)]
        + [jax.ShapeDtypeStruct((capacity, width), BF16)] * experts,
        in_specs=[VMEM] * 4,
        out_specs=[VMEM] * (experts + 1),
        cost_estimate=pl.CostEstimate(
            flops=2 * experts * capacity * rows * width,
            bytes_accessed=2 * width * (rows + experts * capacity),
            transcendentals=0,
        ),
        compiler_params=pltpu.CompilerParams(vmem_limit_bytes=VMEM_LIMIT),
        name="dispatch",
    )(x, gain, routes, gates)


def ffn_kernel(groups, *refs):
    row_refs, refs = refs[:groups], refs[groups:]
    up_refs, down_refs, refs = refs[:4], refs[4:8], refs[8:]
    out_refs, (up, down, sems) = refs[:groups], refs[groups:]
    quarter = up_refs[0].shape[0]
    copies = [
        pltpu.make_async_copy(src, dst.at[pl.ds(i * quarter, quarter)], sems.at[k, i])
        for k, (sources, dst) in enumerate(((up_refs, up), (down_refs, down)))
        for i, src in enumerate(sources)
    ]
    for copy in copies:
        copy.start()
    rows = jnp.concatenate([ref[...].astype(F32) for ref in row_refs], axis=0).astype(BF16)
    for copy in copies[:4]:
        copy.wait()
    hidden = lax.dot_general(
        rows, up[...], (((1,), (1,)), ((), ())), preferred_element_type=F32
    )
    hidden = jax.nn.gelu(hidden).astype(BF16)
    for copy in copies[4:]:
        copy.wait()
    out = jnp.dot(hidden, down[...], preferred_element_type=F32)
    capacity = out_refs[0].shape[0]
    for d, out_ref in enumerate(out_refs):
        out_ref[...] = out[d * capacity : (d + 1) * capacity].astype(BF16)


def ffn(rows, ups, downs):
    groups, (capacity, width) = len(rows), rows[0].shape
    quarter = ups[0].shape[0]
    return pl.pallas_call(
        functools.partial(ffn_kernel, groups),
        out_shape=[jax.ShapeDtypeStruct((capacity, width), BF16)] * groups,
        in_specs=[VMEM] * groups + [ANY] * 8,
        out_specs=[VMEM] * groups,
        scratch_shapes=[
            pltpu.VMEM((4 * quarter, width), BF16),
            pltpu.VMEM((4 * quarter, width), BF16),
            pltpu.SemaphoreType.DMA((2, 4)),
        ],
        cost_estimate=pl.CostEstimate(
            flops=16 * groups * capacity * quarter * width,
            bytes_accessed=4 * width * (groups * capacity + 4 * quarter),
            transcendentals=4 * groups * capacity * quarter,
        ),
        compiler_params=pltpu.CompilerParams(vmem_limit_bytes=VMEM_LIMIT),
        name="ffn",
    )(*rows, *ups, *downs)


def combine_kernel(x_ref, info_ref, *refs):
    result_refs, out_ref = refs[:-1], refs[-1]
    rows = x_ref.shape[0]
    info = jnp.transpose(info_ref[...])
    results = jnp.concatenate([ref[...].astype(F32) for ref in result_refs], axis=0).astype(BF16)
    slots = lax.broadcasted_iota(jnp.int32, (rows, results.shape[0]), 1)
    picks = [
        jnp.where(slots == info[:, k : k + 1].astype(jnp.int32), 1.0, 0.0) for k in range(2)
    ]
    both = jnp.dot(
        jnp.concatenate(picks, axis=0).astype(BF16), results, preferred_element_type=F32
    )
    new = x_ref[...].astype(F32) + info[:, 2:3] * both[:rows] + info[:, 3:4] * both[rows:]
    out_ref[...] = new.astype(BF16)


def combine(x, info, results):
    rows, width = x.shape
    slots = len(results) * results[0].shape[0]
    return pl.pallas_call(
        combine_kernel,
        out_shape=jax.ShapeDtypeStruct((rows, width), BF16),
        in_specs=[VMEM] * (2 + len(results)),
        out_specs=VMEM,
        cost_estimate=pl.CostEstimate(
            flops=4 * rows * slots * width,
            bytes_accessed=2 * width * (2 * rows + slots),
            transcendentals=0,
        ),
        compiler_params=pltpu.CompilerParams(vmem_limit_bytes=VMEM_LIMIT),
        name="combine",
    )(x, info, *results)


def step(carried, norm_gain, w_up, w_down, routes, gate_weights):
    experts = lax.axis_size("expert") // 4
    x = carried[0]
    tok_rows = x.shape[0]
    capacity = min(tok_rows, 4 * ((5 * tok_rows + 8 * experts - 1) // (8 * experts)))
    up, down = w_up[0].T, w_down[0]
    up_far, down_far = exchanged(up, 2), exchanged(down, 2)
    info, *rows = dispatch(x, norm_gain, routes[0, 0].T, gate_weights[0, 0].T, experts, capacity)
    rows = [rows[0]] + [exchanged(rows[d], 4 * d) for d in range(1, experts)]
    up_near, down_near = exchanged(up, 1), exchanged(down, 1)
    x_next, info_next = advanced(x, 0), advanced(info, 0)
    ups = (up, up_near, up_far, exchanged(up_far, 1))
    downs = (down, down_near, down_far, exchanged(down_far, 1))
    first = experts - experts // 4
    early = ffn(rows[:first], ups, downs)
    results = [advanced(early[d], 4 * d) for d in range(first)]
    late = ffn(rows[first:], ups, downs)
    results += [advanced(late[d - first], 4 * d) for d in range(first, experts)]
    return combine(x_next, info_next, results)[None]


def solution(mesh):
    in_specs = (
        P("section", "expert", None),
        P("section", None),
        P("section", None, "expert"),
        P("section", "expert", None),
        P(None, "section", "expert", None),
        P(None, "section", "expert", None),
    )
    out_specs = P("section", "expert", None)
    return jax.shard_map(step, mesh=mesh, in_specs=in_specs, out_specs=out_specs, check_vma=False)
```

profile of v0, /device:TPU:14, one launch (start us, length us, event | category | flops | bytes accessed | tf_op | source)
XLA Modules:
  0.0 129.2 jit_solution(4116430609314557052)
XLA Ops:
  0.0 0.5 collective-permute-start.5
  0.5 1.5 %collective-permute-start.8 = (bf16[192,2048]{1,0:T(8,128)(2,1)}, bf16[192,2048]{1,0:T(8,128)(2,1)S(1)}, u32[]{:S(2)}, u32[]{:S(2)}) collective-permute-start(bf16[192,2048]{1,0:T(8,128)(2,1)} %bitcast.16), channel_id=1, source_target_pairs={{0,2},{1,3},{2,0},{3,1},{4,6},{5,7},{6,4},{7,5},{8,10},{9,11},{10,... | collective-permute-start | bytes 2359304 | tf_op jit(solution)/shard_map/ppermute | solution.py:19
  2.0 0.7 copy-done.3
  2.7 0.7 copy-done.4
  3.4 0.7 copy-done.5
  4.1 2.1 %dispatch.1 = (f32[8,192]{1,0:T(8,128)S(1)}, bf16[120,2048]{1,0:T(8,128)(2,1)S(1)}, bf16[120,2048]{1,0:T(8,128)(2,1)S(1)}, bf16[120,2048]{1,0:T(8,128)(2,1)S(1)}, bf16[120,2048]{1,0:T(8,128)(2,1)S(1)}) custom-call(bf16[192,2048]{1,0:T(8,128)(2,1)} %bitcast.x_ref, f32[1,2048]{1,0:T(1,128)S(1)} %copy-done.3, s32[2,192]{1,0:T(2,128)S(1)} %bitcast.20, ...), custom_call_target="tpu_custom_call" | custom-call | flops 377487360 | bytes 2752512 | tf_op jit(solution)/shard_map/dispatch/pallas_call | solution.py:65
  6.2 0.5 collective-permute-start.2
  6.7 0.5 collective-permute-start.7
  7.2 13.4 %collective-permute-done.5.refs_5_.refs_3_ = bf16[192,2048]{1,0:T(8,128)(2,1)S(1)} collective-permute-done((bf16[192,2048]{1,0:T(8,128)(2,1)}, bf16[192,2048]{1,0:T(8,128)(2,1)S(1)}, u32[]{:S(2)}, u32[]{:S(2)}) %collective-permute-start.5) | collective-permute-done | bytes 786464 | tf_op jit(solution)/shard_map/ppermute | solution.py:19
  20.6 0.0 collective-permute-start.6
  20.6 15.7 %collective-permute-done.8.refs_9_.refs_7_ = bf16[192,2048]{1,0:T(8,128)(2,1)S(1)} collective-permute-done((bf16[192,2048]{1,0:T(8,128)(2,1)}, bf16[192,2048]{1,0:T(8,128)(2,1)S(1)}, u32[]{:S(2)}, u32[]{:S(2)}) %collective-permute-start.8) | collective-permute-done | bytes 786464 | tf_op jit(solution)/shard_map/ppermute | solution.py:19
  36.4 2.6 %collective-permute-start.3 = (bf16[120,2048]{1,0:T(8,128)(2,1)S(1)}, bf16[120,2048]{1,0:T(8,128)(2,1)S(1)}, u32[]{:S(2)}, u32[]{:S(2)}) collective-permute-start(bf16[120,2048]{1,0:T(8,128)(2,1)S(1)} %get-tuple-element.16), channel_id=1, source_target_pairs={{0,8},{1,9},{2,10},{3,11},{4,12},{5,13},{6,14},{7,15},{8,0},{9,1},... | collective-permute-start | bytes 1474568 | tf_op jit(solution)/shard_map/ppermute | solution.py:19
  38.9 21.6 %collective-permute-done.3.refs_2_ = bf16[120,2048]{1,0:T(8,128)(2,1)S(1)} collective-permute-done((bf16[120,2048]{1,0:T(8,128)(2,1)S(1)}, bf16[120,2048]{1,0:T(8,128)(2,1)S(1)}, u32[]{:S(2)}, u32[]{:S(2)}) %collective-permute-start.3) | collective-permute-done | bytes 491552 | tf_op jit(solution)/shard_map/ppermute | solution.py:19
  60.5 0.5 collective-permute-start
  61.1 0.0 collective-permute-done.7.refs_8_.refs_6_
  61.1 1.5 %collective-permute-start.1 = (f32[8,192]{1,0:T(8,128)S(1)}, f32[8,192]{1,0:T(8,128)S(1)}, u32[]{:S(2)}, u32[]{:S(2)}) collective-permute-start(f32[8,192]{1,0:T(8,128)S(1)} %get-tuple-element.13), channel_id=1, source_target_pairs={{0,16},{1,17},{2,18},{3,19},{4,20},{5,21},{6,22},{7,23},{8,24},{9,... | collective-permute-start | bytes 18440 | tf_op jit(solution)/shard_map/ppermute | solution.py:29
  62.6 0.0 collective-permute-done.6.refs_6_.refs_4_
  62.6 0.0 collective-permute-done.9.refs_10_.refs_8_
  62.6 1.1 copy-done.1
  63.7 4.0 %ffn.2 = (bf16[120,2048]{1,0:T(8,128)(2,1)S(1)}, bf16[120,2048]{1,0:T(8,128)(2,1)S(1)}, bf16[120,2048]{1,0:T(8,128)(2,1)S(1)}) custom-call(bf16[120,2048]{1,0:T(8,128)(2,1)S(1)} %get-tuple-element.14.refs_0_, bf16[120,2048]{1,0:T(8,128)(2,1)S(1)} %collective-permute-done.2.refs_1_, bf16[120,2048]{1,0:T(8,128)(2,1)S(1)} %collective-permute-done.3.refs_2_, ...), custom_call_target="tpu_custom_call" | custom-call | flops 2264924160 | bytes 9240576 | tf_op jit(solution)/shard_map/ffn/pallas_call | solution.py:111
  67.7 0.6 collective-permute-start.10
  68.3 5.7 %collective-permute-start.11 = (bf16[120,2048]{1,0:T(8,128)(2,1)S(1)}, bf16[120,2048]{1,0:T(8,128)(2,1)S(1)}, u32[]{:S(2)}, u32[]{:S(2)}) collective-permute-start(bf16[120,2048]{1,0:T(8,128)(2,1)S(1)} %get-tuple-element.18), channel_id=1, source_target_pairs={{0,20},{1,21},{2,22},{3,23},{4,16},{5,17},{6,18},{7,19},{8,28},{9,... | collective-permute-start | bytes 1474568 | tf_op jit(solution)/shard_map/ppermute | solution.py:29
  74.1 10.2 %collective-permute-done.13.refs_0_ = bf16[120,2048]{1,0:T(8,128)(2,1)S(1)} collective-permute-done((bf16[120,2048]{1,0:T(8,128)(2,1)S(1)}, bf16[120,2048]{1,0:T(8,128)(2,1)S(1)}, u32[]{:S(2)}, u32[]{:S(2)}) %collective-permute-start.13) | collective-permute-done | bytes 491552 | tf_op jit(solution)/shard_map/ppermute | solution.py:19
  84.3 2.8 %ffn.3 = bf16[120,2048]{1,0:T(8,128)(2,1)S(1)} custom-call(bf16[120,2048]{1,0:T(8,128)(2,1)S(1)} %collective-permute-done.13.refs_0_, bf16[192,2048]{1,0:T(8,128)(2,1)S(1)} %bitcast.15, bf16[192,2048]{1,0:T(8,128)(2,1)S(1)} %collective-permute-done.4.refs_4_.refs_2_, bf16[192,2048]{1,0:T(8,128)(2,1)S(1)} %collective-permute-done.5.refs_5_.refs_3_, ...), custom_call_target="tpu_custom_call" | custom-call | flops 754974720 | bytes 7274496 | tf_op jit(solution)/shard_map/ffn/pallas_call | solution.py:111
  87.0 15.4 %collective-permute-done.1.info_ref = f32[8,192]{1,0:T(8,128)S(1)} collective-permute-done((f32[8,192]{1,0:T(8,128)S(1)}, f32[8,192]{1,0:T(8,128)S(1)}, u32[]{:S(2)}, u32[]{:S(2)}) %collective-permute-start.1) | collective-permute-done | bytes 6176 | tf_op jit(solution)/shard_map/ppermute | solution.py:29
  102.4 2.0 %collective-permute-start.14 = (bf16[120,2048]{1,0:T(8,128)(2,1)S(1)}, bf16[120,2048]{1,0:T(8,128)(2,1)S(1)}, u32[]{:S(2)}, u32[]{:S(2)}) collective-permute-start(bf16[120,2048]{1,0:T(8,128)(2,1)S(1)} %ffn.3), channel_id=1, source_target_pairs={{0,28},{1,29},{2,30},{3,31},{4,24},{5,25},{6,26},{7,27},{8,20},{9,... | collective-permute-start | bytes 1474568 | tf_op jit(solution)/shard_map/ppermute | solution.py:29
  104.4 0.0 collective-permute-done.x_ref
  104.4 7.6 %collective-permute-done.10.refs_0_ = bf16[120,2048]{1,0:T(8,128)(2,1)S(1)} collective-permute-done((bf16[120,2048]{1,0:T(8,128)(2,1)S(1)}, bf16[120,2048]{1,0:T(8,128)(2,1)S(1)}, u32[]{:S(2)}, u32[]{:S(2)}) %collective-permute-start.10) | collective-permute-done | bytes 491552 | tf_op jit(solution)/shard_map/ppermute | solution.py:29
  112.0 0.0 collective-permute-done.11.refs_1_
  112.0 4.9 %collective-permute-done.12.refs_2_ = bf16[120,2048]{1,0:T(8,128)(2,1)S(1)} collective-permute-done((bf16[120,2048]{1,0:T(8,128)(2,1)S(1)}, bf16[120,2048]{1,0:T(8,128)(2,1)S(1)}, u32[]{:S(2)}, u32[]{:S(2)}) %collective-permute-start.12) | collective-permute-done | bytes 491552 | tf_op jit(solution)/shard_map/ppermute | solution.py:29
  116.9 10.1 %collective-permute-done.14.refs_3_ = bf16[120,2048]{1,0:T(8,128)(2,1)S(1)} collective-permute-done((bf16[120,2048]{1,0:T(8,128)(2,1)S(1)}, bf16[120,2048]{1,0:T(8,128)(2,1)S(1)}, u32[]{:S(2)}, u32[]{:S(2)}) %collective-permute-start.14) | collective-permute-done | bytes 491552 | tf_op jit(solution)/shard_map/ppermute | solution.py:29
  127.0 2.2 %combine.1 = bf16[192,2048]{1,0:T(8,128)(2,1)} custom-call(bf16[192,2048]{1,0:T(8,128)(2,1)S(1)} %collective-permute-done.x_ref, f32[8,192]{1,0:T(8,128)S(1)} %collective-permute-done.1.info_ref, bf16[120,2048]{1,0:T(8,128)(2,1)S(1)} %collective-permute-done.10.refs_0_, bf16[120,2048]{1,0:T(8,128)(2,1)S(1)} %collective-permute-done.11.refs_1_, ...), custom_call_target="tpu_custom_call" | custom-call | flops 754974720 | bytes 3538944 | tf_op jit(solution)/shard_map/combine/pallas_call | solution.py:150
  (14 shorter events, 0.0 us)
Async XLA Ops:
  0.0 6.7 %copy-start = (bf16[1,2048,192]{1,2,0:T(8,128)(2,1)S(1)}, bf16[1,2048,192]{1,2,0:T(8,128)(2,1)}, u32[]{:S(2)}) copy-start(bf16[1,2048,192]{1,2,0:T(8,128)(2,1)} %param.8) | copy-start | bytes 2359300
  0.0 20.6 %collective-permute-start.5 = (bf16[192,2048]{1,0:T(8,128)(2,1)}, bf16[192,2048]{1,0:T(8,128)(2,1)S(1)}, u32[]{:S(2)}, u32[]{:S(2)}) collective-permute-start(bf16[192,2048]{1,0:T(8,128)(2,1)} %bitcast.12), channel_id=1, source_target_pairs={{0,2},{1,3},{2,0},{3,1},{4,6},{5,7},{6,4},{7,5},{8,10},{9,11},{10,... | collective-permute-start | bytes 2359304 | tf_op jit(solution)/shard_map/ppermute | solution.py:19
  0.5 35.8 %collective-permute-start.8 = (bf16[192,2048]{1,0:T(8,128)(2,1)}, bf16[192,2048]{1,0:T(8,128)(2,1)S(1)}, u32[]{:S(2)}, u32[]{:S(2)}) collective-permute-start(bf16[192,2048]{1,0:T(8,128)(2,1)} %bitcast.16), channel_id=1, source_target_pairs={{0,2},{1,3},{2,0},{3,1},{4,6},{5,7},{6,4},{7,5},{8,10},{9,11},{10,... | collective-permute-start | bytes 2359304 | tf_op jit(solution)/shard_map/ppermute | solution.py:19
  2.0 0.7 copy-start.3
  2.7 0.7 copy-start.4
  3.4 0.7 copy-start.5
  6.2 30.2 %collective-permute-start.2 = (bf16[120,2048]{1,0:T(8,128)(2,1)S(1)}, bf16[120,2048]{1,0:T(8,128)(2,1)S(1)}, u32[]{:S(2)}, u32[]{:S(2)}) collective-permute-start(bf16[120,2048]{1,0:T(8,128)(2,1)S(1)} %get-tuple-element.15), channel_id=1, source_target_pairs={{0,4},{1,5},{2,6},{3,7},{4,0},{5,1},{6,2},{7,3},{8,12},{9,13},{10,... | collective-permute-start | bytes 1474568 | tf_op jit(solution)/shard_map/ppermute | solution.py:19
  6.7 53.9 %collective-permute-start.4 = (bf16[192,2048]{1,0:T(8,128)(2,1)S(1)}, bf16[192,2048]{1,0:T(8,128)(2,1)S(1)}, u32[]{:S(2)}, u32[]{:S(2)}) collective-permute-start(bf16[192,2048]{1,0:T(8,128)(2,1)S(1)} %bitcast.13), channel_id=1, source_target_pairs={{0,1},{1,0},{2,3},{3,2},{4,5},{5,4},{6,7},{7,6},{8,9},{9,8},{10,11... | collective-permute-start | bytes 2359304 | tf_op jit(solution)/shard_map/ppermute | solution.py:19
  6.7 54.4 %collective-permute-start.7 = (bf16[192,2048]{1,0:T(8,128)(2,1)}, bf16[192,2048]{1,0:T(8,128)(2,1)S(1)}, u32[]{:S(2)}, u32[]{:S(2)}) collective-permute-start(bf16[192,2048]{1,0:T(8,128)(2,1)} %bitcast.17), channel_id=1, source_target_pairs={{0,1},{1,0},{2,3},{3,2},{4,5},{5,4},{6,7},{7,6},{8,9},{9,8},{10,11... | collective-permute-start | bytes 2359304 | tf_op jit(solution)/shard_map/ppermute | solution.py:19
  20.6 42.0 %collective-permute-start.6 = (bf16[192,2048]{1,0:T(8,128)(2,1)S(1)}, bf16[192,2048]{1,0:T(8,128)(2,1)S(1)}, u32[]{:S(2)}, u32[]{:S(2)}) collective-permute-start(bf16[192,2048]{1,0:T(8,128)(2,1)S(1)} %collective-permute-done.5.refs_5_.refs_3_), channel_id=1, source_target_pairs={{0,1},{1,0},{2,3},{3,2},{4,5},{5,4},{6,7},{7,6},{8,9},{9,8},{10,11... | collective-permute-start | bytes 2359304 | tf_op jit(solution)/shard_map/ppermute | solution.py:19
  36.3 26.2 %collective-permute-start.9 = (bf16[192,2048]{1,0:T(8,128)(2,1)S(1)}, bf16[192,2048]{1,0:T(8,128)(2,1)S(1)}, u32[]{:S(2)}, u32[]{:S(2)}) collective-permute-start(bf16[192,2048]{1,0:T(8,128)(2,1)S(1)} %collective-permute-done.8.refs_9_.refs_7_), channel_id=1, source_target_pairs={{0,1},{1,0},{2,3},{3,2},{4,5},{5,4},{6,7},{7,6},{8,9},{9,8},{10,11... | collective-permute-start | bytes 2359304 | tf_op jit(solution)/shard_map/ppermute | solution.py:19
  36.4 24.2 %collective-permute-start.3 = (bf16[120,2048]{1,0:T(8,128)(2,1)S(1)}, bf16[120,2048]{1,0:T(8,128)(2,1)S(1)}, u32[]{:S(2)}, u32[]{:S(2)}) collective-permute-start(bf16[120,2048]{1,0:T(8,128)(2,1)S(1)} %get-tuple-element.16), channel_id=1, source_target_pairs={{0,8},{1,9},{2,10},{3,11},{4,12},{5,13},{6,14},{7,15},{8,0},{9,1},... | collective-permute-start | bytes 1474568 | tf_op jit(solution)/shard_map/ppermute | solution.py:19
  60.5 23.7 %collective-permute-start.13 = (bf16[120,2048]{1,0:T(8,128)(2,1)S(1)}, bf16[120,2048]{1,0:T(8,128)(2,1)S(1)}, u32[]{:S(2)}, u32[]{:S(2)}) collective-permute-start(bf16[120,2048]{1,0:T(8,128)(2,1)S(1)} %get-tuple-element.20), channel_id=1, source_target_pairs={{0,12},{1,13},{2,14},{3,15},{4,8},{5,9},{6,10},{7,11},{8,4},{9,5},... | collective-permute-start | bytes 1474568 | tf_op jit(solution)/shard_map/ppermute | solution.py:19
  60.5 43.9 %collective-permute-start = (bf16[192,2048]{1,0:T(8,128)(2,1)}, bf16[192,2048]{1,0:T(8,128)(2,1)S(1)}, u32[]{:S(2)}, u32[]{:S(2)}) collective-permute-start(bf16[192,2048]{1,0:T(8,128)(2,1)} %bitcast.x_ref), channel_id=1, source_target_pairs={{0,16},{1,17},{2,18},{3,19},{4,20},{5,21},{6,22},{7,23},{8,24},{9,... | collective-permute-start | bytes 2359304 | tf_op jit(solution)/shard_map/ppermute | solution.py:29
  61.1 41.3 %collective-permute-start.1 = (f32[8,192]{1,0:T(8,128)S(1)}, f32[8,192]{1,0:T(8,128)S(1)}, u32[]{:S(2)}, u32[]{:S(2)}) collective-permute-start(f32[8,192]{1,0:T(8,128)S(1)} %get-tuple-element.13), channel_id=1, source_target_pairs={{0,16},{1,17},{2,18},{3,19},{4,20},{5,21},{6,22},{7,23},{8,24},{9,... | collective-permute-start | bytes 18440 | tf_op jit(solution)/shard_map/ppermute | solution.py:29
  62.6 1.1 copy-start.1
  63.7 20.5 %copy-start.2 = (bf16[1,192,2048]{2,1,0:T(8,128)(2,1)S(1)}, bf16[1,192,2048]{2,1,0:T(8,128)(2,1)}, u32[]{:S(2)}) copy-start(bf16[1,192,2048]{2,1,0:T(8,128)(2,1)} %param.9) | copy-start | bytes 2359300
  67.7 44.3 %collective-permute-start.10 = (bf16[120,2048]{1,0:T(8,128)(2,1)S(1)}, bf16[120,2048]{1,0:T(8,128)(2,1)S(1)}, u32[]{:S(2)}, u32[]{:S(2)}) collective-permute-start(bf16[120,2048]{1,0:T(8,128)(2,1)S(1)} %get-tuple-element.17), channel_id=1, source_target_pairs={{0,16},{1,17},{2,18},{3,19},{4,20},{5,21},{6,22},{7,23},{8,24},{9,... | collective-permute-start | bytes 1474568 | tf_op jit(solution)/shard_map/ppermute | solution.py:29
  68.3 43.7 %collective-permute-start.11 = (bf16[120,2048]{1,0:T(8,128)(2,1)S(1)}, bf16[120,2048]{1,0:T(8,128)(2,1)S(1)}, u32[]{:S(2)}, u32[]{:S(2)}) collective-permute-start(bf16[120,2048]{1,0:T(8,128)(2,1)S(1)} %get-tuple-element.18), channel_id=1, source_target_pairs={{0,20},{1,21},{2,22},{3,23},{4,16},{5,17},{6,18},{7,19},{8,28},{9,... | collective-permute-start | bytes 1474568 | tf_op jit(solution)/shard_map/ppermute | solution.py:29
  84.2 32.7 %collective-permute-start.12 = (bf16[120,2048]{1,0:T(8,128)(2,1)S(1)}, bf16[120,2048]{1,0:T(8,128)(2,1)S(1)}, u32[]{:S(2)}, u32[]{:S(2)}) collective-permute-start(bf16[120,2048]{1,0:T(8,128)(2,1)S(1)} %get-tuple-element.19), channel_id=1, source_target_pairs={{0,24},{1,25},{2,26},{3,27},{4,28},{5,29},{6,30},{7,31},{8,16},{9,... | collective-permute-start | bytes 1474568 | tf_op jit(solution)/shard_map/ppermute | solution.py:29
  102.4 24.6 %collective-permute-start.14 = (bf16[120,2048]{1,0:T(8,128)(2,1)S(1)}, bf16[120,2048]{1,0:T(8,128)(2,1)S(1)}, u32[]{:S(2)}, u32[]{:S(2)}) collective-permute-start(bf16[120,2048]{1,0:T(8,128)(2,1)S(1)} %ffn.3), channel_id=1, source_target_pairs={{0,28},{1,29},{2,30},{3,31},{4,24},{5,25},{6,26},{7,27},{8,20},{9,... | collective-permute-start | bytes 1474568 | tf_op jit(solution)/shard_map/ppermute | solution.py:29
where the time goes:
time: 131 us; the launch traced here: 129 us
  waiting for transfers between devices  98.9 us (75%)
  starting transfers between devices  16 us (12%)
  Pallas kernels  11 us (8%)
  local copies, waits for them, and re-layouts  3.2 us (2%)
    ppermute x9, waiting for transfers between devices, exchanged(): lax.ppermute(value, 'expert', [(i, i ^ distance) for i in range(count)])  60.9 us
    ppermute x6, waiting for transfers between devices, advanced(): return lax.ppermute(value, ('section', 'expert'), pairs)  38 us
    ppermute x6, starting transfers between devices, advanced(): return lax.ppermute(value, ('section', 'expert'), pairs)  10.4 us
    pallas_call x2, Pallas kernels, ffn(): pl.pallas_call(functools.partial(ffn_kernel, groups), out_shape=[jax.Shap...  6.76 us
    ppermute x9, starting transfers between devices, exchanged(): lax.ppermute(value, 'expert', [(i, i ^ distance) for i in range(count)])  5.65 us
    unnamed x12, local copies, waits for them, and re-layouts  3.2 us
  transfers between devices with their start and end apart: 15, of which 8 were waited for; matrix products, arithmetic and copies ran while one was open for 0% of the time, Pallas kernels for 7%

commit v1 on v0

v1 whole, which is shorter than its diff:
```python
import functools

import jax
import jax.numpy as jnp
from jax import lax
from jax.experimental import pallas as pl
from jax.experimental.pallas import tpu as pltpu
from jax.sharding import PartitionSpec as P


VMEM = pl.BlockSpec(memory_space=pltpu.VMEM)
VMEM_LIMIT = 32 * 2**20
BF16, F32 = jnp.bfloat16, jnp.float32


def exchanged(value, distance):
    count = lax.axis_size("expert")
    return lax.ppermute(value, "expert", [(i, i ^ distance) for i in range(count)])


def advanced(value, distance):
    sections, count = lax.axis_size("section"), lax.axis_size("expert")
    pairs = [
        (s * count + i, (s + 1) % sections * count + (i ^ distance))
        for s in range(sections)
        for i in range(count)
    ]
    return lax.ppermute(value, ("section", "expert"), pairs)


def slots_of(routes, blocks, capacity):
    rows = routes.shape[1]
    own = lax.axis_index("expert") // 4
    named = [routes[k : k + 1, :] for k in range(2)]
    ids = lax.broadcasted_iota(jnp.int32, (max(blocks, 8), rows), 0)
    both = jnp.where((ids == named[0]) | (ids == named[1]), 1.0, 0.0).astype(BF16)
    before = lax.broadcasted_iota(jnp.int32, (rows, rows), 0) < lax.broadcasted_iota(
        jnp.int32, (rows, rows), 1
    )
    place = jnp.dot(both, jnp.where(before, 1.0, 0.0).astype(BF16), preferred_element_type=F32)
    return [
        (r ^ own) * capacity
        + jnp.sum(jnp.where(ids == r, place, 0.0), axis=0, keepdims=True).astype(jnp.int32)
        for r in named
    ]


def sort_kernel(capacity, x_ref, routes_ref, *out_refs):
    blocks = len(out_refs)
    s0, s1 = slots_of(routes_ref[...], blocks, capacity)
    ids = lax.broadcasted_iota(jnp.int32, (blocks * capacity, x_ref.shape[0]), 0)
    chosen = jnp.where((ids == s0) | (ids == s1), 1.0, 0.0).astype(BF16)
    sent = jnp.dot(chosen, x_ref[...], preferred_element_type=F32)
    for d, out_ref in enumerate(out_refs):
        out_ref[...] = sent[d * capacity : (d + 1) * capacity].astype(BF16)


def sort(x, routes, blocks, capacity):
    rows, width = x.shape
    return pl.pallas_call(
        functools.partial(sort_kernel, capacity),
        out_shape=[jax.ShapeDtypeStruct((capacity, width), BF16)] * blocks,
        in_specs=[VMEM] * 2,
        out_specs=[VMEM] * blocks,
        cost_estimate=pl.CostEstimate(
            flops=2 * blocks * capacity * rows * width,
            bytes_accessed=2 * width * (rows + blocks * capacity),
            transcendentals=0,
        ),
        compiler_params=pltpu.CompilerParams(vmem_limit_bytes=VMEM_LIMIT),
        name="sort",
    )(x, routes)


def joined(sources, target, sems):
    size = sources[0].shape[0]
    copies = [
        pltpu.make_async_copy(src, target.at[pl.ds(i * size, size)], sems.at[i])
        for i, src in enumerate(sources)
    ]
    for copy in copies:
        copy.start()

    def read():
        for copy in copies:
            copy.wait()
        return target[...]

    return read


def hidden_of(row_refs, gain, up):
    values = jnp.concatenate([ref[...].astype(F32) for ref in row_refs], axis=0)
    scale = lax.rsqrt(jnp.mean(values * values, axis=-1, keepdims=True) + 1e-05)
    rows = (values * scale * gain).astype(BF16)
    hidden = lax.dot_general(rows, up(), (((1,), (1,)), ((), ())), preferred_element_type=F32)
    return jax.nn.gelu(hidden)


def outputs_of(hidden, down, out_refs):
    out = jnp.dot(hidden, down, preferred_element_type=F32)
    capacity = out_refs[0].shape[0]
    for d, out_ref in enumerate(out_refs):
        out_ref[...] = out[d * capacity : (d + 1) * capacity].astype(BF16)


def up_kernel(groups, *refs):
    gain_ref, up_refs = refs[groups], refs[groups + 1 : groups + 5]
    own_ref, hidden_ref, up_ref, sems = refs[groups + 5 :]
    hidden = hidden_of(refs[:groups], gain_ref[...], joined(up_refs, up_ref, sems))
    capacity = own_ref.shape[0]
    own_ref[...] = hidden[:capacity].astype(BF16)
    hidden_ref[...] = hidden[capacity:].astype(BF16)


def down_kernel(groups, hidden_ref, *refs):
    down_refs, (*out_refs, down_ref, sems) = refs[:4], refs[4:]
    outputs_of(hidden_ref[...], joined(down_refs, down_ref, sems)(), out_refs)


def home_kernel(groups, hidden_ref, *refs):
    *down_refs, out_ref = refs
    size = down_refs[0].shape[0]
    hidden = hidden_ref[...]
    out_ref[...] = sum(
        jnp.dot(hidden[:, i * size : (i + 1) * size], ref[...], preferred_element_type=F32)
        for i, ref in enumerate(down_refs)
    ).astype(BF16)


def ffn_kernel(groups, *refs):
    gain_ref, up_ref, down_ref = refs[groups : groups + 3]
    hidden = hidden_of(refs[:groups], gain_ref[...], lambda: up_ref[...])
    outputs_of(hidden.astype(BF16), down_ref[...], refs[groups + 3 :])


def expert_call(kernel, groups, inputs, outs, shape, products):
    (capacity, width), units = shape
    rows = groups * capacity
    return pl.pallas_call(
        functools.partial(kernel, groups),
        out_shape=[jax.ShapeDtypeStruct(shape, BF16) for shape in outs],
        in_specs=[VMEM] * len(inputs),
        out_specs=[VMEM] * len(outs),
        scratch_shapes=[pltpu.SemaphoreType.DMA((4,))] if kernel in (up_kernel, down_kernel) else [],
        cost_estimate=pl.CostEstimate(
            flops=2 * products * rows * units * width,
            bytes_accessed=2 * products * width * (rows + units),
            transcendentals=rows * units,
        ),
        compiler_params=pltpu.CompilerParams(vmem_limit_bytes=VMEM_LIMIT),
    )(*inputs)


def slot_weights(info, first, count, dtype):
    slots = first + lax.broadcasted_iota(jnp.int32, (info.shape[0], count), 1)
    return sum(
        jnp.where(slots == info[:, k : k + 1].astype(jnp.int32), info[:, k + 2 : k + 3], 0.0)
        for k in range(2)
    ).astype(dtype)


def parts_of(weights):
    high = weights.astype(BF16)
    return high, (weights - high.astype(F32)).astype(BF16)


def taken(high, low, results):
    return jnp.dot(high, results, preferred_element_type=F32) + jnp.dot(
        low, results, preferred_element_type=F32
    )


def mix_kernel(blocks, x_ref, routes_ref, gates_ref, *refs):
    result_refs, (sum_ref, high_ref, low_ref) = refs[:-3], refs[-3:]
    capacity = result_refs[0].shape[0]
    slots = [s.astype(F32) for s in slots_of(routes_ref[...], blocks, capacity)]
    rows = slots[0].shape[1]
    info = jnp.concatenate(slots + [gates_ref[...], jnp.zeros((4, rows), F32)], axis=0)
    info = jnp.transpose(info)
    results = jnp.concatenate([ref[...].astype(F32) for ref in result_refs], axis=0).astype(BF16)
    count = results.shape[0]
    high, low = parts_of(slot_weights(info, 0, count, F32))
    sum_ref[...] = x_ref[...].astype(F32) + taken(high, low, results)
    high_ref[...], low_ref[...] = parts_of(
        slot_weights(info, count, blocks * capacity - count, F32)
    )


def last_kernel(sum_ref, high_ref, low_ref, *refs):
    results = jnp.concatenate([ref[...].astype(F32) for ref in refs[:-1]], axis=0).astype(BF16)
    refs[-1][...] = (sum_ref[...] + taken(high_ref[...], low_ref[...], results)).astype(BF16)


def combine_call(kernel, inputs, out_shape, slots):
    rows, width = inputs[0].shape
    return pl.pallas_call(
        kernel,
        out_shape=out_shape,
        in_specs=[VMEM] * len(inputs),
        out_specs=[VMEM] * len(out_shape),
        cost_estimate=pl.CostEstimate(
            flops=4 * rows * slots * width,
            bytes_accessed=2 * width * (3 * rows + slots),
            transcendentals=0,
        ),
        compiler_params=pltpu.CompilerParams(vmem_limit_bytes=VMEM_LIMIT),
    )(*inputs)


def step(carried, norm_gain, w_up, w_down, routes, gate_weights):
    experts = lax.axis_size("expert") // 4
    first = experts - experts // 4
    x, routes_now = carried[0], routes[0, 0].T
    tok_rows, width = x.shape
    capacity = min(tok_rows, 4 * ((5 * tok_rows + 8 * experts - 1) // (8 * experts)))
    block = (capacity, width)
    up, down = w_up[0].T, w_down[0]
    units = (4 * up.shape[0], width)
    shape = (block, units[0])

    rows = sort(x, routes_now, experts, capacity)
    rows = [rows[0]] + [exchanged(rows[d], 4 * d) for d in range(1, experts)]
    up_far, down_far = exchanged(up, 2), exchanged(down, 2)
    up_near, down_near = exchanged(up, 1), exchanged(down, 1)
    x_next = advanced(x, 0)
    routes_next = advanced(routes_now, 0)
    gates_next = advanced(gate_weights[0, 0].T, 0)
    ups = [up, up_near, up_far, exchanged(up_far, 1)]
    downs = [down, down_near, down_far, exchanged(down_far, 1)]
    hidden_own, hidden, up_all = expert_call(
        up_kernel,
        first,
        [*rows[:first], norm_gain, *ups],
        [(capacity, units[0]), ((first - 1) * capacity, units[0]), units],
        shape,
        1,
    )
    *early, down_all = expert_call(
        down_kernel, first - 1, [hidden, *downs], [block] * (first - 1) + [units], shape, 1
    )
    hidden_next = advanced(hidden_own, 0)
    down_next = advanced(down, 0)
    down_next_far = exchanged(down_next, 2)
    downs_next = [down_next, exchanged(down_next, 1)]
    downs_next += [down_next_far, exchanged(down_next_far, 1)]
    (home,) = expert_call(home_kernel, 1, [hidden_next, *downs_next], [block], shape, 1)
    late = expert_call(
        ffn_kernel,
        experts - first,
        [*rows[first:], norm_gain, up_all, down_all],
        [block] * (experts - first),
        shape,
        2,
    )
    results = [home] + [advanced(rows, 4 * (d + 1)) for d, rows in enumerate([*early, *late])]
    count = (experts - first) * capacity
    sums = combine_call(
        functools.partial(mix_kernel, experts),
        [x_next, routes_next, gates_next] + results[:first],
        [jax.ShapeDtypeStruct(x.shape, F32)]
        + [jax.ShapeDtypeStruct((tok_rows, count), BF16)] * 2,
        first * capacity,
    )
    (out,) = combine_call(
        last_kernel, [*sums, *results[first:]], [jax.ShapeDtypeStruct(x.shape, BF16)], count
    )
    return out[None]


def solution(mesh):
    in_specs = (
        P("section", "expert", None),
        P("section", None),
        P("section", None, "expert"),
        P("section", "expert", None),
        P(None, "section", "expert", None),
        P(None, "section", "expert", None),
    )
    out_specs = P("section", "expert", None)
    return jax.shard_map(step, mesh=mesh, in_specs=in_specs, out_specs=out_specs, check_vma=False)
```

time: 131 us -> 130 us (level)
  waiting for transfers between devices: 98.9 us -> 93.4 us
  starting transfers between devices: 16 us -> 21.2 us
    ppermute x9 -> x12, waiting for transfers between devices: 60.9 us -> 33.1 us  [exchanged(): lax.ppermute(value, 'expert', [(i, i ^ distance) for i in range(count)])]
    ppermute x6 -> x8, waiting for transfers between devices: 38 us -> 60.3 us  [advanced(): return lax.ppermute(value, ('section', 'expert'), pairs)]
    ppermute x9 -> x12, starting transfers between devices: 5.65 us -> 8.78 us  [exchanged(): lax.ppermute(value, 'expert', [(i, i ^ distance) for i in range(count)])]
    ppermute x6 -> x8, starting transfers between devices: 10.4 us -> 12.4 us  [advanced(): return lax.ppermute(value, ('section', 'expert'), pairs)]
    pallas_call x4 -> x7, Pallas kernels: 11 us -> 10.2 us  [the longest x4 6.59 us: expert_call(): pl.pallas_call(functools.partial(kernel, groups), out_shape=[jax.ShapeDty...]
  transfers between devices with their start and end apart: 15 -> 20, of which waited for: 8 -> 9; matrix products, arithmetic and copies ran while one was open for 0% -> 0% of each run, Pallas kernels for 7% -> 6%
where the time goes in v1:
time: 130 us; the launch traced here: 129 us
  waiting for transfers between devices  93.4 us (72%)
  starting transfers between devices  21.2 us (16%)
  Pallas kernels  10.2 us (8%)
  local copies, waits for them, and re-layouts  3.72 us (3%)
    ppermute x8, waiting for transfers between devices, advanced(): return lax.ppermute(value, ('section', 'expert'), pairs)  60.3 us
    ppermute x12, waiting for transfers between devices, exchanged(): lax.ppermute(value, 'expert', [(i, i ^ distance) for i in range(count)])  33.1 us
    ppermute x8, starting transfers between devices, advanced(): return lax.ppermute(value, ('section', 'expert'), pairs)  12.4 us
    ppermute x12, starting transfers between devices, exchanged(): lax.ppermute(value, 'expert', [(i, i ^ distance) for i in range(count)])  8.78 us
    pallas_call x4, Pallas kernels, expert_call(): pl.pallas_call(functools.partial(kernel, groups), out_shape=[jax.ShapeDty...  6.59 us
    unnamed x12, local copies, waits for them, and re-layouts  3.72 us
    pallas_call x2, Pallas kernels, combine_call(): pl.pallas_call(kernel, out_shape=out_shape, in_specs=[VMEM] * len(inputs)...  2.82 us
  transfers between devices with their start and end apart: 20, of which 9 were waited for; matrix products, arithmetic and copies ran while one was open for 0% of the time, Pallas kernels for 6%

profile of v1, /device:TPU:14, one launch (start us, length us, event | category | flops | bytes accessed | tf_op | source)
XLA Modules:
  0.0 128.6 jit_solution(1928649910707463188)
XLA Ops:
  0.0 1.2 copy-done.3
  1.2 0.7 copy-done.4
  1.9 0.8 sort.1
  2.7 0.5 collective-permute-start.3
  3.2 0.5 collective-permute-start.9
  3.9 3.0 %collective-permute-start.4 = (bf16[120,2048]{1,0:T(8,128)(2,1)S(1)}, bf16[120,2048]{1,0:T(8,128)(2,1)S(1)}, u32[]{:S(2)}, u32[]{:S(2)}) collective-permute-start(bf16[120,2048]{1,0:T(8,128)(2,1)S(1)} %get-tuple-element.20), channel_id=1, source_target_pairs={{0,8},{1,9},{2,10},{3,11},{4,12},{5,13},{6,14},{7,15},{8,0},{9,1},... | collective-permute-start | bytes 1474568 | tf_op jit(solution)/shard_map/ppermute | solution.py:18
  6.9 1.5 %collective-permute-start.1 = (s32[2,192]{1,0:T(2,128)}, s32[2,192]{1,0:T(2,128)S(1)}, u32[]{:S(2)}, u32[]{:S(2)}) collective-permute-start(s32[2,192]{1,0:T(2,128)} %bitcast.21), channel_id=1, source_target_pairs={{0,16},{1,17},{2,18},{3,19},{4,20},{5,21},{6,22},{7,23},{8,24},{9,... | collective-permute-start | bytes 4616 | tf_op jit(solution)/shard_map/ppermute | solution.py:28
  8.4 14.1 %collective-permute-done.1.routes_ref = s32[2,192]{1,0:T(2,128)S(1)} collective-permute-done((s32[2,192]{1,0:T(2,128)}, s32[2,192]{1,0:T(2,128)S(1)}, u32[]{:S(2)}, u32[]{:S(2)}) %collective-permute-start.1) | collective-permute-done | bytes 1568 | tf_op jit(solution)/shard_map/ppermute | solution.py:28
  23.0 0.7 collective-permute-done.3.refs_1_
  23.7 3.7 %collective-permute-done.4.refs_2_ = bf16[120,2048]{1,0:T(8,128)(2,1)S(1)} collective-permute-done((bf16[120,2048]{1,0:T(8,128)(2,1)S(1)}, bf16[120,2048]{1,0:T(8,128)(2,1)S(1)}, u32[]{:S(2)}, u32[]{:S(2)}) %collective-permute-start.4) | collective-permute-done | bytes 491552 | tf_op jit(solution)/shard_map/ppermute | solution.py:18
  27.4 1.2 collective-permute-start.11
  28.9 14.3 %collective-permute-done.14.refs_2_ = bf16[192,2048]{1,0:T(8,128)(2,1)S(1)} collective-permute-done((bf16[192,2048]{1,0:T(8,128)(2,1)}, bf16[192,2048]{1,0:T(8,128)(2,1)S(1)}, u32[]{:S(2)}, u32[]{:S(2)}) %collective-permute-start.14) | collective-permute-done | bytes 786464 | tf_op jit(solution)/shard_map/ppermute | solution.py:18
  43.1 0.5 collective-permute-start.10
  43.6 2.7 %collective-permute-start.18 = (bf16[120,2048]{1,0:T(8,128)(2,1)S(1)}, bf16[120,2048]{1,0:T(8,128)(2,1)S(1)}, u32[]{:S(2)}, u32[]{:S(2)}) collective-permute-start(bf16[120,2048]{1,0:T(8,128)(2,1)S(1)} %get-tuple-element.28), channel_id=1, source_target_pairs={{0,12},{1,13},{2,14},{3,15},{4,8},{5,9},{6,10},{7,11},{8,4},{9,5},... | collective-permute-start | bytes 1474568 | tf_op jit(solution)/shard_map/ppermute | solution.py:18
  46.3 11.4 %collective-permute-done.11.refs_2_ = bf16[192,2048]{1,0:T(8,128)(2,1)S(1)} collective-permute-done((bf16[192,2048]{1,0:T(8,128)(2,1)S(1)}, bf16[192,2048]{1,0:T(8,128)(2,1)S(1)}, u32[]{:S(2)}, u32[]{:S(2)}) %collective-permute-start.11) | collective-permute-done | bytes 786464 | tf_op jit(solution)/shard_map/ppermute | solution.py:18
  57.7 0.5 collective-permute-start
  58.2 1.1 copy-done
  59.4 0.7 copy-done.2
  60.1 2.4 %shard_map.64 = (bf16[120,768]{1,0:T(8,128)(2,1)S(1)}, bf16[240,768]{1,0:T(8,128)(2,1)S(1)}, bf16[768,2048]{1,0:T(8,128)(2,1)S(1)}) custom-call(bf16[120,2048]{1,0:T(8,128)(2,1)S(1)} %get-tuple-element.18.refs_0_, bf16[120,2048]{1,0:T(8,128)(2,1)S(1)} %collective-permute-done.3.refs_1_, bf16[120,2048]{1,0:T(8,128)(2,1)S(1)} %collective-permute-done.4.refs_2_, ...), custom_call_target="tpu_custom_call" | custom-call | flops 1132462080 | bytes 4620288 | tf_op jit(solution)/shard_map/pallas_call | solution.py:140
  62.5 1.6 %collective-permute-start.8 = (bf16[120,768]{1,0:T(8,128)(2,1)S(1)}, bf16[120,768]{1,0:T(8,128)(2,1)S(1)}, u32[]{:S(2)}, u32[]{:S(2)}) collective-permute-start(bf16[120,768]{1,0:T(8,128)(2,1)S(1)} %get-tuple-element.21), channel_id=1, source_target_pairs={{0,16},{1,17},{2,18},{3,19},{4,20},{5,21},{6,22},{7,23},{8,24},{9,... | collective-permute-start | bytes 552968 | tf_op jit(solution)/shard_map/ppermute | solution.py:28
  64.0 1.2 shard_map.66
  65.3 3.1 %collective-permute-done.18.refs_0_ = bf16[120,2048]{1,0:T(8,128)(2,1)S(1)} collective-permute-done((bf16[120,2048]{1,0:T(8,128)(2,1)S(1)}, bf16[120,2048]{1,0:T(8,128)(2,1)S(1)}, u32[]{:S(2)}, u32[]{:S(2)}) %collective-permute-start.18) | collective-permute-done | bytes 491552 | tf_op jit(solution)/shard_map/ppermute | solution.py:18
  68.3 4.1 %collective-permute-start.17 = (bf16[120,2048]{1,0:T(8,128)(2,1)S(1)}, bf16[120,2048]{1,0:T(8,128)(2,1)S(1)}, u32[]{:S(2)}, u32[]{:S(2)}) collective-permute-start(bf16[120,2048]{1,0:T(8,128)(2,1)S(1)} %get-tuple-element.24), channel_id=1, source_target_pairs={{0,24},{1,25},{2,26},{3,27},{4,28},{5,29},{6,30},{7,31},{8,16},{9,... | collective-permute-start | bytes 1474568 | tf_op jit(solution)/shard_map/ppermute | solution.py:28
  72.4 2.3 %shard_map.68 = bf16[120,2048]{1,0:T(8,128)(2,1)S(1)} custom-call(bf16[120,2048]{1,0:T(8,128)(2,1)S(1)} %collective-permute-done.18.refs_0_, f32[1,2048]{1,0:T(1,128)S(1)} %copy-done.2, bf16[768,2048]{1,0:T(8,128)(2,1)S(1)} %get-tuple-element.29.refs_2_, bf16[768,2048]{1,0:T(8,128)(2,1)S(1)} %get-tuple-element.30.refs_3_), custom_call_target="tpu_custom_call" | custom-call | flops 754974720 | bytes 7274496 | tf_op jit(solution)/shard_map/pallas_call | solution.py:140
  74.7 28.2 %collective-permute-done.8.hidden_ref = bf16[120,768]{1,0:T(8,128)(2,1)S(1)} collective-permute-done((bf16[120,768]{1,0:T(8,128)(2,1)S(1)}, bf16[120,768]{1,0:T(8,128)(2,1)S(1)}, u32[]{:S(2)}, u32[]{:S(2)}) %collective-permute-start.8) | collective-permute-done | bytes 184352 | tf_op jit(solution)/shard_map/ppermute | solution.py:28
  102.9 2.7 %collective-permute-start.19 = (bf16[120,2048]{1,0:T(8,128)(2,1)S(1)}, bf16[120,2048]{1,0:T(8,128)(2,1)S(1)}, u32[]{:S(2)}, u32[]{:S(2)}) collective-permute-start(bf16[120,2048]{1,0:T(8,128)(2,1)S(1)} %shard_map.68), channel_id=1, source_target_pairs={{0,28},{1,29},{2,30},{3,31},{4,24},{5,25},{6,26},{7,27},{8,20},{9,... | collective-permute-start | bytes 1474568 | tf_op jit(solution)/shard_map/ppermute | solution.py:28
  105.6 1.5 %collective-permute-start.2 = (f32[2,192]{1,0:T(2,128)S(1)}, f32[2,192]{1,0:T(2,128)S(1)}, u32[]{:S(2)}, u32[]{:S(2)}) collective-permute-start(f32[2,192]{1,0:T(2,128)S(1)} %bitcast.23), channel_id=1, source_target_pairs={{0,16},{1,17},{2,18},{3,19},{4,20},{5,21},{6,22},{7,23},{8,24},{9,... | collective-permute-start | bytes 4616 | tf_op jit(solution)/shard_map/ppermute | solution.py:28
  107.1 0.7 shard_map.65.refs_0_
  107.8 1.4 %collective-permute-done.2.gates_ref = f32[2,192]{1,0:T(2,128)S(1)} collective-permute-done((f32[2,192]{1,0:T(2,128)S(1)}, f32[2,192]{1,0:T(2,128)S(1)}, u32[]{:S(2)}, u32[]{:S(2)}) %collective-permute-start.2) | collective-permute-done | bytes 1568 | tf_op jit(solution)/shard_map/ppermute | solution.py:28
  109.2 1.4 %shard_map.67 = (f32[192,2048]{1,0:T(8,128)S(1)}, bf16[192,120]{1,0:T(8,128)(2,1)S(1)}, bf16[192,120]{1,0:T(8,128)(2,1)S(1)}) custom-call(bf16[192,2048]{1,0:T(8,128)(2,1)S(1)} %collective-permute-done.x_ref, s32[2,192]{1,0:T(2,128)S(1)} %collective-permute-done.1.routes_ref, f32[2,192]{1,0:T(2,128)S(1)} %collective-permute-done.2.gates_ref, ...), custom_call_target="tpu_custom_call" | custom-call | flops 566231040 | bytes 3833856 | tf_op jit(solution)/shard_map/pallas_call | solution.py:197
  110.6 16.6 %collective-permute-done.19.refs_0_ = bf16[120,2048]{1,0:T(8,128)(2,1)S(1)} collective-permute-done((bf16[120,2048]{1,0:T(8,128)(2,1)S(1)}, bf16[120,2048]{1,0:T(8,128)(2,1)S(1)}, u32[]{:S(2)}, u32[]{:S(2)}) %collective-permute-start.19) | collective-permute-done | bytes 491552 | tf_op jit(solution)/shard_map/ppermute | solution.py:28
  127.1 1.4 %shard_map.69 = bf16[192,2048]{1,0:T(8,128)(2,1)} custom-call(f32[192,2048]{1,0:T(8,128)S(1)} %get-tuple-element.25.sum_ref, bf16[192,120]{1,0:T(8,128)(2,1)S(1)} %get-tuple-element.26.high_ref, bf16[192,120]{1,0:T(8,128)(2,1)S(1)} %get-tuple-element.27.low_ref, bf16[120,2048]{1,0:T(8,128)(2,1)S(1)} %collective-permute-done.19.refs_0_), custom_call_target="tpu_custom_call" | custom-call | flops 188743680 | bytes 2850816 | tf_op jit(solution)/shard_map/pallas_call | solution.py:197
  (27 shorter events, 0.9 us)
Async XLA Ops:
  0.0 64.0 %copy-start.1 = (bf16[1,192,2048]{2,1,0:T(8,128)(2,1)S(1)}, bf16[1,192,2048]{2,1,0:T(8,128)(2,1)}, u32[]{:S(2)}) copy-start(bf16[1,192,2048]{2,1,0:T(8,128)(2,1)} %param.9) | copy-start | bytes 2359300
  0.0 1.2 copy-start.3
  1.2 0.7 copy-start.4
  2.7 20.9 %collective-permute-start.3 = (bf16[120,2048]{1,0:T(8,128)(2,1)S(1)}, bf16[120,2048]{1,0:T(8,128)(2,1)S(1)}, u32[]{:S(2)}, u32[]{:S(2)}) collective-permute-start(bf16[120,2048]{1,0:T(8,128)(2,1)S(1)} %get-tuple-element.19), channel_id=1, source_target_pairs={{0,4},{1,5},{2,6},{3,7},{4,0},{5,1},{6,2},{7,3},{8,12},{9,13},{10,... | collective-permute-start | bytes 1474568 | tf_op jit(solution)/shard_map/ppermute | solution.py:18
  3.2 24.2 %collective-permute-start.9 = (bf16[192,2048]{1,0:T(8,128)(2,1)}, bf16[192,2048]{1,0:T(8,128)(2,1)S(1)}, u32[]{:S(2)}, u32[]{:S(2)}) collective-permute-start(bf16[192,2048]{1,0:T(8,128)(2,1)} %bitcast.15), channel_id=1, source_target_pairs={{0,16},{1,17},{2,18},{3,19},{4,20},{5,21},{6,22},{7,23},{8,24},{9,... | collective-permute-start | bytes 2359304 | tf_op jit(solution)/shard_map/ppermute | solution.py:28
  3.8 24.8 %collective-permute-start.6 = (bf16[192,2048]{1,0:T(8,128)(2,1)}, bf16[192,2048]{1,0:T(8,128)(2,1)S(1)}, u32[]{:S(2)}, u32[]{:S(2)}) collective-permute-start(bf16[192,2048]{1,0:T(8,128)(2,1)} %bitcast.12), channel_id=1, source_target_pairs={{0,2},{1,3},{2,0},{3,1},{4,6},{5,7},{6,4},{7,5},{8,10},{9,11},{10,... | collective-permute-start | bytes 2359304 | tf_op jit(solution)/shard_map/ppermute | solution.py:18
  3.9 23.5 %collective-permute-start.4 = (bf16[120,2048]{1,0:T(8,128)(2,1)S(1)}, bf16[120,2048]{1,0:T(8,128)(2,1)S(1)}, u32[]{:S(2)}, u32[]{:S(2)}) collective-permute-start(bf16[120,2048]{1,0:T(8,128)(2,1)S(1)} %get-tuple-element.20), channel_id=1, source_target_pairs={{0,8},{1,9},{2,10},{3,11},{4,12},{5,13},{6,14},{7,15},{8,0},{9,1},... | collective-permute-start | bytes 1474568 | tf_op jit(solution)/shard_map/ppermute | solution.py:18
  6.9 15.6 %collective-permute-start.1 = (s32[2,192]{1,0:T(2,128)}, s32[2,192]{1,0:T(2,128)S(1)}, u32[]{:S(2)}, u32[]{:S(2)}) collective-permute-start(s32[2,192]{1,0:T(2,128)} %bitcast.21), channel_id=1, source_target_pairs={{0,16},{1,17},{2,18},{3,19},{4,20},{5,21},{6,22},{7,23},{8,24},{9,... | collective-permute-start | bytes 4616 | tf_op jit(solution)/shard_map/ppermute | solution.py:28
  22.5 20.6 %collective-permute-start.14 = (bf16[192,2048]{1,0:T(8,128)(2,1)}, bf16[192,2048]{1,0:T(8,128)(2,1)S(1)}, u32[]{:S(2)}, u32[]{:S(2)}) collective-permute-start(bf16[192,2048]{1,0:T(8,128)(2,1)} %bitcast.16), channel_id=1, source_target_pairs={{0,2},{1,3},{2,0},{3,1},{4,6},{5,7},{6,4},{7,5},{8,10},{9,11},{10,... | collective-permute-start | bytes 2359304 | tf_op jit(solution)/shard_map/ppermute | solution.py:18
  23.7 19.5 %collective-permute-start.5 = (bf16[192,2048]{1,0:T(8,128)(2,1)}, bf16[192,2048]{1,0:T(8,128)(2,1)S(1)}, u32[]{:S(2)}, u32[]{:S(2)}) collective-permute-start(bf16[192,2048]{1,0:T(8,128)(2,1)} %bitcast.13), channel_id=1, source_target_pairs={{0,1},{1,0},{2,3},{3,2},{4,5},{5,4},{6,7},{7,6},{8,9},{9,8},{10,11... | collective-permute-start | bytes 2359304 | tf_op jit(solution)/shard_map/ppermute | solution.py:18
  27.4 16.2 %collective-permute-start.13 = (bf16[192,2048]{1,0:T(8,128)(2,1)}, bf16[192,2048]{1,0:T(8,128)(2,1)S(1)}, u32[]{:S(2)}, u32[]{:S(2)}) collective-permute-start(bf16[192,2048]{1,0:T(8,128)(2,1)} %bitcast.17), channel_id=1, source_target_pairs={{0,1},{1,0},{2,3},{3,2},{4,5},{5,4},{6,7},{7,6},{8,9},{9,8},{10,11... | collective-permute-start | bytes 2359304 | tf_op jit(solution)/shard_map/ppermute | solution.py:18
  27.4 30.3 %collective-permute-start.11 = (bf16[192,2048]{1,0:T(8,128)(2,1)S(1)}, bf16[192,2048]{1,0:T(8,128)(2,1)S(1)}, u32[]{:S(2)}, u32[]{:S(2)}) collective-permute-start(bf16[192,2048]{1,0:T(8,128)(2,1)S(1)} %collective-permute-done.9.refs_0_), channel_id=1, source_target_pairs={{0,2},{1,3},{2,0},{3,1},{4,6},{5,7},{6,4},{7,5},{8,10},{9,11},{10,... | collective-permute-start | bytes 2359304 | tf_op jit(solution)/shard_map/ppermute | solution.py:18
  28.6 29.1 %collective-permute-start.7 = (bf16[192,2048]{1,0:T(8,128)(2,1)S(1)}, bf16[192,2048]{1,0:T(8,128)(2,1)S(1)}, u32[]{:S(2)}, u32[]{:S(2)}) collective-permute-start(bf16[192,2048]{1,0:T(8,128)(2,1)S(1)} %collective-permute-done.6.refs_6_), channel_id=1, source_target_pairs={{0,1},{1,0},{2,3},{3,2},{4,5},{5,4},{6,7},{7,6},{8,9},{9,8},{10,11... | collective-permute-start | bytes 2359304 | tf_op jit(solution)/shard_map/ppermute | solution.py:18
  43.1 19.3 %collective-permute-start.15 = (bf16[192,2048]{1,0:T(8,128)(2,1)S(1)}, bf16[192,2048]{1,0:T(8,128)(2,1)S(1)}, u32[]{:S(2)}, u32[]{:S(2)}) collective-permute-start(bf16[192,2048]{1,0:T(8,128)(2,1)S(1)} %collective-permute-done.14.refs_2_), channel_id=1, source_target_pairs={{0,1},{1,0},{2,3},{3,2},{4,5},{5,4},{6,7},{7,6},{8,9},{9,8},{10,11... | collective-permute-start | bytes 2359304 | tf_op jit(solution)/shard_map/ppermute | solution.py:18
  43.1 25.2 %collective-permute-start.10 = (bf16[192,2048]{1,0:T(8,128)(2,1)S(1)}, bf16[192,2048]{1,0:T(8,128)(2,1)S(1)}, u32[]{:S(2)}, u32[]{:S(2)}) collective-permute-start(bf16[192,2048]{1,0:T(8,128)(2,1)S(1)} %collective-permute-done.9.refs_0_), channel_id=1, source_target_pairs={{0,1},{1,0},{2,3},{3,2},{4,5},{5,4},{6,7},{7,6},{8,9},{9,8},{10,11... | collective-permute-start | bytes 2359304 | tf_op jit(solution)/shard_map/ppermute | solution.py:18
  43.6 24.7 %collective-permute-start.18 = (bf16[120,2048]{1,0:T(8,128)(2,1)S(1)}, bf16[120,2048]{1,0:T(8,128)(2,1)S(1)}, u32[]{:S(2)}, u32[]{:S(2)}) collective-permute-start(bf16[120,2048]{1,0:T(8,128)(2,1)S(1)} %get-tuple-element.28), channel_id=1, source_target_pairs={{0,12},{1,13},{2,14},{3,15},{4,8},{5,9},{6,10},{7,11},{8,4},{9,5},... | collective-permute-start | bytes 1474568 | tf_op jit(solution)/shard_map/ppermute | solution.py:18
  57.7 47.9 %collective-permute-start.12 = (bf16[192,2048]{1,0:T(8,128)(2,1)S(1)}, bf16[192,2048]{1,0:T(8,128)(2,1)S(1)}, u32[]{:S(2)}, u32[]{:S(2)}) collective-permute-start(bf16[192,2048]{1,0:T(8,128)(2,1)S(1)} %collective-permute-done.11.refs_2_), channel_id=1, source_target_pairs={{0,1},{1,0},{2,3},{3,2},{4,5},{5,4},{6,7},{7,6},{8,9},{9,8},{10,11... | collective-permute-start | bytes 2359304 | tf_op jit(solution)/shard_map/ppermute | solution.py:18
  57.7 51.5 %collective-permute-start = (bf16[192,2048]{1,0:T(8,128)(2,1)}, bf16[192,2048]{1,0:T(8,128)(2,1)S(1)}, u32[]{:S(2)}, u32[]{:S(2)}) collective-permute-start(bf16[192,2048]{1,0:T(8,128)(2,1)} %bitcast.19), channel_id=1, source_target_pairs={{0,16},{1,17},{2,18},{3,19},{4,20},{5,21},{6,22},{7,23},{8,24},{9,... | collective-permute-start | bytes 2359304 | tf_op jit(solution)/shard_map/ppermute | solution.py:28
  58.2 1.1 copy-start
  59.4 0.7 copy-start.2
  62.5 40.4 %collective-permute-start.8 = (bf16[120,768]{1,0:T(8,128)(2,1)S(1)}, bf16[120,768]{1,0:T(8,128)(2,1)S(1)}, u32[]{:S(2)}, u32[]{:S(2)}) collective-permute-start(bf16[120,768]{1,0:T(8,128)(2,1)S(1)} %get-tuple-element.21), channel_id=1, source_target_pairs={{0,16},{1,17},{2,18},{3,19},{4,20},{5,21},{6,22},{7,23},{8,24},{9,... | collective-permute-start | bytes 552968 | tf_op jit(solution)/shard_map/ppermute | solution.py:28
  68.3 40.8 %collective-permute-start.16 = (bf16[120,2048]{1,0:T(8,128)(2,1)S(1)}, bf16[120,2048]{1,0:T(8,128)(2,1)S(1)}, u32[]{:S(2)}, u32[]{:S(2)}) collective-permute-start(bf16[120,2048]{1,0:T(8,128)(2,1)S(1)} %get-tuple-element.23), channel_id=1, source_target_pairs={{0,20},{1,21},{2,22},{3,23},{4,16},{5,17},{6,18},{7,19},{8,28},{9,... | collective-permute-start | bytes 1474568 | tf_op jit(solution)/shard_map/ppermute | solution.py:28
  68.3 40.8 %collective-permute-start.17 = (bf16[120,2048]{1,0:T(8,128)(2,1)S(1)}, bf16[120,2048]{1,0:T(8,128)(2,1)S(1)}, u32[]{:S(2)}, u32[]{:S(2)}) collective-permute-start(bf16[120,2048]{1,0:T(8,128)(2,1)S(1)} %get-tuple-element.24), channel_id=1, source_target_pairs={{0,24},{1,25},{2,26},{3,27},{4,28},{5,29},{6,30},{7,31},{8,16},{9,... | collective-permute-start | bytes 1474568 | tf_op jit(solution)/shard_map/ppermute | solution.py:28
  72.4 33.1 %copy-start.5 = (f32[1,1,192,2]{2,3,1,0:T(2,128)S(1)}, f32[1,1,192,2]{2,3,1,0:T(2,128)}, u32[]{:S(2)}) copy-start(f32[1,1,192,2]{2,3,1,0:T(2,128)} %param.11) | copy-start | bytes 4612
  102.9 24.2 %collective-permute-start.19 = (bf16[120,2048]{1,0:T(8,128)(2,1)S(1)}, bf16[120,2048]{1,0:T(8,128)(2,1)S(1)}, u32[]{:S(2)}, u32[]{:S(2)}) collective-permute-start(bf16[120,2048]{1,0:T(8,128)(2,1)S(1)} %shard_map.68), channel_id=1, source_target_pairs={{0,28},{1,29},{2,30},{3,31},{4,24},{5,25},{6,26},{7,27},{8,20},{9,... | collective-permute-start | bytes 1474568 | tf_op jit(solution)/shard_map/ppermute | solution.py:28
  105.6 3.6 %collective-permute-start.2 = (f32[2,192]{1,0:T(2,128)S(1)}, f32[2,192]{1,0:T(2,128)S(1)}, u32[]{:S(2)}, u32[]{:S(2)}) collective-permute-start(f32[2,192]{1,0:T(2,128)S(1)} %bitcast.23), channel_id=1, source_target_pairs={{0,16},{1,17},{2,18},{3,19},{4,20},{5,21},{6,22},{7,23},{8,24},{9,... | collective-permute-start | bytes 4616 | tf_op jit(solution)/shard_map/ppermute | solution.py:28

commit v2 on v1

v2 whole, which is shorter than its diff:
```python
import functools

import jax
import jax.numpy as jnp
from jax import lax
from jax.experimental import pallas as pl
from jax.experimental.pallas import tpu as pltpu
from jax.sharding import PartitionSpec as P


VMEM = pl.BlockSpec(memory_space=pltpu.VMEM)
VMEM_LIMIT = 32 * 2**20
BF16, F32 = jnp.bfloat16, jnp.float32


def exchanged(value, distance):
    count = lax.axis_size("expert")
    return lax.ppermute(value, "expert", [(i, i ^ distance) for i in range(count)])


def advanced(value, distance):
    sections, count = lax.axis_size("section"), lax.axis_size("expert")
    pairs = [
        (s * count + i, (s + 1) % sections * count + (i ^ distance))
        for s in range(sections)
        for i in range(count)
    ]
    return lax.ppermute(value, ("section", "expert"), pairs)


def place_of(distance, half):
    return distance + (distance >= half) * (3 * half - 1 - 2 * distance)


def sort_kernel(blocks, capacity, with_info, x_ref, gain_ref, routes_ref, *refs):
    out_refs = refs[-blocks:]
    rows = x_ref.shape[0]
    own = lax.axis_index("expert") // 4
    r0, r1 = routes_ref[0:1, :], routes_ref[1:2, :]
    ids = lax.broadcasted_iota(jnp.int32, (max(2 * blocks, 8), rows), 0)
    named = jnp.where((ids == r0) | (ids == r1), 1.0, 0.0)
    before = lax.broadcasted_iota(jnp.int32, (rows, rows), 0) < lax.broadcasted_iota(
        jnp.int32, (rows, rows), 1
    )
    place = jnp.dot(
        named.astype(BF16), jnp.where(before, 1.0, 0.0).astype(BF16), preferred_element_type=F32
    )
    p0 = jnp.sum(jnp.where(ids == r0, place, 0.0), axis=0, keepdims=True)
    p1 = jnp.sum(jnp.where(ids == r1, place, 0.0), axis=0, keepdims=True)
    t0 = place_of(r0 ^ own, blocks) * capacity + p0.astype(jnp.int32)
    t1 = place_of(r1 ^ own, blocks) * capacity + p1.astype(jnp.int32)
    if with_info:
        gates_ref, info_ref = refs[:2]
        info_ref[0:1, :] = t0.astype(F32)
        info_ref[1:2, :] = t1.astype(F32)
        info_ref[2:4, :] = gates_ref[...]
        info_ref[4:8, :] = jnp.zeros((4, rows), F32)
    slots = lax.broadcasted_iota(jnp.int32, (blocks * capacity, rows), 0)
    chosen = jnp.where((slots == t0) | (slots == t1), 1.0, 0.0).astype(BF16)
    values = x_ref[...].astype(F32)
    scale = lax.rsqrt(jnp.mean(values * values, axis=-1, keepdims=True) + 1e-05)
    normed = (values * scale * gain_ref[...]).astype(BF16)
    sent = jnp.dot(chosen, normed, preferred_element_type=F32)
    for d, out_ref in enumerate(out_refs):
        out_ref[...] = sent[d * capacity : (d + 1) * capacity].astype(BF16)


def sort(x, gain, routes, gates, blocks, capacity):
    rows, width = x.shape
    with_info = gates is not None
    out_shape = [jax.ShapeDtypeStruct((8, rows), F32)] if with_info else []
    out_shape += [jax.ShapeDtypeStruct((capacity, width), BF16)] * blocks
    inputs = (x, gain, routes) + ((gates,) if with_info else ())
    return pl.pallas_call(
        functools.partial(sort_kernel, blocks, capacity, with_info),
        out_shape=out_shape,
        in_specs=[VMEM] * len(inputs),
        out_specs=[VMEM] * len(out_shape),
        cost_estimate=pl.CostEstimate(
            flops=2 * blocks * capacity * rows * width,
            bytes_accessed=2 * width * (rows + blocks * capacity),
            transcendentals=0,
        ),
        compiler_params=pltpu.CompilerParams(vmem_limit_bytes=VMEM_LIMIT),
        name="sort",
    )(*inputs)


def joined(sources, target, sems):
    size = sources[0].shape[0]
    copies = [
        pltpu.make_async_copy(src, target.at[pl.ds(i * size, size)], sems.at[i])
        for i, src in enumerate(sources)
    ]
    for copy in copies:
        copy.start()

    def read():
        for copy in copies:
            copy.wait()
        return target[...]

    return read


def hidden_of(row_refs, up):
    rows = jnp.concatenate([ref[...].astype(F32) for ref in row_refs], axis=0).astype(BF16)
    hidden = lax.dot_general(rows, up, (((1,), (1,)), ((), ())), preferred_element_type=F32)
    return jax.nn.gelu(hidden)


def outputs_of(hidden, down, out_refs):
    out = jnp.dot(hidden, down, preferred_element_type=F32)
    capacity = out_refs[0].shape[0]
    for d, out_ref in enumerate(out_refs):
        out_ref[...] = out[d * capacity : (d + 1) * capacity].astype(BF16)


def up_kernel(groups, *refs):
    own_ref, near_ref, up_ref, sems = refs[groups + 4 :]
    read = joined(refs[groups : groups + 4], up_ref, sems)
    hidden = hidden_of(refs[:groups], read())
    capacity = own_ref.shape[0]
    own_ref[...] = hidden[:capacity].astype(BF16)
    near_ref[...] = hidden[capacity:].astype(BF16)


def far_kernel(groups, *refs):
    up_ref, down_refs = refs[groups], refs[groups + 1 : groups + 5]
    *out_refs, down_ref, sems = refs[groups + 5 :]
    read = joined(down_refs, down_ref, sems)
    hidden = hidden_of(refs[:groups], up_ref[...])
    outputs_of(hidden.astype(BF16), read(), out_refs)


def down_kernel(groups, hidden_ref, down_ref, *out_refs):
    outputs_of(hidden_ref[...], down_ref[...], out_refs)


def ffn_kernel(groups, *refs):
    up_ref, down_ref = refs[groups : groups + 2]
    hidden = hidden_of(refs[:groups], up_ref[...]).astype(BF16)
    outputs_of(hidden, down_ref[...], refs[groups + 2 :])


def home_kernel(groups, hidden_ref, *refs):
    *down_refs, out_ref = refs
    size = down_refs[0].shape[0]
    hidden = hidden_ref[...]
    out_ref[...] = sum(
        jnp.dot(hidden[:, i * size : (i + 1) * size], ref[...], preferred_element_type=F32)
        for i, ref in enumerate(down_refs)
    ).astype(BF16)


def expert_call(kernel, groups, inputs, outs, shape, products):
    (capacity, width), units = shape
    rows = groups * capacity
    return pl.pallas_call(
        functools.partial(kernel, groups),
        out_shape=[jax.ShapeDtypeStruct(shape, BF16) for shape in outs],
        in_specs=[VMEM] * len(inputs),
        out_specs=[VMEM] * len(outs),
        scratch_shapes=[pltpu.SemaphoreType.DMA((4,))] if kernel in (up_kernel, far_kernel) else [],
        cost_estimate=pl.CostEstimate(
            flops=2 * products * rows * units * width,
            bytes_accessed=2 * products * width * (rows + units),
            transcendentals=rows * units,
        ),
        compiler_params=pltpu.CompilerParams(vmem_limit_bytes=VMEM_LIMIT),
    )(*inputs)


def slot_weights(info, first, count, dtype):
    slots = first + lax.broadcasted_iota(jnp.int32, (info.shape[0], count), 1)
    return sum(
        jnp.where(slots == info[:, k : k + 1].astype(jnp.int32), info[:, k + 2 : k + 3], 0.0)
        for k in range(2)
    ).astype(dtype)


def parts_of(weights):
    high = weights.astype(BF16)
    return high, (weights - high.astype(F32)).astype(BF16)


def taken(high, low, results):
    return jnp.dot(high, results, preferred_element_type=F32) + jnp.dot(
        low, results, preferred_element_type=F32
    )


def mix_kernel(late, x_ref, info_ref, *refs):
    result_refs, (sum_ref, high_ref, low_ref) = refs[:-3], refs[-3:]
    info = jnp.transpose(info_ref[...])
    results = jnp.concatenate([ref[...].astype(F32) for ref in result_refs], axis=0).astype(BF16)
    count = results.shape[0]
    high, low = parts_of(slot_weights(info, 0, count, F32))
    sum_ref[...] = x_ref[...].astype(F32) + taken(high, low, results)
    high_ref[...], low_ref[...] = parts_of(slot_weights(info, count, late, F32))


def last_kernel(sum_ref, high_ref, low_ref, *refs):
    results = jnp.concatenate([ref[...].astype(F32) for ref in refs[:-1]], axis=0).astype(BF16)
    refs[-1][...] = (sum_ref[...] + taken(high_ref[...], low_ref[...], results)).astype(BF16)


def combine_call(kernel, inputs, out_shape, slots):
    rows, width = inputs[0].shape
    return pl.pallas_call(
        kernel,
        out_shape=out_shape,
        in_specs=[VMEM] * len(inputs),
        out_specs=[VMEM] * len(out_shape),
        cost_estimate=pl.CostEstimate(
            flops=4 * rows * slots * width,
            bytes_accessed=2 * width * (3 * rows + slots),
            transcendentals=0,
        ),
        compiler_params=pltpu.CompilerParams(vmem_limit_bytes=VMEM_LIMIT),
    )(*inputs)


def step(carried, norm_gain, w_up, w_down, routes, gate_weights):
    half = lax.axis_size("expert") // 8
    x, routes_now = carried[0], routes[0, 0].T
    tok_rows, width = x.shape
    capacity = min(tok_rows, 4 * ((5 * tok_rows + 16 * half - 1) // (16 * half)))
    block = (capacity, width)
    up, down = w_up[0].T, w_down[0]
    units = (4 * up.shape[0], width)
    shape = (block, units[0])

    far_x = exchanged(x, 4 * (2 * half - 1))
    far_routes = exchanged(routes_now, 4 * (2 * half - 1))
    up_far, down_far = exchanged(up, 2), exchanged(down, 2)
    info, *own = sort(x, norm_gain, routes_now, gate_weights[0, 0].T, half, capacity)
    near = own[:1] + [exchanged(own[d], 4 * d) for d in range(1, half)]
    up_near, down_near = exchanged(up, 1), exchanged(down, 1)
    x_next, info_next = advanced(x, 0), advanced(info, 0)
    down_next = advanced(down, 0)
    down_next_far = exchanged(down_next, 2)
    downs_next = [down_next, exchanged(down_next, 1)]
    downs_next += [down_next_far, exchanged(down_next_far, 1)]
    ups = [up, up_near, up_far, exchanged(up_far, 1)]
    downs = [down, down_near, down_far, exchanged(down_far, 1)]
    hidden_own, hidden, up_all = expert_call(
        up_kernel,
        half,
        near + ups,
        [(capacity, units[0]), ((half - 1) * capacity, units[0]), units],
        shape,
        1,
    )
    hidden_next = advanced(hidden_own, 0)
    far, *relayed = sort(far_x, norm_gain, far_routes, None, half, capacity)
    relayed = [exchanged(rows, 4 * (d + 1)) for d, rows in enumerate(relayed)]
    far, down_all = expert_call(far_kernel, 1, [far, up_all] + downs, [block, units], shape, 2)
    near = expert_call(down_kernel, half - 1, [hidden, down_all], [block] * (half - 1), shape, 1)
    late = expert_call(
        ffn_kernel, half - 1, relayed + [up_all, down_all], [block] * (half - 1), shape, 2
    )
    results = list(expert_call(home_kernel, 1, [hidden_next] + downs_next, [block], shape, 1))
    results += [
        advanced(rows, 4 * place_of(d, half))
        for d, rows in enumerate([*near, far, *late], 1)
    ]
    count = (half - 1) * capacity
    sums = combine_call(
        functools.partial(mix_kernel, count),
        [x_next, info_next] + results[: half + 1],
        [jax.ShapeDtypeStruct(x.shape, F32)]
        + [jax.ShapeDtypeStruct((tok_rows, count), BF16)] * 2,
        (half + 1) * capacity,
    )
    (out,) = combine_call(
        last_kernel, [*sums, *results[half + 1 :]], [jax.ShapeDtypeStruct(x.shape, BF16)], count
    )
    return out[None]


def solution(mesh):
    in_specs = (
        P("section", "expert", None),
        P("section", None),
        P("section", None, "expert"),
        P("section", "expert", None),
        P(None, "section", "expert", None),
        P(None, "section", "expert", None),
    )
    out_specs = P("section", "expert", None)
    return jax.shard_map(step, mesh=mesh, in_specs=in_specs, out_specs=out_specs, check_vma=False)
```

time: 130 us -> 134 us (1.031)
  the two profiles are of different devices: /device:TPU:14 before, /device:TPU:0 now
where the time goes in v2:
time: 134 us; the launch traced here: 133 us
  waiting for transfers between devices  81.8 us (61%)
  starting transfers between devices  35.2 us (26%)
  Pallas kernels  11.4 us (9%)
  local copies, waits for them, and re-layouts  5.02 us (4%)
    ppermute x7, waiting for transfers between devices, advanced(): return lax.ppermute(value, ('section', 'expert'), pairs)  51.4 us
    ppermute x13, waiting for transfers between devices, exchanged(): lax.ppermute(value, 'expert', [(i, i ^ distance) for i in range(count)])  30.3 us
    ppermute x13, starting transfers between devices, exchanged(): lax.ppermute(value, 'expert', [(i, i ^ distance) for i in range(count)])  22.4 us
    ppermute x7, starting transfers between devices, advanced(): return lax.ppermute(value, ('section', 'expert'), pairs)  12.7 us
    pallas_call x5, Pallas kernels, expert_call(): pl.pallas_call(functools.partial(kernel, groups), out_shape=[jax.ShapeDty...  7.38 us
    unnamed x14, local copies, waits for them, and re-layouts  5.02 us
  transfers between devices with their start and end apart: 20, of which 9 were waited for; matrix products, arithmetic and copies ran while one was open for 0% of the time, Pallas kernels for 7%

profile of v2, /device:TPU:0, one launch (start us, length us, event | category | flops | bytes accessed | tf_op | source)
XLA Modules:
  0.0 133.4 jit_solution(2784921855242706920)
XLA Ops:
  0.5 1.1 copy-done.1
  1.6 0.7 copy-done.3
  3.7 0.7 sort.2
  4.4 2.7 %collective-permute-start.2 = (bf16[120,2048]{1,0:T(8,128)(2,1)S(1)}, bf16[120,2048]{1,0:T(8,128)(2,1)S(1)}, u32[]{:S(2)}, u32[]{:S(2)}) collective-permute-start(bf16[120,2048]{1,0:T(8,128)(2,1)S(1)} %get-tuple-element.20), channel_id=1, source_target_pairs={{0,4},{1,5},{2,6},{3,7},{4,0},{5,1},{6,2},{7,3},{8,12},{9,13},{10,... | collective-permute-start | bytes 1474568 | tf_op jit(solution)/shard_map/ppermute | solution.py:18
  7.1 1.5 %collective-permute-start.7 = (bf16[192,2048]{1,0:T(8,128)(2,1)}, bf16[192,2048]{1,0:T(8,128)(2,1)S(1)}, u32[]{:S(2)}, u32[]{:S(2)}) collective-permute-start(bf16[192,2048]{1,0:T(8,128)(2,1)} %bitcast.12), channel_id=1, source_target_pairs={{0,16},{1,17},{2,18},{3,19},{4,20},{5,21},{6,22},{7,23},{8,24},{9,... | collective-permute-start | bytes 2359304 | tf_op jit(solution)/shard_map/ppermute | solution.py:28
  8.6 1.5 %collective-permute-start.4 = (bf16[192,2048]{1,0:T(8,128)(2,1)}, bf16[192,2048]{1,0:T(8,128)(2,1)S(1)}, u32[]{:S(2)}, u32[]{:S(2)}) collective-permute-start(bf16[192,2048]{1,0:T(8,128)(2,1)} %bitcast.20), channel_id=1, source_target_pairs={{0,2},{1,3},{2,0},{3,1},{4,6},{5,7},{6,4},{7,5},{8,10},{9,11},{10,... | collective-permute-start | bytes 2359304 | tf_op jit(solution)/shard_map/ppermute | solution.py:18
  10.1 2.5 %collective-permute-start.12 = (s32[2,192]{1,0:T(2,128)S(1)}, s32[2,192]{1,0:T(2,128)S(1)}, u32[]{:S(2)}, u32[]{:S(2)}) collective-permute-start(s32[2,192]{1,0:T(2,128)S(1)} %bitcast.24), channel_id=1, source_target_pairs={{0,12},{1,13},{2,14},{3,15},{4,8},{5,9},{6,10},{7,11},{8,4},{9,5},... | collective-permute-start | bytes 4616 | tf_op jit(solution)/shard_map/ppermute | solution.py:18
  12.6 8.6 %collective-permute-done.12.routes_ref = s32[2,192]{1,0:T(2,128)S(1)} collective-permute-done((s32[2,192]{1,0:T(2,128)S(1)}, s32[2,192]{1,0:T(2,128)S(1)}, u32[]{:S(2)}, u32[]{:S(2)}) %collective-permute-start.12) | collective-permute-done | bytes 1568 | tf_op jit(solution)/shard_map/ppermute | solution.py:18
  21.1 1.5 %collective-permute-start.14 = (bf16[192,2048]{1,0:T(8,128)(2,1)}, bf16[192,2048]{1,0:T(8,128)(2,1)S(1)}, u32[]{:S(2)}, u32[]{:S(2)}) collective-permute-start(bf16[192,2048]{1,0:T(8,128)(2,1)} %bitcast.13), channel_id=1, source_target_pairs={{0,2},{1,3},{2,0},{3,1},{4,6},{5,7},{6,4},{7,5},{8,10},{9,11},{10,... | collective-permute-start | bytes 2359304 | tf_op jit(solution)/shard_map/ppermute | solution.py:18
  22.7 1.5 %collective-permute-start.11 = (bf16[192,2048]{1,0:T(8,128)(2,1)}, bf16[192,2048]{1,0:T(8,128)(2,1)S(1)}, u32[]{:S(2)}, u32[]{:S(2)}) collective-permute-start(bf16[192,2048]{1,0:T(8,128)(2,1)} %bitcast.16), channel_id=1, source_target_pairs={{0,12},{1,13},{2,14},{3,15},{4,8},{5,9},{6,10},{7,11},{8,4},{9,5},... | collective-permute-start | bytes 2359304 | tf_op jit(solution)/shard_map/ppermute | solution.py:18
  24.1 2.8 %collective-permute-done.7.refs_0_ = bf16[192,2048]{1,0:T(8,128)(2,1)S(1)} collective-permute-done((bf16[192,2048]{1,0:T(8,128)(2,1)}, bf16[192,2048]{1,0:T(8,128)(2,1)S(1)}, u32[]{:S(2)}, u32[]{:S(2)}) %collective-permute-start.7) | collective-permute-done | bytes 786464 | tf_op jit(solution)/shard_map/ppermute | solution.py:28
  26.9 1.5 %collective-permute-start.9 = (bf16[192,2048]{1,0:T(8,128)(2,1)S(1)}, bf16[192,2048]{1,0:T(8,128)(2,1)S(1)}, u32[]{:S(2)}, u32[]{:S(2)}) collective-permute-start(bf16[192,2048]{1,0:T(8,128)(2,1)S(1)} %collective-permute-done.7.refs_0_), channel_id=1, source_target_pairs={{0,2},{1,3},{2,0},{3,1},{4,6},{5,7},{6,4},{7,5},{8,10},{9,11},{10,... | collective-permute-start | bytes 2359304 | tf_op jit(solution)/shard_map/ppermute | solution.py:18
  28.4 0.8 collective-permute-done.4.refs_4_
  29.2 16.8 %collective-permute-done.14.refs_4_ = bf16[192,2048]{1,0:T(8,128)(2,1)S(1)} collective-permute-done((bf16[192,2048]{1,0:T(8,128)(2,1)}, bf16[192,2048]{1,0:T(8,128)(2,1)S(1)}, u32[]{:S(2)}, u32[]{:S(2)}) %collective-permute-start.14) | collective-permute-done | bytes 786464 | tf_op jit(solution)/shard_map/ppermute | solution.py:18
  46.6 0.7 copy-done.4
  48.0 10.2 %collective-permute-start.18 = (bf16[120,2048]{1,0:T(8,128)(2,1)S(1)}, bf16[120,2048]{1,0:T(8,128)(2,1)S(1)}, u32[]{:S(2)}, u32[]{:S(2)}) collective-permute-start(bf16[120,2048]{1,0:T(8,128)(2,1)S(1)} %get-tuple-element.30), channel_id=1, source_target_pairs={{0,4},{1,5},{2,6},{3,7},{4,0},{5,1},{6,2},{7,3},{8,12},{9,13},{10,... | collective-permute-start | bytes 1474568 | tf_op jit(solution)/shard_map/ppermute | solution.py:18
  58.2 3.6 %collective-permute-done.9.refs_2_ = bf16[192,2048]{1,0:T(8,128)(2,1)S(1)} collective-permute-done((bf16[192,2048]{1,0:T(8,128)(2,1)S(1)}, bf16[192,2048]{1,0:T(8,128)(2,1)S(1)}, u32[]{:S(2)}, u32[]{:S(2)}) %collective-permute-start.9) | collective-permute-done | bytes 786464 | tf_op jit(solution)/shard_map/ppermute | solution.py:18
  62.4 1.1 copy-done.2
  63.5 1.4 %shard_map.64 = (bf16[120,768]{1,0:T(8,128)(2,1)S(1)}, bf16[120,768]{1,0:T(8,128)(2,1)S(1)}, bf16[768,2048]{1,0:T(8,128)(2,1)S(1)}) custom-call(bf16[120,2048]{1,0:T(8,128)(2,1)S(1)} %get-tuple-element.19.refs_0_, bf16[120,2048]{1,0:T(8,128)(2,1)S(1)} %collective-permute-done.2.refs_1_, bf16[192,2048]{1,0:T(8,128)(2,1)S(1)} %bitcast.21, ...), custom_call_target="tpu_custom_call" | custom-call | flops 754974720 | bytes 4128768 | tf_op jit(solution)/shard_map/pallas_call | solution.py:159
  64.9 1.5 %collective-permute-start.6 = (bf16[120,768]{1,0:T(8,128)(2,1)S(1)}, bf16[120,768]{1,0:T(8,128)(2,1)S(1)}, u32[]{:S(2)}, u32[]{:S(2)}) collective-permute-start(bf16[120,768]{1,0:T(8,128)(2,1)S(1)} %get-tuple-element.21), channel_id=1, source_target_pairs={{0,16},{1,17},{2,18},{3,19},{4,20},{5,21},{6,22},{7,23},{8,24},{9,... | collective-permute-start | bytes 552968 | tf_op jit(solution)/shard_map/ppermute | solution.py:28
  66.5 2.5 %shard_map.66 = (bf16[120,2048]{1,0:T(8,128)(2,1)S(1)}, bf16[768,2048]{1,0:T(8,128)(2,1)S(1)}) custom-call(bf16[120,2048]{1,0:T(8,128)(2,1)S(1)} %get-tuple-element.23.refs_0_, bf16[768,2048]{1,0:T(8,128)(2,1)S(1)} %get-tuple-element.24.refs_1_, bf16[192,2048]{1,0:T(8,128)(2,1)S(1)} %bitcast.15, bf16[192,2048]{1,0:T(8,128)(2,1)S(1)} %collective-permute-done.13.refs_3_, ...), custom_call_target="tpu_custom_call" | custom-call | flops 754974720 | bytes 7274496 | tf_op jit(solution)/shard_map/pallas_call | solution.py:159
  70.1 2.7 %collective-permute-start.16 = (bf16[120,2048]{1,0:T(8,128)(2,1)S(1)}, bf16[120,2048]{1,0:T(8,128)(2,1)S(1)}, u32[]{:S(2)}, u32[]{:S(2)}) collective-permute-start(bf16[120,2048]{1,0:T(8,128)(2,1)S(1)} %shard_map.67), channel_id=1, source_target_pairs={{0,20},{1,21},{2,22},{3,23},{4,16},{5,17},{6,18},{7,19},{8,28},{9,... | collective-permute-start | bytes 1474568 | tf_op jit(solution)/shard_map/ppermute | solution.py:28
  72.8 2.5 %collective-permute-start.17 = (bf16[120,2048]{1,0:T(8,128)(2,1)S(1)}, bf16[120,2048]{1,0:T(8,128)(2,1)S(1)}, u32[]{:S(2)}, u32[]{:S(2)}) collective-permute-start(bf16[120,2048]{1,0:T(8,128)(2,1)S(1)} %get-tuple-element.26), channel_id=1, source_target_pairs={{0,28},{1,29},{2,30},{3,31},{4,24},{5,25},{6,26},{7,27},{8,20},{9,... | collective-permute-start | bytes 1474568 | tf_op jit(solution)/shard_map/ppermute | solution.py:28
  75.2 2.1 %shard_map.69 = bf16[120,2048]{1,0:T(8,128)(2,1)S(1)} custom-call(bf16[120,2048]{1,0:T(8,128)(2,1)S(1)} %collective-permute-done.18.refs_0_, bf16[768,2048]{1,0:T(8,128)(2,1)S(1)} %get-tuple-element.24.refs_1_, bf16[768,2048]{1,0:T(8,128)(2,1)S(1)} %get-tuple-element.25.down_ref.refs_2_), custom_call_target="tpu_custom_call" | custom-call | flops 754974720 | bytes 7274496 | tf_op jit(solution)/shard_map/pallas_call | solution.py:159
  77.3 29.6 %collective-permute-done.6.hidden_ref = bf16[120,768]{1,0:T(8,128)(2,1)S(1)} collective-permute-done((bf16[120,768]{1,0:T(8,128)(2,1)S(1)}, bf16[120,768]{1,0:T(8,128)(2,1)S(1)}, u32[]{:S(2)}, u32[]{:S(2)}) %collective-permute-start.6) | collective-permute-done | bytes 184352 | tf_op jit(solution)/shard_map/ppermute | solution.py:28
  107.0 2.6 %collective-permute-start.19 = (bf16[120,2048]{1,0:T(8,128)(2,1)S(1)}, bf16[120,2048]{1,0:T(8,128)(2,1)S(1)}, u32[]{:S(2)}, u32[]{:S(2)}) collective-permute-start(bf16[120,2048]{1,0:T(8,128)(2,1)S(1)} %shard_map.69), channel_id=1, source_target_pairs={{0,24},{1,25},{2,26},{3,27},{4,28},{5,29},{6,30},{7,31},{8,16},{9,... | collective-permute-start | bytes 1474568 | tf_op jit(solution)/shard_map/ppermute | solution.py:28
  109.6 1.5 %collective-permute-start.1 = (f32[8,192]{1,0:T(8,128)S(1)}, f32[8,192]{1,0:T(8,128)S(1)}, u32[]{:S(2)}, u32[]{:S(2)}) collective-permute-start(f32[8,192]{1,0:T(8,128)S(1)} %get-tuple-element.18), channel_id=1, source_target_pairs={{0,16},{1,17},{2,18},{3,19},{4,20},{5,21},{6,22},{7,23},{8,24},{9,... | collective-permute-start | bytes 18440 | tf_op jit(solution)/shard_map/ppermute | solution.py:28
  111.1 0.7 shard_map.65.refs_0_
  111.8 1.4 %collective-permute-done.1.info_ref = f32[8,192]{1,0:T(8,128)S(1)} collective-permute-done((f32[8,192]{1,0:T(8,128)S(1)}, f32[8,192]{1,0:T(8,128)S(1)}, u32[]{:S(2)}, u32[]{:S(2)}) %collective-permute-start.1) | collective-permute-done | bytes 6176 | tf_op jit(solution)/shard_map/ppermute | solution.py:28
  113.2 1.2 shard_map.68
  114.4 17.6 %collective-permute-done.19.refs_0_ = bf16[120,2048]{1,0:T(8,128)(2,1)S(1)} collective-permute-done((bf16[120,2048]{1,0:T(8,128)(2,1)S(1)}, bf16[120,2048]{1,0:T(8,128)(2,1)S(1)}, u32[]{:S(2)}, u32[]{:S(2)}) %collective-permute-start.19) | collective-permute-done | bytes 491552 | tf_op jit(solution)/shard_map/ppermute | solution.py:28
  132.0 1.4 %shard_map.70 = bf16[192,2048]{1,0:T(8,128)(2,1)} custom-call(f32[192,2048]{1,0:T(8,128)S(1)} %get-tuple-element.27.sum_ref, bf16[192,120]{1,0:T(8,128)(2,1)S(1)} %get-tuple-element.28.high_ref, bf16[192,120]{1,0:T(8,128)(2,1)S(1)} %get-tuple-element.29.low_ref, bf16[120,2048]{1,0:T(8,128)(2,1)S(1)} %collective-permute-done.19.refs_0_), custom_call_target="tpu_custom_call" | custom-call | flops 188743680 | bytes 2850816 | tf_op jit(solution)/shard_map/pallas_call | solution.py:210
  (31 shorter events, 4.7 us)
Async XLA Ops:
  0.0 66.5 %copy-start = (bf16[1,192,2048]{2,1,0:T(8,128)(2,1)S(1)}, bf16[1,192,2048]{2,1,0:T(8,128)(2,1)}, u32[]{:S(2)}) copy-start(bf16[1,192,2048]{2,1,0:T(8,128)(2,1)} %param.9) | copy-start | bytes 2359300
  0.0 24.1 %collective-permute-start.3 = (bf16[192,2048]{1,0:T(8,128)(2,1)}, bf16[192,2048]{1,0:T(8,128)(2,1)S(1)}, u32[]{:S(2)}, u32[]{:S(2)}) collective-permute-start(bf16[192,2048]{1,0:T(8,128)(2,1)} %bitcast.19), channel_id=1, source_target_pairs={{0,1},{1,0},{2,3},{3,2},{4,5},{5,4},{6,7},{7,6},{8,9},{9,8},{10,11... | collective-permute-start | bytes 2359304 | tf_op jit(solution)/shard_map/ppermute | solution.py:18
  0.5 1.1 copy-start.1
  1.6 0.7 copy-start.3
  2.3 0.7 copy-start.5
  3.0 0.7 copy-start.6
  4.4 18.3 %collective-permute-start.2 = (bf16[120,2048]{1,0:T(8,128)(2,1)S(1)}, bf16[120,2048]{1,0:T(8,128)(2,1)S(1)}, u32[]{:S(2)}, u32[]{:S(2)}) collective-permute-start(bf16[120,2048]{1,0:T(8,128)(2,1)S(1)} %get-tuple-element.20), channel_id=1, source_target_pairs={{0,4},{1,5},{2,6},{3,7},{4,0},{5,1},{6,2},{7,3},{8,12},{9,13},{10,... | collective-permute-start | bytes 1474568 | tf_op jit(solution)/shard_map/ppermute | solution.py:18
  7.1 19.8 %collective-permute-start.7 = (bf16[192,2048]{1,0:T(8,128)(2,1)}, bf16[192,2048]{1,0:T(8,128)(2,1)S(1)}, u32[]{:S(2)}, u32[]{:S(2)}) collective-permute-start(bf16[192,2048]{1,0:T(8,128)(2,1)} %bitcast.12), channel_id=1, source_target_pairs={{0,16},{1,17},{2,18},{3,19},{4,20},{5,21},{6,22},{7,23},{8,24},{9,... | collective-permute-start | bytes 2359304 | tf_op jit(solution)/shard_map/ppermute | solution.py:28
  8.6 20.6 %collective-permute-start.4 = (bf16[192,2048]{1,0:T(8,128)(2,1)}, bf16[192,2048]{1,0:T(8,128)(2,1)S(1)}, u32[]{:S(2)}, u32[]{:S(2)}) collective-permute-start(bf16[192,2048]{1,0:T(8,128)(2,1)} %bitcast.20), channel_id=1, source_target_pairs={{0,2},{1,3},{2,0},{3,1},{4,6},{5,7},{6,4},{7,5},{8,10},{9,11},{10,... | collective-permute-start | bytes 2359304 | tf_op jit(solution)/shard_map/ppermute | solution.py:18
  10.1 11.0 %collective-permute-start.12 = (s32[2,192]{1,0:T(2,128)S(1)}, s32[2,192]{1,0:T(2,128)S(1)}, u32[]{:S(2)}, u32[]{:S(2)}) collective-permute-start(s32[2,192]{1,0:T(2,128)S(1)} %bitcast.24), channel_id=1, source_target_pairs={{0,12},{1,13},{2,14},{3,15},{4,8},{5,9},{6,10},{7,11},{8,4},{9,5},... | collective-permute-start | bytes 4616 | tf_op jit(solution)/shard_map/ppermute | solution.py:18
  21.1 24.9 %collective-permute-start.14 = (bf16[192,2048]{1,0:T(8,128)(2,1)}, bf16[192,2048]{1,0:T(8,128)(2,1)S(1)}, u32[]{:S(2)}, u32[]{:S(2)}) collective-permute-start(bf16[192,2048]{1,0:T(8,128)(2,1)} %bitcast.13), channel_id=1, source_target_pairs={{0,2},{1,3},{2,0},{3,1},{4,6},{5,7},{6,4},{7,5},{8,10},{9,11},{10,... | collective-permute-start | bytes 2359304 | tf_op jit(solution)/shard_map/ppermute | solution.py:18
  22.7 23.4 %collective-permute-start.11 = (bf16[192,2048]{1,0:T(8,128)(2,1)}, bf16[192,2048]{1,0:T(8,128)(2,1)S(1)}, u32[]{:S(2)}, u32[]{:S(2)}) collective-permute-start(bf16[192,2048]{1,0:T(8,128)(2,1)} %bitcast.16), channel_id=1, source_target_pairs={{0,12},{1,13},{2,14},{3,15},{4,8},{5,9},{6,10},{7,11},{8,4},{9,5},... | collective-permute-start | bytes 2359304 | tf_op jit(solution)/shard_map/ppermute | solution.py:18
  24.1 23.8 %collective-permute-start.13 = (bf16[192,2048]{1,0:T(8,128)(2,1)}, bf16[192,2048]{1,0:T(8,128)(2,1)S(1)}, u32[]{:S(2)}, u32[]{:S(2)}) collective-permute-start(bf16[192,2048]{1,0:T(8,128)(2,1)} %bitcast.14), channel_id=1, source_target_pairs={{0,1},{1,0},{2,3},{3,2},{4,5},{5,4},{6,7},{7,6},{8,9},{9,8},{10,11... | collective-permute-start | bytes 2359304 | tf_op jit(solution)/shard_map/ppermute | solution.py:18
  26.9 34.9 %collective-permute-start.9 = (bf16[192,2048]{1,0:T(8,128)(2,1)S(1)}, bf16[192,2048]{1,0:T(8,128)(2,1)S(1)}, u32[]{:S(2)}, u32[]{:S(2)}) collective-permute-start(bf16[192,2048]{1,0:T(8,128)(2,1)S(1)} %collective-permute-done.7.refs_0_), channel_id=1, source_target_pairs={{0,2},{1,3},{2,0},{3,1},{4,6},{5,7},{6,4},{7,5},{8,10},{9,11},{10,... | collective-permute-start | bytes 2359304 | tf_op jit(solution)/shard_map/ppermute | solution.py:18
  29.2 32.6 %collective-permute-start.5 = (bf16[192,2048]{1,0:T(8,128)(2,1)S(1)}, bf16[192,2048]{1,0:T(8,128)(2,1)S(1)}, u32[]{:S(2)}, u32[]{:S(2)}) collective-permute-start(bf16[192,2048]{1,0:T(8,128)(2,1)S(1)} %collective-permute-done.4.refs_4_), channel_id=1, source_target_pairs={{0,1},{1,0},{2,3},{3,2},{4,5},{5,4},{6,7},{7,6},{8,9},{9,8},{10,11... | collective-permute-start | bytes 2359304 | tf_op jit(solution)/shard_map/ppermute | solution.py:18
  46.1 18.9 %collective-permute-start.15 = (bf16[192,2048]{1,0:T(8,128)(2,1)S(1)}, bf16[192,2048]{1,0:T(8,128)(2,1)S(1)}, u32[]{:S(2)}, u32[]{:S(2)}) collective-permute-start(bf16[192,2048]{1,0:T(8,128)(2,1)S(1)} %collective-permute-done.14.refs_4_), channel_id=1, source_target_pairs={{0,1},{1,0},{2,3},{3,2},{4,5},{5,4},{6,7},{7,6},{8,9},{9,8},{10,11... | collective-permute-start | bytes 2359304 | tf_op jit(solution)/shard_map/ppermute | solution.py:18
  46.1 26.7 %collective-permute-start.8 = (bf16[192,2048]{1,0:T(8,128)(2,1)S(1)}, bf16[192,2048]{1,0:T(8,128)(2,1)S(1)}, u32[]{:S(2)}, u32[]{:S(2)}) collective-permute-start(bf16[192,2048]{1,0:T(8,128)(2,1)S(1)} %collective-permute-done.7.refs_0_), channel_id=1, source_target_pairs={{0,1},{1,0},{2,3},{3,2},{4,5},{5,4},{6,7},{7,6},{8,9},{9,8},{10,11... | collective-permute-start | bytes 2359304 | tf_op jit(solution)/shard_map/ppermute | solution.py:18
  46.6 0.7 copy-start.4
  48.0 22.1 %collective-permute-start.18 = (bf16[120,2048]{1,0:T(8,128)(2,1)S(1)}, bf16[120,2048]{1,0:T(8,128)(2,1)S(1)}, u32[]{:S(2)}, u32[]{:S(2)}) collective-permute-start(bf16[120,2048]{1,0:T(8,128)(2,1)S(1)} %get-tuple-element.30), channel_id=1, source_target_pairs={{0,4},{1,5},{2,6},{3,7},{4,0},{5,1},{6,2},{7,3},{8,12},{9,13},{10,... | collective-permute-start | bytes 1474568 | tf_op jit(solution)/shard_map/ppermute | solution.py:18
  61.8 47.8 %collective-permute-start.10 = (bf16[192,2048]{1,0:T(8,128)(2,1)S(1)}, bf16[192,2048]{1,0:T(8,128)(2,1)S(1)}, u32[]{:S(2)}, u32[]{:S(2)}) collective-permute-start(bf16[192,2048]{1,0:T(8,128)(2,1)S(1)} %collective-permute-done.9.refs_2_), channel_id=1, source_target_pairs={{0,1},{1,0},{2,3},{3,2},{4,5},{5,4},{6,7},{7,6},{8,9},{9,8},{10,11... | collective-permute-start | bytes 2359304 | tf_op jit(solution)/shard_map/ppermute | solution.py:18
  61.8 51.4 %collective-permute-start = (bf16[192,2048]{1,0:T(8,128)(2,1)}, bf16[192,2048]{1,0:T(8,128)(2,1)S(1)}, u32[]{:S(2)}, u32[]{:S(2)}) collective-permute-start(bf16[192,2048]{1,0:T(8,128)(2,1)} %bitcast.17), channel_id=1, source_target_pairs={{0,16},{1,17},{2,18},{3,19},{4,20},{5,21},{6,22},{7,23},{8,24},{9,... | collective-permute-start | bytes 2359304 | tf_op jit(solution)/shard_map/ppermute | solution.py:28
  62.4 1.1 copy-start.2
  64.9 42.1 %collective-permute-start.6 = (bf16[120,768]{1,0:T(8,128)(2,1)S(1)}, bf16[120,768]{1,0:T(8,128)(2,1)S(1)}, u32[]{:S(2)}, u32[]{:S(2)}) collective-permute-start(bf16[120,768]{1,0:T(8,128)(2,1)S(1)} %get-tuple-element.21), channel_id=1, source_target_pairs={{0,16},{1,17},{2,18},{3,19},{4,20},{5,21},{6,22},{7,23},{8,24},{9,... | collective-permute-start | bytes 552968 | tf_op jit(solution)/shard_map/ppermute | solution.py:28
  70.1 43.1 %collective-permute-start.16 = (bf16[120,2048]{1,0:T(8,128)(2,1)S(1)}, bf16[120,2048]{1,0:T(8,128)(2,1)S(1)}, u32[]{:S(2)}, u32[]{:S(2)}) collective-permute-start(bf16[120,2048]{1,0:T(8,128)(2,1)S(1)} %shard_map.67), channel_id=1, source_target_pairs={{0,20},{1,21},{2,22},{3,23},{4,16},{5,17},{6,18},{7,19},{8,28},{9,... | collective-permute-start | bytes 1474568 | tf_op jit(solution)/shard_map/ppermute | solution.py:28
  72.8 40.5 %collective-permute-start.17 = (bf16[120,2048]{1,0:T(8,128)(2,1)S(1)}, bf16[120,2048]{1,0:T(8,128)(2,1)S(1)}, u32[]{:S(2)}, u32[]{:S(2)}) collective-permute-start(bf16[120,2048]{1,0:T(8,128)(2,1)S(1)} %get-tuple-element.26), channel_id=1, source_target_pairs={{0,28},{1,29},{2,30},{3,31},{4,24},{5,25},{6,26},{7,27},{8,20},{9,... | collective-permute-start | bytes 1474568 | tf_op jit(solution)/shard_map/ppermute | solution.py:28
  107.0 25.0 %collective-permute-start.19 = (bf16[120,2048]{1,0:T(8,128)(2,1)S(1)}, bf16[120,2048]{1,0:T(8,128)(2,1)S(1)}, u32[]{:S(2)}, u32[]{:S(2)}) collective-permute-start(bf16[120,2048]{1,0:T(8,128)(2,1)S(1)} %shard_map.69), channel_id=1, source_target_pairs={{0,24},{1,25},{2,26},{3,27},{4,28},{5,29},{6,30},{7,31},{8,16},{9,... | collective-permute-start | bytes 1474568 | tf_op jit(solution)/shard_map/ppermute | solution.py:28
  109.6 3.7 %collective-permute-start.1 = (f32[8,192]{1,0:T(8,128)S(1)}, f32[8,192]{1,0:T(8,128)S(1)}, u32[]{:S(2)}, u32[]{:S(2)}) collective-permute-start(f32[8,192]{1,0:T(8,128)S(1)} %get-tuple-element.18), channel_id=1, source_target_pairs={{0,16},{1,17},{2,18},{3,19},{4,20},{5,21},{6,22},{7,23},{8,24},{9,... | collective-permute-start | bytes 18440 | tf_op jit(solution)/shard_map/ppermute | solution.py:28

commit v3 on v2

--- a/solution.py
+++ b/solution.py
@@ -125,12 +125,13 @@
     near_ref[...] = hidden[capacity:].astype(BF16)
 
 
-def far_kernel(groups, *refs):
-    up_ref, down_refs = refs[groups], refs[groups + 1 : groups + 5]
-    *out_refs, down_ref, sems = refs[groups + 5 :]
-    read = joined(down_refs, down_ref, sems)
-    hidden = hidden_of(refs[:groups], up_ref[...])
-    outputs_of(hidden.astype(BF16), read(), out_refs)
+def rise_kernel(groups, *refs):
+    refs[-1][...] = hidden_of(refs[:groups], refs[groups][...]).astype(BF16)
+
+
+def fall_kernel(groups, hidden_ref, *refs):
+    *out_refs, down_ref, sems = refs[4:]
+    outputs_of(hidden_ref[...], joined(refs[:4], down_ref, sems)(), out_refs)
 
 
 def down_kernel(groups, hidden_ref, down_ref, *out_refs):
@@ -161,7 +162,7 @@
         out_shape=[jax.ShapeDtypeStruct(shape, BF16) for shape in outs],
         in_specs=[VMEM] * len(inputs),
         out_specs=[VMEM] * len(outs),
-        scratch_shapes=[pltpu.SemaphoreType.DMA((4,))] if kernel in (up_kernel, far_kernel) else [],
+        scratch_shapes=[pltpu.SemaphoreType.DMA((4,))] if kernel in (up_kernel, fall_kernel) else [],
         cost_estimate=pl.CostEstimate(
             flops=2 * products * rows * units * width,
             bytes_accessed=2 * products * width * (rows + units),
@@ -255,7 +256,8 @@
     hidden_next = advanced(hidden_own, 0)
     far, *relayed = sort(far_x, norm_gain, far_routes, None, half, capacity)
     relayed = [exchanged(rows, 4 * (d + 1)) for d, rows in enumerate(relayed)]
-    far, down_all = expert_call(far_kernel, 1, [far, up_all] + downs, [block, units], shape, 2)
+    (rise,) = expert_call(rise_kernel, 1, [far, up_all], [(capacity, units[0])], shape, 1)
+    far, down_all = expert_call(fall_kernel, 1, [rise, *downs], [block, units], shape, 1)
     near = expert_call(down_kernel, half - 1, [hidden, down_all], [block] * (half - 1), shape, 1)
     late = expert_call(
         ffn_kernel, half - 1, relayed + [up_all, down_all], [block] * (half - 1), shape, 2

time: 134 us -> 134 us (level)
    unnamed x14 -> x12, local copies, waits for them, and re-layouts: 5.02 us -> 4.33 us
    pallas_call x5 -> x6, Pallas kernels: 7.38 us -> 6.98 us  [expert_call(): pl.pallas_call(functools.partial(kernel, groups), out_shape=[jax.ShapeDty...]
where the time goes in v3:
time: 134 us; the launch traced here: 133 us
  waiting for transfers between devices  83 us (62%)
  starting transfers between devices  35 us (26%)
  Pallas kernels  11 us (8%)
  local copies, waits for them, and re-layouts  4.33 us (3%)
    ppermute x7, waiting for transfers between devices, advanced(): return lax.ppermute(value, ('section', 'expert'), pairs)  52.2 us
    ppermute x13, waiting for transfers between devices, exchanged(): lax.ppermute(value, 'expert', [(i, i ^ distance) for i in range(count)])  30.7 us
    ppermute x13, starting transfers between devices, exchanged(): lax.ppermute(value, 'expert', [(i, i ^ distance) for i in range(count)])  22.3 us
    ppermute x7, starting transfers between devices, advanced(): return lax.ppermute(value, ('section', 'expert'), pairs)  12.8 us
    pallas_call x6, Pallas kernels, expert_call(): pl.pallas_call(functools.partial(kernel, groups), out_shape=[jax.ShapeDty...  6.98 us
    unnamed x12, local copies, waits for them, and re-layouts  4.33 us
  transfers between devices with their start and end apart: 20, of which 9 were waited for; matrix products, arithmetic and copies ran while one was open for 0% of the time, Pallas kernels for 7%

profile of v3, /device:TPU:0, one launch (start us, length us, event | category | flops | bytes accessed | tf_op | source)
XLA Modules:
  0.0 133.4 jit_solution(9243762792212676564)
XLA Ops:
  0.5 1.1 copy-done
  1.6 0.7 copy-done.3
  3.7 0.7 sort.2
  4.4 2.6 %collective-permute-start.2 = (bf16[120,2048]{1,0:T(8,128)(2,1)S(1)}, bf16[120,2048]{1,0:T(8,128)(2,1)S(1)}, u32[]{:S(2)}, u32[]{:S(2)}) collective-permute-start(bf16[120,2048]{1,0:T(8,128)(2,1)S(1)} %get-tuple-element.20), channel_id=1, source_target_pairs={{0,4},{1,5},{2,6},{3,7},{4,0},{5,1},{6,2},{7,3},{8,12},{9,13},{10,... | collective-permute-start | bytes 1474568 | tf_op jit(solution)/shard_map/ppermute | solution.py:18
  7.0 1.5 %collective-permute-start.7 = (bf16[192,2048]{1,0:T(8,128)(2,1)}, bf16[192,2048]{1,0:T(8,128)(2,1)S(1)}, u32[]{:S(2)}, u32[]{:S(2)}) collective-permute-start(bf16[192,2048]{1,0:T(8,128)(2,1)} %bitcast.15), channel_id=1, source_target_pairs={{0,16},{1,17},{2,18},{3,19},{4,20},{5,21},{6,22},{7,23},{8,24},{9,... | collective-permute-start | bytes 2359304 | tf_op jit(solution)/shard_map/ppermute | solution.py:28
  8.5 1.5 %collective-permute-start.4 = (bf16[192,2048]{1,0:T(8,128)(2,1)}, bf16[192,2048]{1,0:T(8,128)(2,1)S(1)}, u32[]{:S(2)}, u32[]{:S(2)}) collective-permute-start(bf16[192,2048]{1,0:T(8,128)(2,1)} %bitcast.20), channel_id=1, source_target_pairs={{0,2},{1,3},{2,0},{3,1},{4,6},{5,7},{6,4},{7,5},{8,10},{9,11},{10,... | collective-permute-start | bytes 2359304 | tf_op jit(solution)/shard_map/ppermute | solution.py:18
  10.0 2.5 %collective-permute-start.12 = (s32[2,192]{1,0:T(2,128)S(1)}, s32[2,192]{1,0:T(2,128)S(1)}, u32[]{:S(2)}, u32[]{:S(2)}) collective-permute-start(s32[2,192]{1,0:T(2,128)S(1)} %bitcast.24), channel_id=1, source_target_pairs={{0,12},{1,13},{2,14},{3,15},{4,8},{5,9},{6,10},{7,11},{8,4},{9,5},... | collective-permute-start | bytes 4616 | tf_op jit(solution)/shard_map/ppermute | solution.py:18
  12.5 8.6 %collective-permute-done.12.routes_ref = s32[2,192]{1,0:T(2,128)S(1)} collective-permute-done((s32[2,192]{1,0:T(2,128)S(1)}, s32[2,192]{1,0:T(2,128)S(1)}, u32[]{:S(2)}, u32[]{:S(2)}) %collective-permute-start.12) | collective-permute-done | bytes 1568 | tf_op jit(solution)/shard_map/ppermute | solution.py:18
  21.1 1.5 %collective-permute-start.14 = (bf16[192,2048]{1,0:T(8,128)(2,1)}, bf16[192,2048]{1,0:T(8,128)(2,1)S(1)}, u32[]{:S(2)}, u32[]{:S(2)}) collective-permute-start(bf16[192,2048]{1,0:T(8,128)(2,1)} %bitcast.16), channel_id=1, source_target_pairs={{0,2},{1,3},{2,0},{3,1},{4,6},{5,7},{6,4},{7,5},{8,10},{9,11},{10,... | collective-permute-start | bytes 2359304 | tf_op jit(solution)/shard_map/ppermute | solution.py:18
  22.7 1.4 %collective-permute-start.11 = (bf16[192,2048]{1,0:T(8,128)(2,1)S(1)}, bf16[192,2048]{1,0:T(8,128)(2,1)S(1)}, u32[]{:S(2)}, u32[]{:S(2)}) collective-permute-start(bf16[192,2048]{1,0:T(8,128)(2,1)S(1)} %bitcast.14), channel_id=1, source_target_pairs={{0,12},{1,13},{2,14},{3,15},{4,8},{5,9},{6,10},{7,11},{8,4},{9,5},... | collective-permute-start | bytes 2359304 | tf_op jit(solution)/shard_map/ppermute | solution.py:18
  24.1 2.8 %collective-permute-done.7.refs_0_ = bf16[192,2048]{1,0:T(8,128)(2,1)S(1)} collective-permute-done((bf16[192,2048]{1,0:T(8,128)(2,1)}, bf16[192,2048]{1,0:T(8,128)(2,1)S(1)}, u32[]{:S(2)}, u32[]{:S(2)}) %collective-permute-start.7) | collective-permute-done | bytes 786464 | tf_op jit(solution)/shard_map/ppermute | solution.py:28
  26.9 1.5 %collective-permute-start.9 = (bf16[192,2048]{1,0:T(8,128)(2,1)S(1)}, bf16[192,2048]{1,0:T(8,128)(2,1)S(1)}, u32[]{:S(2)}, u32[]{:S(2)}) collective-permute-start(bf16[192,2048]{1,0:T(8,128)(2,1)S(1)} %collective-permute-done.7.refs_0_), channel_id=1, source_target_pairs={{0,2},{1,3},{2,0},{3,1},{4,6},{5,7},{6,4},{7,5},{8,10},{9,11},{10,... | collective-permute-start | bytes 2359304 | tf_op jit(solution)/shard_map/ppermute | solution.py:18
  28.4 0.7 collective-permute-done.4.refs_4_
  29.1 16.8 %collective-permute-done.14.refs_2_ = bf16[192,2048]{1,0:T(8,128)(2,1)S(1)} collective-permute-done((bf16[192,2048]{1,0:T(8,128)(2,1)}, bf16[192,2048]{1,0:T(8,128)(2,1)S(1)}, u32[]{:S(2)}, u32[]{:S(2)}) %collective-permute-start.14) | collective-permute-done | bytes 786464 | tf_op jit(solution)/shard_map/ppermute | solution.py:18
  47.2 10.2 %collective-permute-start.18 = (bf16[120,2048]{1,0:T(8,128)(2,1)S(1)}, bf16[120,2048]{1,0:T(8,128)(2,1)S(1)}, u32[]{:S(2)}, u32[]{:S(2)}) collective-permute-start(bf16[120,2048]{1,0:T(8,128)(2,1)S(1)} %get-tuple-element.30), channel_id=1, source_target_pairs={{0,4},{1,5},{2,6},{3,7},{4,0},{5,1},{6,2},{7,3},{8,12},{9,13},{10,... | collective-permute-start | bytes 1474568 | tf_op jit(solution)/shard_map/ppermute | solution.py:18
  57.4 4.5 %collective-permute-done.9.refs_2_ = bf16[192,2048]{1,0:T(8,128)(2,1)S(1)} collective-permute-done((bf16[192,2048]{1,0:T(8,128)(2,1)S(1)}, bf16[192,2048]{1,0:T(8,128)(2,1)S(1)}, u32[]{:S(2)}, u32[]{:S(2)}) %collective-permute-start.9) | collective-permute-done | bytes 786464 | tf_op jit(solution)/shard_map/ppermute | solution.py:18
  62.4 1.1 copy-done.2
  63.5 1.4 %shard_map.64 = (bf16[120,768]{1,0:T(8,128)(2,1)S(1)}, bf16[120,768]{1,0:T(8,128)(2,1)S(1)}, bf16[768,2048]{1,0:T(8,128)(2,1)S(1)}) custom-call(bf16[120,2048]{1,0:T(8,128)(2,1)S(1)} %get-tuple-element.19.refs_0_, bf16[120,2048]{1,0:T(8,128)(2,1)S(1)} %collective-permute-done.2.refs_1_, bf16[192,2048]{1,0:T(8,128)(2,1)S(1)} %bitcast.21, ...), custom_call_target="tpu_custom_call" | custom-call | flops 754974720 | bytes 4128768 | tf_op jit(solution)/shard_map/pallas_call | solution.py:160
  64.9 1.6 %collective-permute-start.6 = (bf16[120,768]{1,0:T(8,128)(2,1)S(1)}, bf16[120,768]{1,0:T(8,128)(2,1)S(1)}, u32[]{:S(2)}, u32[]{:S(2)}) collective-permute-start(bf16[120,768]{1,0:T(8,128)(2,1)S(1)} %get-tuple-element.21), channel_id=1, source_target_pairs={{0,16},{1,17},{2,18},{3,19},{4,20},{5,21},{6,22},{7,23},{8,24},{9,... | collective-permute-start | bytes 552968 | tf_op jit(solution)/shard_map/ppermute | solution.py:28
  66.5 1.2 shard_map.66.hidden_ref
  67.7 0.8 shard_map.67
  69.2 2.7 %collective-permute-start.16 = (bf16[120,2048]{1,0:T(8,128)(2,1)S(1)}, bf16[120,2048]{1,0:T(8,128)(2,1)S(1)}, u32[]{:S(2)}, u32[]{:S(2)}) collective-permute-start(bf16[120,2048]{1,0:T(8,128)(2,1)S(1)} %shard_map.68), channel_id=1, source_target_pairs={{0,20},{1,21},{2,22},{3,23},{4,16},{5,17},{6,18},{7,19},{8,28},{9,... | collective-permute-start | bytes 1474568 | tf_op jit(solution)/shard_map/ppermute | solution.py:28
  71.9 2.5 %collective-permute-start.17 = (bf16[120,2048]{1,0:T(8,128)(2,1)S(1)}, bf16[120,2048]{1,0:T(8,128)(2,1)S(1)}, u32[]{:S(2)}, u32[]{:S(2)}) collective-permute-start(bf16[120,2048]{1,0:T(8,128)(2,1)S(1)} %get-tuple-element.26), channel_id=1, source_target_pairs={{0,28},{1,29},{2,30},{3,31},{4,24},{5,25},{6,26},{7,27},{8,20},{9,... | collective-permute-start | bytes 1474568 | tf_op jit(solution)/shard_map/ppermute | solution.py:28
  74.4 2.2 %shard_map.70 = bf16[120,2048]{1,0:T(8,128)(2,1)S(1)} custom-call(bf16[120,2048]{1,0:T(8,128)(2,1)S(1)} %collective-permute-done.18.refs_0_, bf16[768,2048]{1,0:T(8,128)(2,1)S(1)} %get-tuple-element.24.refs_1_, bf16[768,2048]{1,0:T(8,128)(2,1)S(1)} %get-tuple-element.25.down_ref.refs_2_), custom_call_target="tpu_custom_call" | custom-call | flops 754974720 | bytes 7274496 | tf_op jit(solution)/shard_map/pallas_call | solution.py:160
  76.5 30.5 %collective-permute-done.6.hidden_ref = bf16[120,768]{1,0:T(8,128)(2,1)S(1)} collective-permute-done((bf16[120,768]{1,0:T(8,128)(2,1)S(1)}, bf16[120,768]{1,0:T(8,128)(2,1)S(1)}, u32[]{:S(2)}, u32[]{:S(2)}) %collective-permute-start.6) | collective-permute-done | bytes 184352 | tf_op jit(solution)/shard_map/ppermute | solution.py:28
  107.0 2.6 %collective-permute-start.19 = (bf16[120,2048]{1,0:T(8,128)(2,1)S(1)}, bf16[120,2048]{1,0:T(8,128)(2,1)S(1)}, u32[]{:S(2)}, u32[]{:S(2)}) collective-permute-start(bf16[120,2048]{1,0:T(8,128)(2,1)S(1)} %shard_map.70), channel_id=1, source_target_pairs={{0,24},{1,25},{2,26},{3,27},{4,28},{5,29},{6,30},{7,31},{8,16},{9,... | collective-permute-start | bytes 1474568 | tf_op jit(solution)/shard_map/ppermute | solution.py:28
  109.6 1.5 %collective-permute-start.1 = (f32[8,192]{1,0:T(8,128)S(1)}, f32[8,192]{1,0:T(8,128)S(1)}, u32[]{:S(2)}, u32[]{:S(2)}) collective-permute-start(f32[8,192]{1,0:T(8,128)S(1)} %get-tuple-element.18), channel_id=1, source_target_pairs={{0,16},{1,17},{2,18},{3,19},{4,20},{5,21},{6,22},{7,23},{8,24},{9,... | collective-permute-start | bytes 18440 | tf_op jit(solution)/shard_map/ppermute | solution.py:28
  111.1 0.7 shard_map.65.refs_0_
  111.8 1.4 %collective-permute-done.1.info_ref = f32[8,192]{1,0:T(8,128)S(1)} collective-permute-done((f32[8,192]{1,0:T(8,128)S(1)}, f32[8,192]{1,0:T(8,128)S(1)}, u32[]{:S(2)}, u32[]{:S(2)}) %collective-permute-start.1) | collective-permute-done | bytes 6176 | tf_op jit(solution)/shard_map/ppermute | solution.py:28
  113.2 1.2 shard_map.69
  114.4 17.6 %collective-permute-done.19.refs_0_ = bf16[120,2048]{1,0:T(8,128)(2,1)S(1)} collective-permute-done((bf16[120,2048]{1,0:T(8,128)(2,1)S(1)}, bf16[120,2048]{1,0:T(8,128)(2,1)S(1)}, u32[]{:S(2)}, u32[]{:S(2)}) %collective-permute-start.19) | collective-permute-done | bytes 491552 | tf_op jit(solution)/shard_map/ppermute | solution.py:28
  132.0 1.4 %shard_map.71 = bf16[192,2048]{1,0:T(8,128)(2,1)} custom-call(f32[192,2048]{1,0:T(8,128)S(1)} %get-tuple-element.27.sum_ref, bf16[192,120]{1,0:T(8,128)(2,1)S(1)} %get-tuple-element.28.high_ref, bf16[192,120]{1,0:T(8,128)(2,1)S(1)} %get-tuple-element.29.low_ref, bf16[120,2048]{1,0:T(8,128)(2,1)S(1)} %collective-permute-done.19.refs_0_), custom_call_target="tpu_custom_call" | custom-call | flops 188743680 | bytes 2850816 | tf_op jit(solution)/shard_map/pallas_call | solution.py:211
  (30 shorter events, 4.3 us)
Async XLA Ops:
  0.0 24.1 %collective-permute-start.3 = (bf16[192,2048]{1,0:T(8,128)(2,1)}, bf16[192,2048]{1,0:T(8,128)(2,1)S(1)}, u32[]{:S(2)}, u32[]{:S(2)}) collective-permute-start(bf16[192,2048]{1,0:T(8,128)(2,1)} %bitcast.19), channel_id=1, source_target_pairs={{0,1},{1,0},{2,3},{3,2},{4,5},{5,4},{6,7},{7,6},{8,9},{9,8},{10,11... | collective-permute-start | bytes 2359304 | tf_op jit(solution)/shard_map/ppermute | solution.py:18
  0.5 1.1 copy-start
  1.6 0.7 copy-start.3
  2.3 0.7 copy-start.4
  3.0 0.7 copy-start.5
  4.4 18.3 %collective-permute-start.2 = (bf16[120,2048]{1,0:T(8,128)(2,1)S(1)}, bf16[120,2048]{1,0:T(8,128)(2,1)S(1)}, u32[]{:S(2)}, u32[]{:S(2)}) collective-permute-start(bf16[120,2048]{1,0:T(8,128)(2,1)S(1)} %get-tuple-element.20), channel_id=1, source_target_pairs={{0,4},{1,5},{2,6},{3,7},{4,0},{5,1},{6,2},{7,3},{8,12},{9,13},{10,... | collective-permute-start | bytes 1474568 | tf_op jit(solution)/shard_map/ppermute | solution.py:18
  7.0 19.9 %collective-permute-start.7 = (bf16[192,2048]{1,0:T(8,128)(2,1)}, bf16[192,2048]{1,0:T(8,128)(2,1)S(1)}, u32[]{:S(2)}, u32[]{:S(2)}) collective-permute-start(bf16[192,2048]{1,0:T(8,128)(2,1)} %bitcast.15), channel_id=1, source_target_pairs={{0,16},{1,17},{2,18},{3,19},{4,20},{5,21},{6,22},{7,23},{8,24},{9,... | collective-permute-start | bytes 2359304 | tf_op jit(solution)/shard_map/ppermute | solution.py:28
  8.5 20.6 %collective-permute-start.4 = (bf16[192,2048]{1,0:T(8,128)(2,1)}, bf16[192,2048]{1,0:T(8,128)(2,1)S(1)}, u32[]{:S(2)}, u32[]{:S(2)}) collective-permute-start(bf16[192,2048]{1,0:T(8,128)(2,1)} %bitcast.20), channel_id=1, source_target_pairs={{0,2},{1,3},{2,0},{3,1},{4,6},{5,7},{6,4},{7,5},{8,10},{9,11},{10,... | collective-permute-start | bytes 2359304 | tf_op jit(solution)/shard_map/ppermute | solution.py:18
  10.0 11.1 %collective-permute-start.12 = (s32[2,192]{1,0:T(2,128)S(1)}, s32[2,192]{1,0:T(2,128)S(1)}, u32[]{:S(2)}, u32[]{:S(2)}) collective-permute-start(s32[2,192]{1,0:T(2,128)S(1)} %bitcast.24), channel_id=1, source_target_pairs={{0,12},{1,13},{2,14},{3,15},{4,8},{5,9},{6,10},{7,11},{8,4},{9,5},... | collective-permute-start | bytes 4616 | tf_op jit(solution)/shard_map/ppermute | solution.py:18
  21.1 24.8 %collective-permute-start.14 = (bf16[192,2048]{1,0:T(8,128)(2,1)}, bf16[192,2048]{1,0:T(8,128)(2,1)S(1)}, u32[]{:S(2)}, u32[]{:S(2)}) collective-permute-start(bf16[192,2048]{1,0:T(8,128)(2,1)} %bitcast.16), channel_id=1, source_target_pairs={{0,2},{1,3},{2,0},{3,1},{4,6},{5,7},{6,4},{7,5},{8,10},{9,11},{10,... | collective-permute-start | bytes 2359304 | tf_op jit(solution)/shard_map/ppermute | solution.py:18
  22.7 23.3 %collective-permute-start.11 = (bf16[192,2048]{1,0:T(8,128)(2,1)S(1)}, bf16[192,2048]{1,0:T(8,128)(2,1)S(1)}, u32[]{:S(2)}, u32[]{:S(2)}) collective-permute-start(bf16[192,2048]{1,0:T(8,128)(2,1)S(1)} %bitcast.14), channel_id=1, source_target_pairs={{0,12},{1,13},{2,14},{3,15},{4,8},{5,9},{6,10},{7,11},{8,4},{9,5},... | collective-permute-start | bytes 2359304 | tf_op jit(solution)/shard_map/ppermute | solution.py:18
  24.1 23.1 %collective-permute-start.13 = (bf16[192,2048]{1,0:T(8,128)(2,1)}, bf16[192,2048]{1,0:T(8,128)(2,1)S(1)}, u32[]{:S(2)}, u32[]{:S(2)}) collective-permute-start(bf16[192,2048]{1,0:T(8,128)(2,1)} %bitcast.17), channel_id=1, source_target_pairs={{0,1},{1,0},{2,3},{3,2},{4,5},{5,4},{6,7},{7,6},{8,9},{9,8},{10,11... | collective-permute-start | bytes 2359304 | tf_op jit(solution)/shard_map/ppermute | solution.py:18
  26.9 34.9 %collective-permute-start.9 = (bf16[192,2048]{1,0:T(8,128)(2,1)S(1)}, bf16[192,2048]{1,0:T(8,128)(2,1)S(1)}, u32[]{:S(2)}, u32[]{:S(2)}) collective-permute-start(bf16[192,2048]{1,0:T(8,128)(2,1)S(1)} %collective-permute-done.7.refs_0_), channel_id=1, source_target_pairs={{0,2},{1,3},{2,0},{3,1},{4,6},{5,7},{6,4},{7,5},{8,10},{9,11},{10,... | collective-permute-start | bytes 2359304 | tf_op jit(solution)/shard_map/ppermute | solution.py:18
  29.1 32.7 %collective-permute-start.5 = (bf16[192,2048]{1,0:T(8,128)(2,1)S(1)}, bf16[192,2048]{1,0:T(8,128)(2,1)S(1)}, u32[]{:S(2)}, u32[]{:S(2)}) collective-permute-start(bf16[192,2048]{1,0:T(8,128)(2,1)S(1)} %collective-permute-done.4.refs_4_), channel_id=1, source_target_pairs={{0,1},{1,0},{2,3},{3,2},{4,5},{5,4},{6,7},{7,6},{8,9},{9,8},{10,11... | collective-permute-start | bytes 2359304 | tf_op jit(solution)/shard_map/ppermute | solution.py:18
  46.0 18.9 %collective-permute-start.15 = (bf16[192,2048]{1,0:T(8,128)(2,1)S(1)}, bf16[192,2048]{1,0:T(8,128)(2,1)S(1)}, u32[]{:S(2)}, u32[]{:S(2)}) collective-permute-start(bf16[192,2048]{1,0:T(8,128)(2,1)S(1)} %collective-permute-done.14.refs_2_), channel_id=1, source_target_pairs={{0,1},{1,0},{2,3},{3,2},{4,5},{5,4},{6,7},{7,6},{8,9},{9,8},{10,11... | collective-permute-start | bytes 2359304 | tf_op jit(solution)/shard_map/ppermute | solution.py:18
  46.0 25.9 %collective-permute-start.8 = (bf16[192,2048]{1,0:T(8,128)(2,1)S(1)}, bf16[192,2048]{1,0:T(8,128)(2,1)S(1)}, u32[]{:S(2)}, u32[]{:S(2)}) collective-permute-start(bf16[192,2048]{1,0:T(8,128)(2,1)S(1)} %collective-permute-done.7.refs_0_), channel_id=1, source_target_pairs={{0,1},{1,0},{2,3},{3,2},{4,5},{5,4},{6,7},{7,6},{8,9},{9,8},{10,11... | collective-permute-start | bytes 2359304 | tf_op jit(solution)/shard_map/ppermute | solution.py:18
  47.2 22.1 %collective-permute-start.18 = (bf16[120,2048]{1,0:T(8,128)(2,1)S(1)}, bf16[120,2048]{1,0:T(8,128)(2,1)S(1)}, u32[]{:S(2)}, u32[]{:S(2)}) collective-permute-start(bf16[120,2048]{1,0:T(8,128)(2,1)S(1)} %get-tuple-element.30), channel_id=1, source_target_pairs={{0,4},{1,5},{2,6},{3,7},{4,0},{5,1},{6,2},{7,3},{8,12},{9,13},{10,... | collective-permute-start | bytes 1474568 | tf_op jit(solution)/shard_map/ppermute | solution.py:18
  61.8 47.8 %collective-permute-start.10 = (bf16[192,2048]{1,0:T(8,128)(2,1)S(1)}, bf16[192,2048]{1,0:T(8,128)(2,1)S(1)}, u32[]{:S(2)}, u32[]{:S(2)}) collective-permute-start(bf16[192,2048]{1,0:T(8,128)(2,1)S(1)} %collective-permute-done.9.refs_2_), channel_id=1, source_target_pairs={{0,1},{1,0},{2,3},{3,2},{4,5},{5,4},{6,7},{7,6},{8,9},{9,8},{10,11... | collective-permute-start | bytes 2359304 | tf_op jit(solution)/shard_map/ppermute | solution.py:18
  61.8 51.4 %collective-permute-start = (bf16[192,2048]{1,0:T(8,128)(2,1)}, bf16[192,2048]{1,0:T(8,128)(2,1)S(1)}, u32[]{:S(2)}, u32[]{:S(2)}) collective-permute-start(bf16[192,2048]{1,0:T(8,128)(2,1)} %bitcast.12), channel_id=1, source_target_pairs={{0,16},{1,17},{2,18},{3,19},{4,20},{5,21},{6,22},{7,23},{8,24},{9,... | collective-permute-start | bytes 2359304 | tf_op jit(solution)/shard_map/ppermute | solution.py:28
  62.3 1.1 copy-start.2
  63.5 4.2 %copy-start.1 = (bf16[1,192,2048]{2,1,0:T(8,128)(2,1)S(1)}, bf16[1,192,2048]{2,1,0:T(8,128)(2,1)}, u32[]{:S(2)}) copy-start(bf16[1,192,2048]{2,1,0:T(8,128)(2,1)} %param.9) | copy-start | bytes 2359300
  64.9 42.1 %collective-permute-start.6 = (bf16[120,768]{1,0:T(8,128)(2,1)S(1)}, bf16[120,768]{1,0:T(8,128)(2,1)S(1)}, u32[]{:S(2)}, u32[]{:S(2)}) collective-permute-start(bf16[120,768]{1,0:T(8,128)(2,1)S(1)} %get-tuple-element.21), channel_id=1, source_target_pairs={{0,16},{1,17},{2,18},{3,19},{4,20},{5,21},{6,22},{7,23},{8,24},{9,... | collective-permute-start | bytes 552968 | tf_op jit(solution)/shard_map/ppermute | solution.py:28
  69.2 44.0 %collective-permute-start.16 = (bf16[120,2048]{1,0:T(8,128)(2,1)S(1)}, bf16[120,2048]{1,0:T(8,128)(2,1)S(1)}, u32[]{:S(2)}, u32[]{:S(2)}) collective-permute-start(bf16[120,2048]{1,0:T(8,128)(2,1)S(1)} %shard_map.68), channel_id=1, source_target_pairs={{0,20},{1,21},{2,22},{3,23},{4,16},{5,17},{6,18},{7,19},{8,28},{9,... | collective-permute-start | bytes 1474568 | tf_op jit(solution)/shard_map/ppermute | solution.py:28
  71.9 41.3 %collective-permute-start.17 = (bf16[120,2048]{1,0:T(8,128)(2,1)S(1)}, bf16[120,2048]{1,0:T(8,128)(2,1)S(1)}, u32[]{:S(2)}, u32[]{:S(2)}) collective-permute-start(bf16[120,2048]{1,0:T(8,128)(2,1)S(1)} %get-tuple-element.26), channel_id=1, source_target_pairs={{0,28},{1,29},{2,30},{3,31},{4,24},{5,25},{6,26},{7,27},{8,20},{9,... | collective-permute-start | bytes 1474568 | tf_op jit(solution)/shard_map/ppermute | solution.py:28
  107.0 25.0 %collective-permute-start.19 = (bf16[120,2048]{1,0:T(8,128)(2,1)S(1)}, bf16[120,2048]{1,0:T(8,128)(2,1)S(1)}, u32[]{:S(2)}, u32[]{:S(2)}) collective-permute-start(bf16[120,2048]{1,0:T(8,128)(2,1)S(1)} %shard_map.70), channel_id=1, source_target_pairs={{0,24},{1,25},{2,26},{3,27},{4,28},{5,29},{6,30},{7,31},{8,16},{9,... | collective-permute-start | bytes 1474568 | tf_op jit(solution)/shard_map/ppermute | solution.py:28
  109.6 3.7 %collective-permute-start.1 = (f32[8,192]{1,0:T(8,128)S(1)}, f32[8,192]{1,0:T(8,128)S(1)}, u32[]{:S(2)}, u32[]{:S(2)}) collective-permute-start(f32[8,192]{1,0:T(8,128)S(1)} %get-tuple-element.18), channel_id=1, source_target_pairs={{0,16},{1,17},{2,18},{3,19},{4,20},{5,21},{6,22},{7,23},{8,24},{9,... | collective-permute-start | bytes 18440 | tf_op jit(solution)/shard_map/ppermute | solution.py:28

commit v4 on v3

--- a/solution.py
+++ b/solution.py
@@ -9,6 +9,7 @@
 
 
 VMEM = pl.BlockSpec(memory_space=pltpu.VMEM)
+ANY = pl.BlockSpec(memory_space=pl.ANY)
 VMEM_LIMIT = 32 * 2**20
 BF16, F32 = jnp.bfloat16, jnp.float32
 
@@ -30,6 +31,11 @@
 
 def place_of(distance, half):
     return distance + (distance >= half) * (3 * half - 1 - 2 * distance)
+
+
+def use_of(place, half):
+    near = (place > 0) & (place < half)
+    return jnp.where(place == half, 1, jnp.where(near, place + 1, place))
 
 
 def sort_kernel(blocks, capacity, with_info, x_ref, gain_ref, routes_ref, *refs):
@@ -47,12 +53,13 @@
     )
     p0 = jnp.sum(jnp.where(ids == r0, place, 0.0), axis=0, keepdims=True)
     p1 = jnp.sum(jnp.where(ids == r1, place, 0.0), axis=0, keepdims=True)
-    t0 = place_of(r0 ^ own, blocks) * capacity + p0.astype(jnp.int32)
-    t1 = place_of(r1 ^ own, blocks) * capacity + p1.astype(jnp.int32)
+    b0, b1 = place_of(r0 ^ own, blocks), place_of(r1 ^ own, blocks)
+    p0, p1 = p0.astype(jnp.int32), p1.astype(jnp.int32)
+    t0, t1 = b0 * capacity + p0, b1 * capacity + p1
     if with_info:
         gates_ref, info_ref = refs[:2]
-        info_ref[0:1, :] = t0.astype(F32)
-        info_ref[1:2, :] = t1.astype(F32)
+        info_ref[0:1, :] = (use_of(b0, blocks) * capacity + p0).astype(F32)
+        info_ref[1:2, :] = (use_of(b1, blocks) * capacity + p1).astype(F32)
         info_ref[2:4, :] = gates_ref[...]
         info_ref[4:8, :] = jnp.zeros((4, rows), F32)
     slots = lax.broadcasted_iota(jnp.int32, (blocks * capacity, rows), 0)
@@ -202,17 +209,30 @@
 
 
 def last_kernel(sum_ref, high_ref, low_ref, *refs):
-    results = jnp.concatenate([ref[...].astype(F32) for ref in refs[:-1]], axis=0).astype(BF16)
-    refs[-1][...] = (sum_ref[...] + taken(high_ref[...], low_ref[...], results)).astype(BF16)
-
-
-def combine_call(kernel, inputs, out_shape, slots):
+    *result_refs, out_ref, held, sems = refs
+    high, low = high_ref[...], low_ref[...]
+    pieces = sems.shape[0]
+    width = out_ref.shape[1] // pieces
+    copies = []
+    for i in range(pieces):
+        columns = pl.ds(i * width, width)
+        results = [ref[:, columns].astype(F32) for ref in result_refs]
+        results = jnp.concatenate(results, axis=0).astype(BF16)
+        held[:, columns] = (sum_ref[:, columns] + taken(high, low, results)).astype(BF16)
+        copies.append(pltpu.make_async_copy(held.at[:, columns], out_ref.at[:, columns], sems.at[i]))
+        copies[-1].start()
+    for copy in copies:
+        copy.wait()
+
+
+def combine_call(kernel, inputs, out_shape, slots, scratch=()):
     rows, width = inputs[0].shape
     return pl.pallas_call(
         kernel,
         out_shape=out_shape,
         in_specs=[VMEM] * len(inputs),
-        out_specs=[VMEM] * len(out_shape),
+        out_specs=[ANY if scratch else VMEM] * len(out_shape),
+        scratch_shapes=list(scratch),
         cost_estimate=pl.CostEstimate(
             flops=4 * rows * slots * width,
             bytes_accessed=2 * width * (3 * rows + slots),
@@ -267,16 +287,21 @@
         advanced(rows, 4 * place_of(d, half))
         for d, rows in enumerate([*near, far, *late], 1)
     ]
-    count = (half - 1) * capacity
+    results = [results[0], results[half], *results[1:half], *results[half + 1 :]]
+    count = (len(results) - 2) * capacity
     sums = combine_call(
         functools.partial(mix_kernel, count),
-        [x_next, info_next] + results[: half + 1],
+        [x_next, info_next] + results[:2],
         [jax.ShapeDtypeStruct(x.shape, F32)]
         + [jax.ShapeDtypeStruct((tok_rows, count), BF16)] * 2,
-        (half + 1) * capacity,
+        2 * capacity,
     )
     (out,) = combine_call(
-        last_kernel, [*sums, *results[half + 1 :]], [jax.ShapeDtypeStruct(x.shape, BF16)], count
+        last_kernel,
+        [*sums, *results[2:]],
+        [jax.ShapeDtypeStruct(x.shape, BF16)],
+        count,
+        [pltpu.VMEM(x.shape, BF16), pltpu.SemaphoreType.DMA((2,))],
     )
     return out[None]
 

time: 134 us -> 125 us (0.933)
  waiting for transfers between devices: 83 us -> 76.8 us
  starting transfers between devices: 35 us -> 33 us
    ppermute x7, waiting for transfers between devices: 52.2 us -> 48.3 us  [advanced(): return lax.ppermute(value, ('section', 'expert'), pairs)]
    ppermute x7, starting transfers between devices: 12.8 us -> 9.25 us  [advanced(): return lax.ppermute(value, ('section', 'expert'), pairs)]
    ppermute x13, waiting for transfers between devices: 30.7 us -> 28.5 us  [exchanged(): lax.ppermute(value, 'expert', [(i, i ^ distance) for i in range(count)])]
    ppermute x13, starting transfers between devices: 22.3 us -> 23.8 us  [exchanged(): lax.ppermute(value, 'expert', [(i, i ^ distance) for i in range(count)])]
  transfers between devices with their start and end apart: 20 -> 20, of which waited for: 9 -> 7; matrix products, arithmetic and copies ran while one was open for 0% -> 0% of each run, Pallas kernels for 7% -> 7%
where the time goes in v4:
time: 125 us
  waiting for transfers between devices  76.8 us (61%)
  starting transfers between devices  33 us (26%)
  Pallas kernels  10.4 us (8%)
  local copies, waits for them, and re-layouts  4.33 us (3%)
    ppermute x7, waiting for transfers between devices, advanced(): return lax.ppermute(value, ('section', 'expert'), pairs)  48.3 us
    ppermute x13, waiting for transfers between devices, exchanged(): lax.ppermute(value, 'expert', [(i, i ^ distance) for i in range(count)])  28.5 us
    ppermute x13, starting transfers between devices, exchanged(): lax.ppermute(value, 'expert', [(i, i ^ distance) for i in range(count)])  23.8 us
    ppermute x7, starting transfers between devices, advanced(): return lax.ppermute(value, ('section', 'expert'), pairs)  9.25 us
    pallas_call x6, Pallas kernels, expert_call(): pl.pallas_call(functools.partial(kernel, groups), out_shape=[jax.ShapeDty...  6.97 us
    unnamed x12, local copies, waits for them, and re-layouts  4.33 us
  transfers between devices with their start and end apart: 20, of which 7 were waited for; matrix products, arithmetic and copies ran while one was open for 0% of the time, Pallas kernels for 7%

profile of v4, /device:TPU:0, one launch (start us, length us, event | category | flops | bytes accessed | tf_op | source)
XLA Modules:
  0.0 124.7 jit_solution(6316419141251305001)
XLA Ops:
  0.0 3.0 %collective-permute-start.4 = (bf16[192,2048]{1,0:T(8,128)(2,1)}, bf16[192,2048]{1,0:T(8,128)(2,1)S(1)}, u32[]{:S(2)}, u32[]{:S(2)}) collective-permute-start(bf16[192,2048]{1,0:T(8,128)(2,1)} %bitcast.19), channel_id=1, source_target_pairs={{0,2},{1,3},{2,0},{3,1},{4,6},{5,7},{6,4},{7,5},{8,10},{9,11},{10,... | collective-permute-start | bytes 2359304 | tf_op jit(solution)/shard_map/ppermute | solution.py:19
  3.0 1.1 copy-done
  4.1 0.7 copy-done.3
  4.8 0.7 copy-done.4
  5.5 0.7 copy-done.5
  6.2 0.7 sort.2
  6.9 1.6 %collective-permute-start.2 = (bf16[120,2048]{1,0:T(8,128)(2,1)S(1)}, bf16[120,2048]{1,0:T(8,128)(2,1)S(1)}, u32[]{:S(2)}, u32[]{:S(2)}) collective-permute-start(bf16[120,2048]{1,0:T(8,128)(2,1)S(1)} %get-tuple-element.20), channel_id=1, source_target_pairs={{0,4},{1,5},{2,6},{3,7},{4,0},{5,1},{6,2},{7,3},{8,12},{9,13},{10,... | collective-permute-start | bytes 1474568 | tf_op jit(solution)/shard_map/ppermute | solution.py:19
  8.5 1.5 %collective-permute-start.7 = (bf16[192,2048]{1,0:T(8,128)(2,1)}, bf16[192,2048]{1,0:T(8,128)(2,1)S(1)}, u32[]{:S(2)}, u32[]{:S(2)}) collective-permute-start(bf16[192,2048]{1,0:T(8,128)(2,1)} %bitcast.15), channel_id=1, source_target_pairs={{0,16},{1,17},{2,18},{3,19},{4,20},{5,21},{6,22},{7,23},{8,24},{9,... | collective-permute-start | bytes 2359304 | tf_op jit(solution)/shard_map/ppermute | solution.py:29
  10.0 2.5 %collective-permute-start.12 = (s32[2,192]{1,0:T(2,128)S(1)}, s32[2,192]{1,0:T(2,128)S(1)}, u32[]{:S(2)}, u32[]{:S(2)}) collective-permute-start(s32[2,192]{1,0:T(2,128)S(1)} %bitcast.24), channel_id=1, source_target_pairs={{0,12},{1,13},{2,14},{3,15},{4,8},{5,9},{6,10},{7,11},{8,4},{9,5},... | collective-permute-start | bytes 4616 | tf_op jit(solution)/shard_map/ppermute | solution.py:19
  12.5 9.2 %collective-permute-done.12.routes_ref = s32[2,192]{1,0:T(2,128)S(1)} collective-permute-done((s32[2,192]{1,0:T(2,128)S(1)}, s32[2,192]{1,0:T(2,128)S(1)}, u32[]{:S(2)}, u32[]{:S(2)}) %collective-permute-start.12) | collective-permute-done | bytes 1568 | tf_op jit(solution)/shard_map/ppermute | solution.py:19
  22.2 1.5 %collective-permute-start.11 = (bf16[192,2048]{1,0:T(8,128)(2,1)S(1)}, bf16[192,2048]{1,0:T(8,128)(2,1)S(1)}, u32[]{:S(2)}, u32[]{:S(2)}) collective-permute-start(bf16[192,2048]{1,0:T(8,128)(2,1)S(1)} %bitcast.14), channel_id=1, source_target_pairs={{0,12},{1,13},{2,14},{3,15},{4,8},{5,9},{6,10},{7,11},{8,4},{9,5},... | collective-permute-start | bytes 2359304 | tf_op jit(solution)/shard_map/ppermute | solution.py:19
  23.6 3.8 %collective-permute-done.7.refs_0_ = bf16[192,2048]{1,0:T(8,128)(2,1)S(1)} collective-permute-done((bf16[192,2048]{1,0:T(8,128)(2,1)}, bf16[192,2048]{1,0:T(8,128)(2,1)S(1)}, u32[]{:S(2)}, u32[]{:S(2)}) %collective-permute-start.7) | collective-permute-done | bytes 786464 | tf_op jit(solution)/shard_map/ppermute | solution.py:29
  27.9 14.4 %collective-permute-done.14.refs_2_ = bf16[192,2048]{1,0:T(8,128)(2,1)S(1)} collective-permute-done((bf16[192,2048]{1,0:T(8,128)(2,1)}, bf16[192,2048]{1,0:T(8,128)(2,1)S(1)}, u32[]{:S(2)}, u32[]{:S(2)}) %collective-permute-start.14) | collective-permute-done | bytes 786464 | tf_op jit(solution)/shard_map/ppermute | solution.py:19
  42.8 0.7 sort.3
  43.5 13.4 %collective-permute-start.18 = (bf16[120,2048]{1,0:T(8,128)(2,1)S(1)}, bf16[120,2048]{1,0:T(8,128)(2,1)S(1)}, u32[]{:S(2)}, u32[]{:S(2)}) collective-permute-start(bf16[120,2048]{1,0:T(8,128)(2,1)S(1)} %get-tuple-element.30), channel_id=1, source_target_pairs={{0,4},{1,5},{2,6},{3,7},{4,0},{5,1},{6,2},{7,3},{8,12},{9,13},{10,... | collective-permute-start | bytes 1474568 | tf_op jit(solution)/shard_map/ppermute | solution.py:19
  57.2 1.5 %collective-permute-start = (bf16[192,2048]{1,0:T(8,128)(2,1)}, bf16[192,2048]{1,0:T(8,128)(2,1)S(1)}, u32[]{:S(2)}, u32[]{:S(2)}) collective-permute-start(bf16[192,2048]{1,0:T(8,128)(2,1)} %bitcast.12), channel_id=1, source_target_pairs={{0,16},{1,17},{2,18},{3,19},{4,20},{5,21},{6,22},{7,23},{8,24},{9,... | collective-permute-start | bytes 2359304 | tf_op jit(solution)/shard_map/ppermute | solution.py:29
  58.7 1.1 copy-done.2
  59.8 1.4 %shard_map.64 = (bf16[120,768]{1,0:T(8,128)(2,1)S(1)}, bf16[120,768]{1,0:T(8,128)(2,1)S(1)}, bf16[768,2048]{1,0:T(8,128)(2,1)S(1)}) custom-call(bf16[120,2048]{1,0:T(8,128)(2,1)S(1)} %get-tuple-element.19.refs_0_, bf16[120,2048]{1,0:T(8,128)(2,1)S(1)} %collective-permute-done.2.refs_1_, bf16[192,2048]{1,0:T(8,128)(2,1)S(1)} %bitcast.21, ...), custom_call_target="tpu_custom_call" | custom-call | flops 754974720 | bytes 4128768 | tf_op jit(solution)/shard_map/pallas_call | solution.py:167
  61.2 0.6 collective-permute-start.6
  61.8 1.2 shard_map.66.hidden_ref
  63.1 0.8 shard_map.67
  63.9 4.9 %collective-permute-done.18.refs_0_ = bf16[120,2048]{1,0:T(8,128)(2,1)S(1)} collective-permute-done((bf16[120,2048]{1,0:T(8,128)(2,1)S(1)}, bf16[120,2048]{1,0:T(8,128)(2,1)S(1)}, u32[]{:S(2)}, u32[]{:S(2)}) %collective-permute-start.18) | collective-permute-done | bytes 491552 | tf_op jit(solution)/shard_map/ppermute | solution.py:19
  68.8 3.4 %collective-permute-start.16 = (bf16[120,2048]{1,0:T(8,128)(2,1)S(1)}, bf16[120,2048]{1,0:T(8,128)(2,1)S(1)}, u32[]{:S(2)}, u32[]{:S(2)}) collective-permute-start(bf16[120,2048]{1,0:T(8,128)(2,1)S(1)} %get-tuple-element.24), channel_id=1, source_target_pairs={{0,28},{1,29},{2,30},{3,31},{4,24},{5,25},{6,26},{7,27},{8,20},{9,... | collective-permute-start | bytes 1474568 | tf_op jit(solution)/shard_map/ppermute | solution.py:29
  72.2 2.2 %shard_map.70 = bf16[120,2048]{1,0:T(8,128)(2,1)S(1)} custom-call(bf16[120,2048]{1,0:T(8,128)(2,1)S(1)} %collective-permute-done.18.refs_0_, bf16[768,2048]{1,0:T(8,128)(2,1)S(1)} %get-tuple-element.23.refs_1_, bf16[768,2048]{1,0:T(8,128)(2,1)S(1)} %get-tuple-element.29.down_ref.refs_2_), custom_call_target="tpu_custom_call" | custom-call | flops 754974720 | bytes 7274496 | tf_op jit(solution)/shard_map/pallas_call | solution.py:167
  75.0 0.8 collective-permute-start.19
  75.8 15.8 %collective-permute-done.6.hidden_ref = bf16[120,768]{1,0:T(8,128)(2,1)S(1)} collective-permute-done((bf16[120,768]{1,0:T(8,128)(2,1)S(1)}, bf16[120,768]{1,0:T(8,128)(2,1)S(1)}, u32[]{:S(2)}, u32[]{:S(2)}) %collective-permute-start.6) | collective-permute-done | bytes 184352 | tf_op jit(solution)/shard_map/ppermute | solution.py:29
  91.6 1.5 %collective-permute-start.1 = (f32[8,192]{1,0:T(8,128)S(1)}, f32[8,192]{1,0:T(8,128)S(1)}, u32[]{:S(2)}, u32[]{:S(2)}) collective-permute-start(f32[8,192]{1,0:T(8,128)S(1)} %get-tuple-element.18), channel_id=1, source_target_pairs={{0,16},{1,17},{2,18},{3,19},{4,20},{5,21},{6,22},{7,23},{8,24},{9,... | collective-permute-start | bytes 18440 | tf_op jit(solution)/shard_map/ppermute | solution.py:29
  93.1 0.7 shard_map.65.refs_0_
  93.9 2.2 %collective-permute-done.1.info_ref = f32[8,192]{1,0:T(8,128)S(1)} collective-permute-done((f32[8,192]{1,0:T(8,128)S(1)}, f32[8,192]{1,0:T(8,128)S(1)}, u32[]{:S(2)}, u32[]{:S(2)}) %collective-permute-start.1) | collective-permute-done | bytes 6176 | tf_op jit(solution)/shard_map/ppermute | solution.py:29
  96.1 0.8 shard_map.68
  96.9 26.4 %collective-permute-done.19.refs_1_ = bf16[120,2048]{1,0:T(8,128)(2,1)S(1)} collective-permute-done((bf16[120,2048]{1,0:T(8,128)(2,1)S(1)}, bf16[120,2048]{1,0:T(8,128)(2,1)S(1)}, u32[]{:S(2)}, u32[]{:S(2)}) %collective-permute-start.19) | collective-permute-done | bytes 491552 | tf_op jit(solution)/shard_map/ppermute | solution.py:29
  123.3 1.3 %shard_map.71 = bf16[192,2048]{1,0:T(8,128)(2,1)} custom-call(f32[192,2048]{1,0:T(8,128)S(1)} %get-tuple-element.25.sum_ref, bf16[192,240]{1,0:T(8,128)(2,1)S(1)} %get-tuple-element.26.high_ref, bf16[192,240]{1,0:T(8,128)(2,1)S(1)} %get-tuple-element.27.low_ref, bf16[120,2048]{1,0:T(8,128)(2,1)S(1)} %collective-permute-done.17.refs_0_, ...), custom_call_target="tpu_custom_call" | custom-call | flops 377487360 | bytes 3342336 | tf_op jit(solution)/shard_map/pallas_call | solution.py:230
  (30 shorter events, 2.4 us)
Async XLA Ops:
  0.0 23.6 %collective-permute-start.4 = (bf16[192,2048]{1,0:T(8,128)(2,1)}, bf16[192,2048]{1,0:T(8,128)(2,1)S(1)}, u32[]{:S(2)}, u32[]{:S(2)}) collective-permute-start(bf16[192,2048]{1,0:T(8,128)(2,1)} %bitcast.19), channel_id=1, source_target_pairs={{0,2},{1,3},{2,0},{3,1},{4,6},{5,7},{6,4},{7,5},{8,10},{9,11},{10,... | collective-permute-start | bytes 2359304 | tf_op jit(solution)/shard_map/ppermute | solution.py:19
  3.0 1.1 copy-start
  4.1 0.7 copy-start.3
  4.8 0.7 copy-start.4
  5.5 0.7 copy-start.5
  6.9 15.3 %collective-permute-start.2 = (bf16[120,2048]{1,0:T(8,128)(2,1)S(1)}, bf16[120,2048]{1,0:T(8,128)(2,1)S(1)}, u32[]{:S(2)}, u32[]{:S(2)}) collective-permute-start(bf16[120,2048]{1,0:T(8,128)(2,1)S(1)} %get-tuple-element.20), channel_id=1, source_target_pairs={{0,4},{1,5},{2,6},{3,7},{4,0},{5,1},{6,2},{7,3},{8,12},{9,13},{10,... | collective-permute-start | bytes 1474568 | tf_op jit(solution)/shard_map/ppermute | solution.py:19
  8.5 18.9 %collective-permute-start.7 = (bf16[192,2048]{1,0:T(8,128)(2,1)}, bf16[192,2048]{1,0:T(8,128)(2,1)S(1)}, u32[]{:S(2)}, u32[]{:S(2)}) collective-permute-start(bf16[192,2048]{1,0:T(8,128)(2,1)} %bitcast.15), channel_id=1, source_target_pairs={{0,16},{1,17},{2,18},{3,19},{4,20},{5,21},{6,22},{7,23},{8,24},{9,... | collective-permute-start | bytes 2359304 | tf_op jit(solution)/shard_map/ppermute | solution.py:29
  10.0 18.0 %collective-permute-start.3 = (bf16[192,2048]{1,0:T(8,128)(2,1)}, bf16[192,2048]{1,0:T(8,128)(2,1)S(1)}, u32[]{:S(2)}, u32[]{:S(2)}) collective-permute-start(bf16[192,2048]{1,0:T(8,128)(2,1)} %bitcast.20), channel_id=1, source_target_pairs={{0,1},{1,0},{2,3},{3,2},{4,5},{5,4},{6,7},{7,6},{8,9},{9,8},{10,11... | collective-permute-start | bytes 2359304 | tf_op jit(solution)/shard_map/ppermute | solution.py:19
  10.0 11.7 %collective-permute-start.12 = (s32[2,192]{1,0:T(2,128)S(1)}, s32[2,192]{1,0:T(2,128)S(1)}, u32[]{:S(2)}, u32[]{:S(2)}) collective-permute-start(s32[2,192]{1,0:T(2,128)S(1)} %bitcast.24), channel_id=1, source_target_pairs={{0,12},{1,13},{2,14},{3,15},{4,8},{5,9},{6,10},{7,11},{8,4},{9,5},... | collective-permute-start | bytes 4616 | tf_op jit(solution)/shard_map/ppermute | solution.py:19
  21.7 20.6 %collective-permute-start.14 = (bf16[192,2048]{1,0:T(8,128)(2,1)}, bf16[192,2048]{1,0:T(8,128)(2,1)S(1)}, u32[]{:S(2)}, u32[]{:S(2)}) collective-permute-start(bf16[192,2048]{1,0:T(8,128)(2,1)} %bitcast.16), channel_id=1, source_target_pairs={{0,2},{1,3},{2,0},{3,1},{4,6},{5,7},{6,4},{7,5},{8,10},{9,11},{10,... | collective-permute-start | bytes 2359304 | tf_op jit(solution)/shard_map/ppermute | solution.py:19
  22.2 20.1 %collective-permute-start.11 = (bf16[192,2048]{1,0:T(8,128)(2,1)S(1)}, bf16[192,2048]{1,0:T(8,128)(2,1)S(1)}, u32[]{:S(2)}, u32[]{:S(2)}) collective-permute-start(bf16[192,2048]{1,0:T(8,128)(2,1)S(1)} %bitcast.14), channel_id=1, source_target_pairs={{0,12},{1,13},{2,14},{3,15},{4,8},{5,9},{6,10},{7,11},{8,4},{9,5},... | collective-permute-start | bytes 2359304 | tf_op jit(solution)/shard_map/ppermute | solution.py:19
  23.6 19.9 %collective-permute-start.13 = (bf16[192,2048]{1,0:T(8,128)(2,1)}, bf16[192,2048]{1,0:T(8,128)(2,1)S(1)}, u32[]{:S(2)}, u32[]{:S(2)}) collective-permute-start(bf16[192,2048]{1,0:T(8,128)(2,1)} %bitcast.17), channel_id=1, source_target_pairs={{0,1},{1,0},{2,3},{3,2},{4,5},{5,4},{6,7},{7,6},{8,9},{9,8},{10,11... | collective-permute-start | bytes 2359304 | tf_op jit(solution)/shard_map/ppermute | solution.py:19
  27.4 29.5 %collective-permute-start.9 = (bf16[192,2048]{1,0:T(8,128)(2,1)S(1)}, bf16[192,2048]{1,0:T(8,128)(2,1)S(1)}, u32[]{:S(2)}, u32[]{:S(2)}) collective-permute-start(bf16[192,2048]{1,0:T(8,128)(2,1)S(1)} %collective-permute-done.7.refs_0_), channel_id=1, source_target_pairs={{0,2},{1,3},{2,0},{3,1},{4,6},{5,7},{6,4},{7,5},{8,10},{9,11},{10,... | collective-permute-start | bytes 2359304 | tf_op jit(solution)/shard_map/ppermute | solution.py:19
  27.9 29.2 %collective-permute-start.5 = (bf16[192,2048]{1,0:T(8,128)(2,1)S(1)}, bf16[192,2048]{1,0:T(8,128)(2,1)S(1)}, u32[]{:S(2)}, u32[]{:S(2)}) collective-permute-start(bf16[192,2048]{1,0:T(8,128)(2,1)S(1)} %collective-permute-done.4.refs_4_), channel_id=1, source_target_pairs={{0,1},{1,0},{2,3},{3,2},{4,5},{5,4},{6,7},{7,6},{8,9},{9,8},{10,11... | collective-permute-start | bytes 2359304 | tf_op jit(solution)/shard_map/ppermute | solution.py:19
  42.3 18.9 %collective-permute-start.15 = (bf16[192,2048]{1,0:T(8,128)(2,1)S(1)}, bf16[192,2048]{1,0:T(8,128)(2,1)S(1)}, u32[]{:S(2)}, u32[]{:S(2)}) collective-permute-start(bf16[192,2048]{1,0:T(8,128)(2,1)S(1)} %collective-permute-done.14.refs_2_), channel_id=1, source_target_pairs={{0,1},{1,0},{2,3},{3,2},{4,5},{5,4},{6,7},{7,6},{8,9},{9,8},{10,11... | collective-permute-start | bytes 2359304 | tf_op jit(solution)/shard_map/ppermute | solution.py:19
  42.3 32.7 %collective-permute-start.8 = (bf16[192,2048]{1,0:T(8,128)(2,1)S(1)}, bf16[192,2048]{1,0:T(8,128)(2,1)S(1)}, u32[]{:S(2)}, u32[]{:S(2)}) collective-permute-start(bf16[192,2048]{1,0:T(8,128)(2,1)S(1)} %collective-permute-done.7.refs_0_), channel_id=1, source_target_pairs={{0,1},{1,0},{2,3},{3,2},{4,5},{5,4},{6,7},{7,6},{8,9},{9,8},{10,11... | collective-permute-start | bytes 2359304 | tf_op jit(solution)/shard_map/ppermute | solution.py:19
  43.5 25.3 %collective-permute-start.18 = (bf16[120,2048]{1,0:T(8,128)(2,1)S(1)}, bf16[120,2048]{1,0:T(8,128)(2,1)S(1)}, u32[]{:S(2)}, u32[]{:S(2)}) collective-permute-start(bf16[120,2048]{1,0:T(8,128)(2,1)S(1)} %get-tuple-element.30), channel_id=1, source_target_pairs={{0,4},{1,5},{2,6},{3,7},{4,0},{5,1},{6,2},{7,3},{8,12},{9,13},{10,... | collective-permute-start | bytes 1474568 | tf_op jit(solution)/shard_map/ppermute | solution.py:19
  57.0 34.7 %collective-permute-start.10 = (bf16[192,2048]{1,0:T(8,128)(2,1)S(1)}, bf16[192,2048]{1,0:T(8,128)(2,1)S(1)}, u32[]{:S(2)}, u32[]{:S(2)}) collective-permute-start(bf16[192,2048]{1,0:T(8,128)(2,1)S(1)} %collective-permute-done.9.refs_2_), channel_id=1, source_target_pairs={{0,1},{1,0},{2,3},{3,2},{4,5},{5,4},{6,7},{7,6},{8,9},{9,8},{10,11... | collective-permute-start | bytes 2359304 | tf_op jit(solution)/shard_map/ppermute | solution.py:19
  57.2 38.9 %collective-permute-start = (bf16[192,2048]{1,0:T(8,128)(2,1)}, bf16[192,2048]{1,0:T(8,128)(2,1)S(1)}, u32[]{:S(2)}, u32[]{:S(2)}) collective-permute-start(bf16[192,2048]{1,0:T(8,128)(2,1)} %bitcast.12), channel_id=1, source_target_pairs={{0,16},{1,17},{2,18},{3,19},{4,20},{5,21},{6,22},{7,23},{8,24},{9,... | collective-permute-start | bytes 2359304 | tf_op jit(solution)/shard_map/ppermute | solution.py:29
  58.7 1.1 copy-start.2
  59.8 3.3 %copy-start.1 = (bf16[1,192,2048]{2,1,0:T(8,128)(2,1)S(1)}, bf16[1,192,2048]{2,1,0:T(8,128)(2,1)}, u32[]{:S(2)}) copy-start(bf16[1,192,2048]{2,1,0:T(8,128)(2,1)} %param.9) | copy-start | bytes 2359300
  61.2 30.4 %collective-permute-start.6 = (bf16[120,768]{1,0:T(8,128)(2,1)S(1)}, bf16[120,768]{1,0:T(8,128)(2,1)S(1)}, u32[]{:S(2)}, u32[]{:S(2)}) collective-permute-start(bf16[120,768]{1,0:T(8,128)(2,1)S(1)} %get-tuple-element.21), channel_id=1, source_target_pairs={{0,16},{1,17},{2,18},{3,19},{4,20},{5,21},{6,22},{7,23},{8,24},{9,... | collective-permute-start | bytes 552968 | tf_op jit(solution)/shard_map/ppermute | solution.py:29
  68.8 27.2 %collective-permute-start.16 = (bf16[120,2048]{1,0:T(8,128)(2,1)S(1)}, bf16[120,2048]{1,0:T(8,128)(2,1)S(1)}, u32[]{:S(2)}, u32[]{:S(2)}) collective-permute-start(bf16[120,2048]{1,0:T(8,128)(2,1)S(1)} %get-tuple-element.24), channel_id=1, source_target_pairs={{0,28},{1,29},{2,30},{3,31},{4,24},{5,25},{6,26},{7,27},{8,20},{9,... | collective-permute-start | bytes 1474568 | tf_op jit(solution)/shard_map/ppermute | solution.py:29
  75.0 48.3 %collective-permute-start.19 = (bf16[120,2048]{1,0:T(8,128)(2,1)S(1)}, bf16[120,2048]{1,0:T(8,128)(2,1)S(1)}, u32[]{:S(2)}, u32[]{:S(2)}) collective-permute-start(bf16[120,2048]{1,0:T(8,128)(2,1)S(1)} %shard_map.70), channel_id=1, source_target_pairs={{0,24},{1,25},{2,26},{3,27},{4,28},{5,29},{6,30},{7,31},{8,16},{9,... | collective-permute-start | bytes 1474568 | tf_op jit(solution)/shard_map/ppermute | solution.py:29
  91.6 31.7 %collective-permute-start.17 = (bf16[120,2048]{1,0:T(8,128)(2,1)S(1)}, bf16[120,2048]{1,0:T(8,128)(2,1)S(1)}, u32[]{:S(2)}, u32[]{:S(2)}) collective-permute-start(bf16[120,2048]{1,0:T(8,128)(2,1)S(1)} %shard_map.69), channel_id=1, source_target_pairs={{0,20},{1,21},{2,22},{3,23},{4,16},{5,17},{6,18},{7,19},{8,28},{9,... | collective-permute-start | bytes 1474568 | tf_op jit(solution)/shard_map/ppermute | solution.py:29
  91.6 4.5 %collective-permute-start.1 = (f32[8,192]{1,0:T(8,128)S(1)}, f32[8,192]{1,0:T(8,128)S(1)}, u32[]{:S(2)}, u32[]{:S(2)}) collective-permute-start(f32[8,192]{1,0:T(8,128)S(1)} %get-tuple-element.18), channel_id=1, source_target_pairs={{0,16},{1,17},{2,18},{3,19},{4,20},{5,21},{6,22},{7,23},{8,24},{9,... | collective-permute-start | bytes 18440 | tf_op jit(solution)/shard_map/ppermute | solution.py:29

commit v5 on v4

--- a/solution.py
+++ b/solution.py
@@ -124,12 +124,9 @@
 
 
 def up_kernel(groups, *refs):
-    own_ref, near_ref, up_ref, sems = refs[groups + 4 :]
+    own_ref, up_ref, sems = refs[groups + 4 :]
     read = joined(refs[groups : groups + 4], up_ref, sems)
-    hidden = hidden_of(refs[:groups], read())
-    capacity = own_ref.shape[0]
-    own_ref[...] = hidden[:capacity].astype(BF16)
-    near_ref[...] = hidden[capacity:].astype(BF16)
+    own_ref[...] = hidden_of(refs[:groups], read()).astype(BF16)
 
 
 def rise_kernel(groups, *refs):
@@ -139,10 +136,6 @@
 def fall_kernel(groups, hidden_ref, *refs):
     *out_refs, down_ref, sems = refs[4:]
     outputs_of(hidden_ref[...], joined(refs[:4], down_ref, sems)(), out_refs)
-
-
-def down_kernel(groups, hidden_ref, down_ref, *out_refs):
-    outputs_of(hidden_ref[...], down_ref[...], out_refs)
 
 
 def ffn_kernel(groups, *refs):
@@ -193,9 +186,9 @@
 
 
 def taken(high, low, results):
-    return jnp.dot(high, results, preferred_element_type=F32) + jnp.dot(
-        low, results, preferred_element_type=F32
-    )
+    rows = high.shape[0]
+    both = jnp.dot(jnp.concatenate([high, low], axis=0), results, preferred_element_type=F32)
+    return both[:rows] + both[rows:]
 
 
 def mix_kernel(late, x_ref, info_ref, *refs):
@@ -265,20 +258,17 @@
     downs_next += [down_next_far, exchanged(down_next_far, 1)]
     ups = [up, up_near, up_far, exchanged(up_far, 1)]
     downs = [down, down_near, down_far, exchanged(down_far, 1)]
-    hidden_own, hidden, up_all = expert_call(
-        up_kernel,
-        half,
-        near + ups,
-        [(capacity, units[0]), ((half - 1) * capacity, units[0]), units],
-        shape,
-        1,
+    hidden_own, up_all = expert_call(
+        up_kernel, 1, near[:1] + ups, [(capacity, units[0]), units], shape, 1
     )
     hidden_next = advanced(hidden_own, 0)
     far, *relayed = sort(far_x, norm_gain, far_routes, None, half, capacity)
     relayed = [exchanged(rows, 4 * (d + 1)) for d, rows in enumerate(relayed)]
     (rise,) = expert_call(rise_kernel, 1, [far, up_all], [(capacity, units[0])], shape, 1)
     far, down_all = expert_call(fall_kernel, 1, [rise, *downs], [block, units], shape, 1)
-    near = expert_call(down_kernel, half - 1, [hidden, down_all], [block] * (half - 1), shape, 1)
+    near = expert_call(
+        ffn_kernel, half - 1, near[1:] + [up_all, down_all], [block] * (half - 1), shape, 2
+    )
     late = expert_call(
         ffn_kernel, half - 1, relayed + [up_all, down_all], [block] * (half - 1), shape, 2
     )
@@ -301,7 +291,7 @@
         [*sums, *results[2:]],
         [jax.ShapeDtypeStruct(x.shape, BF16)],
         count,
-        [pltpu.VMEM(x.shape, BF16), pltpu.SemaphoreType.DMA((2,))],
+        [pltpu.VMEM(x.shape, BF16), pltpu.SemaphoreType.DMA((4,))],
     )
     return out[None]
 

time: 125 us -> 129 us (1.032)
  waiting for transfers between devices: 76.8 us -> 78.7 us
  Pallas kernels: 10.4 us -> 12 us
    ppermute x7, waiting for transfers between devices: 48.3 us -> 52.4 us  [advanced(): return lax.ppermute(value, ('section', 'expert'), pairs)]
    ppermute x13, waiting for transfers between devices: 28.5 us -> 26.3 us  [exchanged(): lax.ppermute(value, 'expert', [(i, i ^ distance) for i in range(count)])]
    pallas_call x6, Pallas kernels: 6.97 us -> 8.53 us  [expert_call(): pl.pallas_call(functools.partial(kernel, groups), out_shape=[jax.ShapeDty...]
    unnamed x12 -> x14, local copies, waits for them, and re-layouts: 4.33 us -> 5.02 us
  transfers between devices with their start and end apart: 20 -> 20, of which waited for: 7 -> 7; matrix products, arithmetic and copies ran while one was open for 0% -> 0% of each run, Pallas kernels for 7% -> 8%
where the time goes in v5:
time: 129 us
  waiting for transfers between devices  78.7 us (61%)
  starting transfers between devices  33.1 us (26%)
  Pallas kernels  12 us (9%)
  local copies, waits for them, and re-layouts  5.02 us (4%)
    ppermute x7, waiting for transfers between devices, advanced(): return lax.ppermute(value, ('section', 'expert'), pairs)  52.4 us
    ppermute x13, waiting for transfers between devices, exchanged(): lax.ppermute(value, 'expert', [(i, i ^ distance) for i in range(count)])  26.3 us
    ppermute x13, starting transfers between devices, exchanged(): lax.ppermute(value, 'expert', [(i, i ^ distance) for i in range(count)])  23.7 us
    ppermute x7, starting transfers between devices, advanced(): return lax.ppermute(value, ('section', 'expert'), pairs)  9.36 us
    pallas_call x6, Pallas kernels, expert_call(): pl.pallas_call(functools.partial(kernel, groups), out_shape=[jax.ShapeDty...  8.53 us
    unnamed x14, local copies, waits for them, and re-layouts  5.02 us
  transfers between devices with their start and end apart: 20, of which 7 were waited for; matrix products, arithmetic and copies ran while one was open for 0% of the time, Pallas kernels for 8%

profile of v5, /device:TPU:0, one launch (start us, length us, event | category | flops | bytes accessed | tf_op | source)
XLA Modules:
  0.0 128.9 jit_solution(10781367865666691885)
XLA Ops:
  0.0 3.0 %collective-permute-start.3 = (bf16[192,2048]{1,0:T(8,128)(2,1)}, bf16[192,2048]{1,0:T(8,128)(2,1)S(1)}, u32[]{:S(2)}, u32[]{:S(2)}) collective-permute-start(bf16[192,2048]{1,0:T(8,128)(2,1)} %bitcast.12), channel_id=1, source_target_pairs={{0,2},{1,3},{2,0},{3,1},{4,6},{5,7},{6,4},{7,5},{8,10},{9,11},{10,... | collective-permute-start | bytes 2359304 | tf_op jit(solution)/shard_map/ppermute | solution.py:19
  3.0 1.1 copy-done.1
  4.1 0.7 copy-done.3
  4.8 0.7 copy-done.5
  5.5 0.7 copy-done.6
  6.9 1.6 %collective-permute-start.16 = (bf16[120,2048]{1,0:T(8,128)(2,1)S(1)}, bf16[120,2048]{1,0:T(8,128)(2,1)S(1)}, u32[]{:S(2)}, u32[]{:S(2)}) collective-permute-start(bf16[120,2048]{1,0:T(8,128)(2,1)S(1)} %get-tuple-element.26), channel_id=1, source_target_pairs={{0,4},{1,5},{2,6},{3,7},{4,0},{5,1},{6,2},{7,3},{8,12},{9,13},{10,... | collective-permute-start | bytes 1474568 | tf_op jit(solution)/shard_map/ppermute | solution.py:19
  8.5 1.5 %collective-permute-start.6 = (bf16[192,2048]{1,0:T(8,128)(2,1)}, bf16[192,2048]{1,0:T(8,128)(2,1)S(1)}, u32[]{:S(2)}, u32[]{:S(2)}) collective-permute-start(bf16[192,2048]{1,0:T(8,128)(2,1)} %bitcast.18), channel_id=1, source_target_pairs={{0,16},{1,17},{2,18},{3,19},{4,20},{5,21},{6,22},{7,23},{8,24},{9,... | collective-permute-start | bytes 2359304 | tf_op jit(solution)/shard_map/ppermute | solution.py:29
  10.0 2.5 %collective-permute-start.11 = (s32[2,192]{1,0:T(2,128)}, s32[2,192]{1,0:T(2,128)S(1)}, u32[]{:S(2)}, u32[]{:S(2)}) collective-permute-start(s32[2,192]{1,0:T(2,128)} %bitcast.23), channel_id=1, source_target_pairs={{0,12},{1,13},{2,14},{3,15},{4,8},{5,9},{6,10},{7,11},{8,4},{9,5},... | collective-permute-start | bytes 4616 | tf_op jit(solution)/shard_map/ppermute | solution.py:19
  12.5 9.2 %collective-permute-done.11.routes_ref = s32[2,192]{1,0:T(2,128)S(1)} collective-permute-done((s32[2,192]{1,0:T(2,128)}, s32[2,192]{1,0:T(2,128)S(1)}, u32[]{:S(2)}, u32[]{:S(2)}) %collective-permute-start.11) | collective-permute-done | bytes 1568 | tf_op jit(solution)/shard_map/ppermute | solution.py:19
  22.2 1.5 %collective-permute-start.10 = (bf16[192,2048]{1,0:T(8,128)(2,1)S(1)}, bf16[192,2048]{1,0:T(8,128)(2,1)S(1)}, u32[]{:S(2)}, u32[]{:S(2)}) collective-permute-start(bf16[192,2048]{1,0:T(8,128)(2,1)S(1)} %bitcast.17), channel_id=1, source_target_pairs={{0,12},{1,13},{2,14},{3,15},{4,8},{5,9},{6,10},{7,11},{8,4},{9,5},... | collective-permute-start | bytes 2359304 | tf_op jit(solution)/shard_map/ppermute | solution.py:19
  23.6 3.8 %collective-permute-done.6.refs_0_ = bf16[192,2048]{1,0:T(8,128)(2,1)S(1)} collective-permute-done((bf16[192,2048]{1,0:T(8,128)(2,1)}, bf16[192,2048]{1,0:T(8,128)(2,1)S(1)}, u32[]{:S(2)}, u32[]{:S(2)}) %collective-permute-start.6) | collective-permute-done | bytes 786464 | tf_op jit(solution)/shard_map/ppermute | solution.py:29
  27.9 14.4 %collective-permute-done.13.refs_2_ = bf16[192,2048]{1,0:T(8,128)(2,1)S(1)} collective-permute-done((bf16[192,2048]{1,0:T(8,128)(2,1)}, bf16[192,2048]{1,0:T(8,128)(2,1)S(1)}, u32[]{:S(2)}, u32[]{:S(2)}) %collective-permute-start.13) | collective-permute-done | bytes 786464 | tf_op jit(solution)/shard_map/ppermute | solution.py:19
  42.8 0.7 copy-done.4
  43.5 0.7 sort.3
  44.2 13.4 %collective-permute-start.18 = (bf16[120,2048]{1,0:T(8,128)(2,1)S(1)}, bf16[120,2048]{1,0:T(8,128)(2,1)S(1)}, u32[]{:S(2)}, u32[]{:S(2)}) collective-permute-start(bf16[120,2048]{1,0:T(8,128)(2,1)S(1)} %get-tuple-element.28), channel_id=1, source_target_pairs={{0,4},{1,5},{2,6},{3,7},{4,0},{5,1},{6,2},{7,3},{8,12},{9,13},{10,... | collective-permute-start | bytes 1474568 | tf_op jit(solution)/shard_map/ppermute | solution.py:19
  57.9 1.5 %collective-permute-start = (bf16[192,2048]{1,0:T(8,128)(2,1)}, bf16[192,2048]{1,0:T(8,128)(2,1)S(1)}, u32[]{:S(2)}, u32[]{:S(2)}) collective-permute-start(bf16[192,2048]{1,0:T(8,128)(2,1)} %bitcast.15), channel_id=1, source_target_pairs={{0,16},{1,17},{2,18},{3,19},{4,20},{5,21},{6,22},{7,23},{8,24},{9,... | collective-permute-start | bytes 2359304 | tf_op jit(solution)/shard_map/ppermute | solution.py:29
  59.4 1.1 copy-done
  60.5 1.5 %shard_map.64 = (bf16[120,768]{1,0:T(8,128)(2,1)S(1)}, bf16[768,2048]{1,0:T(8,128)(2,1)S(1)}) custom-call(bf16[120,2048]{1,0:T(8,128)(2,1)S(1)} %get-tuple-element.18.refs_0_, bf16[192,2048]{1,0:T(8,128)(2,1)S(1)} %bitcast.14, bf16[192,2048]{1,0:T(8,128)(2,1)S(1)} %collective-permute-done.2.refs_2_, bf16[192,2048]{1,0:T(8,128)(2,1)S(1)} %collective-permute-done.3.refs_3_, ...), custom_call_target="tpu_custom_call" | custom-call | flops 377487360 | bytes 3637248 | tf_op jit(solution)/shard_map/pallas_call | solution.py:160
  62.6 1.2 shard_map.66.hidden_ref
  63.8 0.8 shard_map.67
  64.7 2.1 %shard_map.69 = bf16[120,2048]{1,0:T(8,128)(2,1)S(1)} custom-call(bf16[120,2048]{1,0:T(8,128)(2,1)S(1)} %collective-permute-done.16.refs_0_, bf16[768,2048]{1,0:T(8,128)(2,1)S(1)} %get-tuple-element.21.refs_1_, bf16[768,2048]{1,0:T(8,128)(2,1)S(1)} %get-tuple-element.27.refs_2_), custom_call_target="tpu_custom_call" | custom-call | flops 754974720 | bytes 7274496 | tf_op jit(solution)/shard_map/pallas_call | solution.py:160
  66.8 2.7 %collective-permute-done.18.refs_0_ = bf16[120,2048]{1,0:T(8,128)(2,1)S(1)} collective-permute-done((bf16[120,2048]{1,0:T(8,128)(2,1)S(1)}, bf16[120,2048]{1,0:T(8,128)(2,1)S(1)}, u32[]{:S(2)}, u32[]{:S(2)}) %collective-permute-start.18) | collective-permute-done | bytes 491552 | tf_op jit(solution)/shard_map/ppermute | solution.py:19
  69.5 3.4 %collective-permute-start.15 = (bf16[120,2048]{1,0:T(8,128)(2,1)S(1)}, bf16[120,2048]{1,0:T(8,128)(2,1)S(1)}, u32[]{:S(2)}, u32[]{:S(2)}) collective-permute-start(bf16[120,2048]{1,0:T(8,128)(2,1)S(1)} %get-tuple-element.22), channel_id=1, source_target_pairs={{0,28},{1,29},{2,30},{3,31},{4,24},{5,25},{6,26},{7,27},{8,20},{9,... | collective-permute-start | bytes 1474568 | tf_op jit(solution)/shard_map/ppermute | solution.py:29
  72.9 2.1 %shard_map.70 = bf16[120,2048]{1,0:T(8,128)(2,1)S(1)} custom-call(bf16[120,2048]{1,0:T(8,128)(2,1)S(1)} %collective-permute-done.18.refs_0_, bf16[768,2048]{1,0:T(8,128)(2,1)S(1)} %get-tuple-element.21.refs_1_, bf16[768,2048]{1,0:T(8,128)(2,1)S(1)} %get-tuple-element.27.refs_2_), custom_call_target="tpu_custom_call" | custom-call | flops 754974720 | bytes 7274496 | tf_op jit(solution)/shard_map/pallas_call | solution.py:160
  75.1 0.9 collective-permute-start.17
  76.0 26.9 %collective-permute-done.5.hidden_ref = bf16[120,768]{1,0:T(8,128)(2,1)S(1)} collective-permute-done((bf16[120,768]{1,0:T(8,128)(2,1)S(1)}, bf16[120,768]{1,0:T(8,128)(2,1)S(1)}, u32[]{:S(2)}, u32[]{:S(2)}) %collective-permute-start.5) | collective-permute-done | bytes 184352 | tf_op jit(solution)/shard_map/ppermute | solution.py:29
  102.8 1.5 %collective-permute-start.1 = (f32[8,192]{1,0:T(8,128)S(1)}, f32[8,192]{1,0:T(8,128)S(1)}, u32[]{:S(2)}, u32[]{:S(2)}) collective-permute-start(f32[8,192]{1,0:T(8,128)S(1)} %get-tuple-element.17), channel_id=1, source_target_pairs={{0,16},{1,17},{2,18},{3,19},{4,20},{5,21},{6,22},{7,23},{8,24},{9,... | collective-permute-start | bytes 18440 | tf_op jit(solution)/shard_map/ppermute | solution.py:29
  104.3 0.7 shard_map.65.refs_0_
  105.1 1.4 %collective-permute-done.1.info_ref = f32[8,192]{1,0:T(8,128)S(1)} collective-permute-done((f32[8,192]{1,0:T(8,128)S(1)}, f32[8,192]{1,0:T(8,128)S(1)}, u32[]{:S(2)}, u32[]{:S(2)}) %collective-permute-start.1) | collective-permute-done | bytes 6176 | tf_op jit(solution)/shard_map/ppermute | solution.py:29
  106.5 0.8 shard_map.68
  107.3 20.3 %collective-permute-done.19.refs_1_ = bf16[120,2048]{1,0:T(8,128)(2,1)S(1)} collective-permute-done((bf16[120,2048]{1,0:T(8,128)(2,1)S(1)}, bf16[120,2048]{1,0:T(8,128)(2,1)S(1)}, u32[]{:S(2)}, u32[]{:S(2)}) %collective-permute-start.19) | collective-permute-done | bytes 491552 | tf_op jit(solution)/shard_map/ppermute | solution.py:29
  127.6 1.3 %shard_map.71 = bf16[192,2048]{1,0:T(8,128)(2,1)} custom-call(f32[192,2048]{1,0:T(8,128)S(1)} %get-tuple-element.23.sum_ref, bf16[192,240]{1,0:T(8,128)(2,1)S(1)} %get-tuple-element.24.high_ref, bf16[192,240]{1,0:T(8,128)(2,1)S(1)} %get-tuple-element.25.low_ref, bf16[120,2048]{1,0:T(8,128)(2,1)S(1)} %collective-permute-done.17.refs_0_, ...), custom_call_target="tpu_custom_call" | custom-call | flops 377487360 | bytes 3342336 | tf_op jit(solution)/shard_map/pallas_call | solution.py:223
  (32 shorter events, 3.1 us)
Async XLA Ops:
  0.0 23.6 %collective-permute-start.3 = (bf16[192,2048]{1,0:T(8,128)(2,1)}, bf16[192,2048]{1,0:T(8,128)(2,1)S(1)}, u32[]{:S(2)}, u32[]{:S(2)}) collective-permute-start(bf16[192,2048]{1,0:T(8,128)(2,1)} %bitcast.12), channel_id=1, source_target_pairs={{0,2},{1,3},{2,0},{3,1},{4,6},{5,7},{6,4},{7,5},{8,10},{9,11},{10,... | collective-permute-start | bytes 2359304 | tf_op jit(solution)/shard_map/ppermute | solution.py:19
  3.0 1.1 copy-start.1
  4.1 0.7 copy-start.3
  4.8 0.7 copy-start.5
  5.5 0.7 copy-start.6
  6.9 15.3 %collective-permute-start.16 = (bf16[120,2048]{1,0:T(8,128)(2,1)S(1)}, bf16[120,2048]{1,0:T(8,128)(2,1)S(1)}, u32[]{:S(2)}, u32[]{:S(2)}) collective-permute-start(bf16[120,2048]{1,0:T(8,128)(2,1)S(1)} %get-tuple-element.26), channel_id=1, source_target_pairs={{0,4},{1,5},{2,6},{3,7},{4,0},{5,1},{6,2},{7,3},{8,12},{9,13},{10,... | collective-permute-start | bytes 1474568 | tf_op jit(solution)/shard_map/ppermute | solution.py:19
  8.5 18.9 %collective-permute-start.6 = (bf16[192,2048]{1,0:T(8,128)(2,1)}, bf16[192,2048]{1,0:T(8,128)(2,1)S(1)}, u32[]{:S(2)}, u32[]{:S(2)}) collective-permute-start(bf16[192,2048]{1,0:T(8,128)(2,1)} %bitcast.18), channel_id=1, source_target_pairs={{0,16},{1,17},{2,18},{3,19},{4,20},{5,21},{6,22},{7,23},{8,24},{9,... | collective-permute-start | bytes 2359304 | tf_op jit(solution)/shard_map/ppermute | solution.py:29
  10.0 18.0 %collective-permute-start.2 = (bf16[192,2048]{1,0:T(8,128)(2,1)}, bf16[192,2048]{1,0:T(8,128)(2,1)S(1)}, u32[]{:S(2)}, u32[]{:S(2)}) collective-permute-start(bf16[192,2048]{1,0:T(8,128)(2,1)} %bitcast.13), channel_id=1, source_target_pairs={{0,1},{1,0},{2,3},{3,2},{4,5},{5,4},{6,7},{7,6},{8,9},{9,8},{10,11... | collective-permute-start | bytes 2359304 | tf_op jit(solution)/shard_map/ppermute | solution.py:19
  10.0 11.7 %collective-permute-start.11 = (s32[2,192]{1,0:T(2,128)}, s32[2,192]{1,0:T(2,128)S(1)}, u32[]{:S(2)}, u32[]{:S(2)}) collective-permute-start(s32[2,192]{1,0:T(2,128)} %bitcast.23), channel_id=1, source_target_pairs={{0,12},{1,13},{2,14},{3,15},{4,8},{5,9},{6,10},{7,11},{8,4},{9,5},... | collective-permute-start | bytes 4616 | tf_op jit(solution)/shard_map/ppermute | solution.py:19
  21.7 20.6 %collective-permute-start.13 = (bf16[192,2048]{1,0:T(8,128)(2,1)}, bf16[192,2048]{1,0:T(8,128)(2,1)S(1)}, u32[]{:S(2)}, u32[]{:S(2)}) collective-permute-start(bf16[192,2048]{1,0:T(8,128)(2,1)} %bitcast.19), channel_id=1, source_target_pairs={{0,2},{1,3},{2,0},{3,1},{4,6},{5,7},{6,4},{7,5},{8,10},{9,11},{10,... | collective-permute-start | bytes 2359304 | tf_op jit(solution)/shard_map/ppermute | solution.py:19
  22.2 20.1 %collective-permute-start.10 = (bf16[192,2048]{1,0:T(8,128)(2,1)S(1)}, bf16[192,2048]{1,0:T(8,128)(2,1)S(1)}, u32[]{:S(2)}, u32[]{:S(2)}) collective-permute-start(bf16[192,2048]{1,0:T(8,128)(2,1)S(1)} %bitcast.17), channel_id=1, source_target_pairs={{0,12},{1,13},{2,14},{3,15},{4,8},{5,9},{6,10},{7,11},{8,4},{9,5},... | collective-permute-start | bytes 2359304 | tf_op jit(solution)/shard_map/ppermute | solution.py:19
  23.6 20.6 %collective-permute-start.12 = (bf16[192,2048]{1,0:T(8,128)(2,1)}, bf16[192,2048]{1,0:T(8,128)(2,1)S(1)}, u32[]{:S(2)}, u32[]{:S(2)}) collective-permute-start(bf16[192,2048]{1,0:T(8,128)(2,1)} %bitcast.20), channel_id=1, source_target_pairs={{0,1},{1,0},{2,3},{3,2},{4,5},{5,4},{6,7},{7,6},{8,9},{9,8},{10,11... | collective-permute-start | bytes 2359304 | tf_op jit(solution)/shard_map/ppermute | solution.py:19
  27.4 30.2 %collective-permute-start.8 = (bf16[192,2048]{1,0:T(8,128)(2,1)S(1)}, bf16[192,2048]{1,0:T(8,128)(2,1)S(1)}, u32[]{:S(2)}, u32[]{:S(2)}) collective-permute-start(bf16[192,2048]{1,0:T(8,128)(2,1)S(1)} %collective-permute-done.6.refs_0_), channel_id=1, source_target_pairs={{0,2},{1,3},{2,0},{3,1},{4,6},{5,7},{6,4},{7,5},{8,10},{9,11},{10,... | collective-permute-start | bytes 2359304 | tf_op jit(solution)/shard_map/ppermute | solution.py:19
  27.9 29.9 %collective-permute-start.4 = (bf16[192,2048]{1,0:T(8,128)(2,1)S(1)}, bf16[192,2048]{1,0:T(8,128)(2,1)S(1)}, u32[]{:S(2)}, u32[]{:S(2)}) collective-permute-start(bf16[192,2048]{1,0:T(8,128)(2,1)S(1)} %collective-permute-done.3.refs_3_), channel_id=1, source_target_pairs={{0,1},{1,0},{2,3},{3,2},{4,5},{5,4},{6,7},{7,6},{8,9},{9,8},{10,11... | collective-permute-start | bytes 2359304 | tf_op jit(solution)/shard_map/ppermute | solution.py:19
  42.3 19.7 %collective-permute-start.14 = (bf16[192,2048]{1,0:T(8,128)(2,1)S(1)}, bf16[192,2048]{1,0:T(8,128)(2,1)S(1)}, u32[]{:S(2)}, u32[]{:S(2)}) collective-permute-start(bf16[192,2048]{1,0:T(8,128)(2,1)S(1)} %collective-permute-done.13.refs_2_), channel_id=1, source_target_pairs={{0,1},{1,0},{2,3},{3,2},{4,5},{5,4},{6,7},{7,6},{8,9},{9,8},{10,11... | collective-permute-start | bytes 2359304 | tf_op jit(solution)/shard_map/ppermute | solution.py:19
  42.3 32.8 %collective-permute-start.7 = (bf16[192,2048]{1,0:T(8,128)(2,1)S(1)}, bf16[192,2048]{1,0:T(8,128)(2,1)S(1)}, u32[]{:S(2)}, u32[]{:S(2)}) collective-permute-start(bf16[192,2048]{1,0:T(8,128)(2,1)S(1)} %collective-permute-done.6.refs_0_), channel_id=1, source_target_pairs={{0,1},{1,0},{2,3},{3,2},{4,5},{5,4},{6,7},{7,6},{8,9},{9,8},{10,11... | collective-permute-start | bytes 2359304 | tf_op jit(solution)/shard_map/ppermute | solution.py:19
  42.8 0.7 copy-start.4
  44.2 25.3 %collective-permute-start.18 = (bf16[120,2048]{1,0:T(8,128)(2,1)S(1)}, bf16[120,2048]{1,0:T(8,128)(2,1)S(1)}, u32[]{:S(2)}, u32[]{:S(2)}) collective-permute-start(bf16[120,2048]{1,0:T(8,128)(2,1)S(1)} %get-tuple-element.28), channel_id=1, source_target_pairs={{0,4},{1,5},{2,6},{3,7},{4,0},{5,1},{6,2},{7,3},{8,12},{9,13},{10,... | collective-permute-start | bytes 1474568 | tf_op jit(solution)/shard_map/ppermute | solution.py:19
  57.7 45.2 %collective-permute-start.9 = (bf16[192,2048]{1,0:T(8,128)(2,1)S(1)}, bf16[192,2048]{1,0:T(8,128)(2,1)S(1)}, u32[]{:S(2)}, u32[]{:S(2)}) collective-permute-start(bf16[192,2048]{1,0:T(8,128)(2,1)S(1)} %collective-permute-done.8.refs_2_), channel_id=1, source_target_pairs={{0,1},{1,0},{2,3},{3,2},{4,5},{5,4},{6,7},{7,6},{8,9},{9,8},{10,11... | collective-permute-start | bytes 2359304 | tf_op jit(solution)/shard_map/ppermute | solution.py:19
  57.9 48.6 %collective-permute-start = (bf16[192,2048]{1,0:T(8,128)(2,1)}, bf16[192,2048]{1,0:T(8,128)(2,1)S(1)}, u32[]{:S(2)}, u32[]{:S(2)}) collective-permute-start(bf16[192,2048]{1,0:T(8,128)(2,1)} %bitcast.15), channel_id=1, source_target_pairs={{0,16},{1,17},{2,18},{3,19},{4,20},{5,21},{6,22},{7,23},{8,24},{9,... | collective-permute-start | bytes 2359304 | tf_op jit(solution)/shard_map/ppermute | solution.py:29
  59.4 1.1 copy-start
  60.5 3.3 %copy-start.2 = (bf16[1,192,2048]{2,1,0:T(8,128)(2,1)S(1)}, bf16[1,192,2048]{2,1,0:T(8,128)(2,1)}, u32[]{:S(2)}) copy-start(bf16[1,192,2048]{2,1,0:T(8,128)(2,1)} %param.9) | copy-start | bytes 2359300
  62.0 40.8 %collective-permute-start.5 = (bf16[120,768]{1,0:T(8,128)(2,1)S(1)}, bf16[120,768]{1,0:T(8,128)(2,1)S(1)}, u32[]{:S(2)}, u32[]{:S(2)}) collective-permute-start(bf16[120,768]{1,0:T(8,128)(2,1)S(1)} %get-tuple-element.19), channel_id=1, source_target_pairs={{0,16},{1,17},{2,18},{3,19},{4,20},{5,21},{6,22},{7,23},{8,24},{9,... | collective-permute-start | bytes 552968 | tf_op jit(solution)/shard_map/ppermute | solution.py:29
  69.5 37.0 %collective-permute-start.15 = (bf16[120,2048]{1,0:T(8,128)(2,1)S(1)}, bf16[120,2048]{1,0:T(8,128)(2,1)S(1)}, u32[]{:S(2)}, u32[]{:S(2)}) collective-permute-start(bf16[120,2048]{1,0:T(8,128)(2,1)S(1)} %get-tuple-element.22), channel_id=1, source_target_pairs={{0,28},{1,29},{2,30},{3,31},{4,24},{5,25},{6,26},{7,27},{8,20},{9,... | collective-permute-start | bytes 1474568 | tf_op jit(solution)/shard_map/ppermute | solution.py:29
  75.1 32.2 %collective-permute-start.17 = (bf16[120,2048]{1,0:T(8,128)(2,1)S(1)}, bf16[120,2048]{1,0:T(8,128)(2,1)S(1)}, u32[]{:S(2)}, u32[]{:S(2)}) collective-permute-start(bf16[120,2048]{1,0:T(8,128)(2,1)S(1)} %shard_map.69), channel_id=1, source_target_pairs={{0,20},{1,21},{2,22},{3,23},{4,16},{5,17},{6,18},{7,19},{8,28},{9,... | collective-permute-start | bytes 1474568 | tf_op jit(solution)/shard_map/ppermute | solution.py:29
  102.8 24.7 %collective-permute-start.19 = (bf16[120,2048]{1,0:T(8,128)(2,1)S(1)}, bf16[120,2048]{1,0:T(8,128)(2,1)S(1)}, u32[]{:S(2)}, u32[]{:S(2)}) collective-permute-start(bf16[120,2048]{1,0:T(8,128)(2,1)S(1)} %shard_map.70), channel_id=1, source_target_pairs={{0,24},{1,25},{2,26},{3,27},{4,28},{5,29},{6,30},{7,31},{8,16},{9,... | collective-permute-start | bytes 1474568 | tf_op jit(solution)/shard_map/ppermute | solution.py:29
  102.8 3.7 %collective-permute-start.1 = (f32[8,192]{1,0:T(8,128)S(1)}, f32[8,192]{1,0:T(8,128)S(1)}, u32[]{:S(2)}, u32[]{:S(2)}) collective-permute-start(f32[8,192]{1,0:T(8,128)S(1)} %get-tuple-element.17), channel_id=1, source_target_pairs={{0,16},{1,17},{2,18},{3,19},{4,20},{5,21},{6,22},{7,23},{8,24},{9,... | collective-permute-start | bytes 18440 | tf_op jit(solution)/shard_map/ppermute | solution.py:29
